TPU v7x, 32 devices: a whole 2x2x4 slice. The times are simulated.
32 devices in a mesh: section: 4 (over z), vit: 2 (over x), dp: 4 (over y, core).
Axes of the slice: x: 2, y: 2, z: 4, core: 2. Of those that a mesh axis runs over, the one named last changes fastest.
Arguments:
- grad_llm: bfloat16 [4, 1024, 4096], P('section', ('dp', 'vit')), parts along dimension 1, may hold values from -6 to 6
- vis_slot: int32 [8, 128], P('dp'), parts along dimension 0, may hold values from 0 to 255, as said below
- image_rows: int32 [16, 2], P('dp'), parts along dimension 0, may hold values from 8 to 32, as said below
- section_layer: int32 [4], replicated, may hold values from 0 to 3, each once
- vit_in: bfloat16 [4096, 1152], P(('dp', 'section', 'vit')), parts along dimension 0, may hold values from -6 to 6
- vit_out: bfloat16 [4096, 1152], P(('dp', 'section', 'vit')), parts along dimension 0, may hold values from -6 to 6
- ln_gain: float32 [1152], replicated, may hold values from 0.5 to 1.5
- ln_bias: float32 [1152], replicated, may hold values from -3 to 3
- qkv_weight: bfloat16 [1152, 3456], P('section'), may hold values from -0.1875 to 0.1875
- proj_weight: bfloat16 [1152, 1152], P('section'), may hold values from -0.1875 to 0.1875
- merge_gain: float32 [1152], replicated, may hold values from 0.5 to 1.5
- merge_bias: float32 [1152], replicated, may hold values from -3 to 3
- fc1_weight: bfloat16 [4608, 4608], P(None, 'vit'), may hold values from -0.09375 to 0.09375
- fc1_bias: float32 [4608], P('vit'), may hold values from -3 to 3
- fc2_weight: bfloat16 [4608, 4096], P('vit'), may hold values from -0.09375 to 0.09375
Outputs:
- vit_grad: bfloat16 [4096, 1152], P(('dp', 'section', 'vit')), parts along dimension 0
There are 4 independent parts, one for each index of `dp`. A program takes and returns all parts, laid end to end along the dimension named above; an argument that names none is the same for every part. Nothing has to cross between parts.
Inputs may be any that keep to these rules, and one draw needn't show every extreme that they name: `vis_slot`: every slot number appears once. On every language-model device v, the rows d * 16 to d * 16 + 15 name 16 consecutive slots that start at a multiple of 16 inside d * 32 to d * 32 + 31, the slots of vision device d (devices numbered with the group first). `image_rows`: in every group one image has exactly 32 merged tokens. `section_layer`: A permutation; the section with value 3 holds no DeepStack layer.
All inputs are finite; a program needn't handle non-finite values.
Results may differ from a plain program's by a relative error of at most 0.02.
Values may be sent and summed in bfloat16 or wider, within the bound.
No kernel may reach another device: no remote copies, remote signals or barrier semaphores. Data moves between devices by JAX's collectives and lax.ppermute only.
A program may use at most 128 MiB of HBM per device.

v0:
```python
import jax
import jax.numpy as jnp
from jax import lax
from jax.experimental import pallas as pl
from jax.experimental.pallas import tpu as pltpu
from jax.sharding import PartitionSpec as P

HEADS = 16
LEVELS = 3


norm_eps = 1e-06


def normalize(values):
    row_mean = jnp.mean(values, axis=-1, keepdims=True)
    centered = values - row_mean
    variance = jnp.mean(centered * centered, axis=-1, keepdims=True)
    inverse = lax.rsqrt(variance + norm_eps)
    return (centered * inverse, inverse)


def normalize_back(upstream, normed_rows, inverse, gain):
    scaled = upstream * gain
    mean_scaled = jnp.mean(scaled, axis=-1, keepdims=True)
    mean_cross = jnp.mean(scaled * normed_rows, axis=-1, keepdims=True)
    return (scaled - mean_scaled - normed_rows * mean_cross) * inverse


def gelu_slope(pre_act):
    cumulative = 0.5 * (1.0 + lax.erf(pre_act * 0.7071067811865476))
    density = jnp.exp(-0.5 * pre_act * pre_act) * 0.3989422804014327
    return cumulative + pre_act * density


def local(
    grad_llm,
    vis_slot,
    image_rows,
    section_layer,
    vit_in,
    vit_out,
    ln_gain,
    ln_bias,
    qkv_weight,
    proj_weight,
    merge_gain,
    merge_bias,
    fc1_weight,
    fc1_bias,
    fc2_weight,
):
    sections = lax.axis_size("section")
    shards = lax.axis_size("vit")
    section_index = lax.axis_index("section")
    shard_index = lax.axis_index("vit")
    devices = sections * shards
    patches = vit_in.shape[0]
    slots_here = patches // 4
    run_rows = grad_llm.shape[1] // devices
    llm_width = grad_llm.shape[2]
    vit_width = vit_in.shape[1]
    head_dim = vit_width // HEADS
    device_index = section_index * shards + shard_index
    qkv_full, proj_full = (
        lax.all_gather(qkv_weight, "section", axis=0, tiled=True),
        lax.all_gather(proj_weight, "section", axis=0, tiled=True),
    )
    in_rows, in_inverse = normalize(vit_in.astype(jnp.float32))
    normed = (in_rows * ln_gain + ln_bias).astype(jnp.bfloat16)
    projected = lax.dot_general(
        qkv_full, normed, (((0,), (1,)), ((), ())), preferred_element_type=jnp.float32
    )
    projected = projected.astype(jnp.bfloat16).reshape(3, HEADS, head_dim, patches)
    section_weight = jnp.where(
        section_layer < LEVELS, (section_layer + 1).astype(jnp.float32) / LEVELS, 0.0
    )
    outgoing = grad_llm[0].reshape(devices, run_rows, llm_width)
    image_ends = jnp.cumsum(image_rows[section_index])
    out_rows, out_inverse = normalize(vit_out.astype(jnp.float32))
    merge_in = (
        (out_rows * merge_gain + merge_bias).astype(jnp.bfloat16).reshape(slots_here, 4 * vit_width)
    )
    arrived = lax.all_to_all(outgoing, ("section", "vit"), split_axis=0, concat_axis=0, tiled=True)
    arrived_f = arrived.reshape(sections, shards, run_rows, llm_width).astype(jnp.float32)
    incoming = jnp.sum(arrived_f * section_weight[:, None, None, None], axis=0)
    columns = lax.dynamic_slice_in_dim(vis_slot, device_index * run_rows, run_rows, 1)
    local_slot = (columns - device_index * slots_here).reshape(-1)
    placed = (
        jnp.zeros((slots_here, llm_width), jnp.float32)
        .at[local_slot]
        .set(incoming.reshape(-1, llm_width))
    )
    slot_position = shard_index * slots_here + jnp.arange(slots_here, dtype=jnp.int32)
    merged_grad = jnp.where((slot_position < image_ends[-1])[:, None], placed, 0.0).astype(
        jnp.bfloat16
    )
    rows_in, rows_grad = (
        lax.all_gather(merge_in, "vit", axis=0, tiled=True),
        lax.all_gather(merged_grad, "vit", axis=0, tiled=True),
    )
    pre_act = jnp.dot(rows_in, fc1_weight, preferred_element_type=jnp.float32) + fc1_bias
    hidden_grad = lax.dot_general(
        rows_grad, fc2_weight, (((1,), (1,)), ((), ())), preferred_element_type=jnp.float32
    )
    pre_grad = (hidden_grad * gelu_slope(pre_act)).astype(jnp.bfloat16)
    merge_grad = lax.psum_scatter(
        lax.dot_general(
            pre_grad, fc1_weight, (((1,), (1,)), ((), ())), preferred_element_type=jnp.float32
        ).astype(jnp.bfloat16),
        "vit",
        scatter_dimension=0,
        tiled=True,
    ).astype(jnp.float32)
    out_grad = normalize_back(
        merge_grad.reshape(patches, vit_width), out_rows, out_inverse, merge_gain
    ).astype(jnp.bfloat16)
    grad_cols = lax.dot_general(
        proj_full, out_grad, (((1,), (1,)), ((), ())), preferred_element_type=jnp.float32
    )
    grad_cols = grad_cols.astype(jnp.bfloat16).reshape(1, HEADS, head_dim, patches)
    head_inputs, head_grad = (
        lax.all_to_all(projected, "vit", split_axis=1, concat_axis=3, tiled=True),
        lax.all_to_all(grad_cols, "vit", split_axis=1, concat_axis=3, tiled=True),
    )
    length = shards * patches
    block_size = min(512, length)
    block_count = length // block_size
    slot_of = jnp.arange(length, dtype=jnp.int32) // 4
    patch_image = jnp.sum((slot_of[:, None] >= image_ends[None, :]).astype(jnp.int32), axis=1)
    patch_live = slot_of < image_ends[-1]
    score_scale = head_dim ** (-0.5)
    contract_first = (((0,), (0,)), ((), ()))

    def head_backward(query_cols, key_cols, value_cols, grad_head):

        def step(carry, block_index):
            key_acc, value_acc = carry
            first_row = block_index * block_size
            query_block = lax.dynamic_slice_in_dim(query_cols, first_row, block_size, 1)
            grad_block = lax.dynamic_slice_in_dim(grad_head, first_row, block_size, 1)
            image_block = lax.dynamic_slice_in_dim(patch_image, first_row, block_size, 0)
            live_block = lax.dynamic_slice_in_dim(patch_live, first_row, block_size, 0)
            scores = (
                lax.dot_general(
                    query_block, key_cols, contract_first, preferred_element_type=jnp.float32
                )
                * score_scale
            )
            allowed = (
                (image_block[:, None] == patch_image[None, :])
                & live_block[:, None]
                & patch_live[None, :]
            )
            exponent = jnp.where(allowed, jnp.exp(jnp.where(allowed, scores, 0.0)), 0.0)
            denominator = (
                jnp.sum(exponent, axis=1, keepdims=True)
                + 1.0
                - live_block.astype(jnp.float32)[:, None]
            )
            softmax_weights = (exponent / denominator).astype(jnp.bfloat16)
            prob_grad = lax.dot_general(
                grad_block, value_cols, contract_first, preferred_element_type=jnp.float32
            )
            weighted = softmax_weights.astype(jnp.float32)
            row_dot = jnp.sum(weighted * prob_grad, axis=1, keepdims=True)
            score_grad = (weighted * (prob_grad - row_dot) * score_scale).astype(jnp.bfloat16)
            query_grad = lax.dot_general(
                key_cols, score_grad, (((1,), (1,)), ((), ())), preferred_element_type=jnp.float32
            )
            key_acc = key_acc + lax.dot_general(
                query_block,
                score_grad,
                (((1,), (0,)), ((), ())),
                preferred_element_type=jnp.float32,
            )
            value_acc = value_acc + lax.dot_general(
                grad_block,
                softmax_weights,
                (((1,), (0,)), ((), ())),
                preferred_element_type=jnp.float32,
            )
            return ((key_acc, value_acc), query_grad.astype(jnp.bfloat16))

        empty = jnp.zeros((head_dim, length), jnp.float32)
        (key_total, value_total), query_blocks = lax.scan(
            step, (empty, empty), jnp.arange(block_count, dtype=jnp.int32)
        )
        query_total = query_blocks.transpose(1, 0, 2).reshape(head_dim, length)
        return (query_total, key_total.astype(jnp.bfloat16), value_total.astype(jnp.bfloat16))

    query_all, key_all, value_all = jax.vmap(head_backward)(
        head_inputs[0], head_inputs[1], head_inputs[2], head_grad[0]
    )
    head_result = jnp.stack([query_all, key_all, value_all])
    returned = lax.all_to_all(head_result, "vit", split_axis=3, concat_axis=1, tiled=True)
    projected_grad = returned.reshape(3 * vit_width, patches)
    normed_grad = lax.dot_general(
        projected_grad, qkv_full, (((0,), (1,)), ((), ())), preferred_element_type=jnp.float32
    )
    vit_grad = out_grad.astype(jnp.float32) + normalize_back(
        normed_grad, in_rows, in_inverse, ln_gain
    )
    return vit_grad.astype(jnp.bfloat16)


bf16, f32 = jnp.bfloat16, jnp.float32


def swap(values, axis, bit):
    count = lax.axis_size(axis)
    return lax.ppermute(values, axis, [(i, i ^ bit) for i in range(count)])


def fits(mesh):
    sections, copies, shards = (mesh.shape[name] for name in ("section", "dp", "vit"))
    return (sections, copies, shards) == (4, 4, 2)


def dot(a, b, ca=1, cb=0):
    return lax.dot_general(a, b, (((ca,), (cb,)), ((), ())), preferred_element_type=f32)


def block_of(size, limit):
    return max(b for b in range(128, limit + 1, 128) if size % b == 0)


def run_kernel(body, grid, in_specs, out_specs, out_shape, scratch=(), prefetch=0, limit=10):
    return pl.pallas_call(
        body,
        grid_spec=pltpu.PrefetchScalarGridSpec(
            num_scalar_prefetch=prefetch,
            grid=grid,
            in_specs=in_specs,
            out_specs=out_specs,
            scratch_shapes=list(scratch),
        ),
        out_shape=out_shape,
        compiler_params=pltpu.CompilerParams(
            dimension_semantics=("arbitrary",) * len(grid), vmem_limit_bytes=limit << 20
        ),
    )


def whole(array):
    return pl.BlockSpec(array.shape, lambda i, *_: (0,) * array.ndim)


RESIDENT = pl.BlockSpec(memory_space=pltpu.VMEM)


def struct(shape, dtype):
    return jax.ShapeDtypeStruct(shape, dtype)


LANES = 128


def put_rows(ref, first, values):
    for c in range(ref.shape[0]):
        ref[c, first : first + values.shape[0], :] = values[:, c * LANES : (c + 1) * LANES]


def every_fourth(ref, j, count):
    return jnp.concatenate(
        [ref[c, pl.ds(j, count, stride=4), :] for c in range(ref.shape[0])], axis=1
    )


def image_ends(image_ref, images):
    group, ends = lax.axis_index("section"), []
    for k in range(images):
        ends.append(image_ref[k, group] + (ends[-1] if ends else 0))
    return ends


def weighted_sum(section_layer, grad_llm, arrived):
    rows, width = arrived[0].shape

    def body(layer_ref, grad_ref, *refs):
        arrived_refs, (out_ref, own, sem) = refs[:-3], refs[-3:]
        here = lax.axis_index("section")
        window = pl.ds(pl.multiple_of(here * rows, 16), rows)
        copy = pltpu.make_async_copy(grad_ref.at[0, window, :], own, sem)
        copy.start()

        def term(section, values):
            layer = layer_ref[section]
            weight = jnp.where(layer < LEVELS, (layer + 1).astype(f32) / LEVELS, 0.0)
            return weight * values.astype(f32)

        total = sum(term(here ^ (k + 1), ref[...]) for k, ref in enumerate(arrived_refs))
        copy.wait()
        out_ref[...] = (total + term(here, own[...])).astype(bf16)

    return run_kernel(
        body,
        (1,),
        [pl.BlockSpec(memory_space=pl.ANY)] + [whole(x) for x in arrived],
        pl.BlockSpec((rows, width), lambda i, *_: (0, 0)),
        struct((rows, width), bf16),
        [pltpu.VMEM((rows, width), bf16), pltpu.SemaphoreType.DMA],
        prefetch=1,
    )(section_layer, grad_llm, *arrived)


def slope_of(own, other, gain, bias, fc1_weight, fc1_bias):
    patches, width = own.shape
    slots = patches * 2 // 4
    depth, hidden = fc1_weight.shape
    block = block_of(hidden, 256)
    steps = hidden // block

    def body(own_ref, other_ref, gain_ref, bias_ref, fc1b_ref, fc1_ref, out_ref, x, m):
        put_rows(x, 0, own_ref[...].astype(f32))
        put_rows(x, patches, other_ref[...].astype(f32))
        gain, bias = gain_ref[...].reshape(1, width), bias_ref[...].reshape(1, width)
        for j in range(4):
            rows, _ = normalize(every_fourth(x, j, slots))
            m[:, j * width : (j + 1) * width] = (rows * gain + bias).astype(bf16)

        def step(i, carry):
            window = pl.ds(pl.multiple_of(i * block, LANES), block)
            pre_act = dot(m[...], fc1_ref[:, window]) + fc1b_ref[window].reshape(1, block)
            out_ref[:, window] = gelu_slope(pre_act)
            return carry

        lax.fori_loop(0, steps, step, 0)

    return run_kernel(
        body,
        (1,),
        [whole(x) for x in (own, other, gain, bias, fc1_bias)]
        + [RESIDENT],
        pl.BlockSpec((slots, hidden), lambda i, *_: (0, 0)),
        struct((slots, hidden), f32),
        [
            pltpu.VMEM((width // LANES, 2 * patches, LANES), f32),
            pltpu.VMEM((slots, depth), bf16),
        ],
    )(own, other, gain, bias, fc1_bias, fc1_weight)


def pre_grad_of(image_rows, vis_slot, own, other, fc2_weight, slope):
    rows, width = own.shape
    slots, hidden = slope.shape
    half = slots // 2
    llm_rows = vis_slot.shape[1]
    images = image_rows.shape[0]
    block = block_of(hidden, 256)
    steps = hidden // block

    def body(image_ref, slot_ref, own_ref, other_ref, slope_ref, fc2_ref, out_ref, merged):
        section, shard = lax.axis_index("section"), lax.axis_index("vit")
        index = lax.broadcasted_iota(jnp.int32, (slots, llm_rows), 0)
        position = ((index // half) ^ shard) * half + index % half
        live = position < image_ends(image_ref, images)[-1]
        shift = (
            lax.broadcasted_iota(jnp.int32, (llm_rows, rows), 0)
            == lax.broadcasted_iota(jnp.int32, (llm_rows, rows), 1) + section * rows
        ).astype(bf16)
        chosen = []
        for part in range(2):
            named = slot_ref[pl.ds(shard ^ part, 1), :] - section * slots
            found = ((position == named) & live).astype(f32).astype(bf16)
            chosen.append(dot(found, shift))
        chosen = jnp.concatenate(chosen, axis=1).astype(bf16)
        total = dot(chosen, jnp.concatenate([own_ref[...], other_ref[...]], axis=0))
        merged[...] = total.astype(bf16)

        def step(i, carry):
            window = pl.ds(pl.multiple_of(i * block, LANES), block)
            hidden_grad = dot(merged[...], fc2_ref[window, :], 1, 1)
            out_ref[:, window] = (hidden_grad * slope_ref[:, window]).astype(bf16)
            return carry

        lax.fori_loop(0, steps, step, 0)

    return run_kernel(
        body,
        (1,),
        [whole(x) for x in (vis_slot, own, other, slope)] + [RESIDENT],
        pl.BlockSpec((slots, hidden), lambda i, *_: (0, 0)),
        struct((slots, hidden), bf16),
        [
            pltpu.VMEM((slots, width), bf16),
        ],
        prefetch=1,
    )(image_rows, vis_slot, own, other, slope, fc2_weight)


def merge_part(pre_grad, fc1_weight, part, parts):
    slots, _ = pre_grad.shape
    columns = fc1_weight.shape[0] // parts
    block = block_of(columns, 256)
    steps = columns // block

    def body(pre_ref, fc1_ref, out_ref):
        def step(i, carry):
            window = pl.ds(pl.multiple_of(i * block, LANES), block)
            rows = pl.ds(pl.multiple_of(part * columns + i * block, LANES), block)
            out_ref[:, window] = dot(pre_ref[...], fc1_ref[rows, :], 1, 1).astype(bf16)
            return carry

        lax.fori_loop(0, steps, step, 0)

    return run_kernel(
        body,
        (1,),
        [whole(pre_grad), RESIDENT],
        pl.BlockSpec((slots, columns), lambda i, *_: (0, 0)),
        struct((slots, columns), bf16),
    )(pre_grad, fc1_weight)


def project(own, other, gain, bias, weights, head_dim):
    patches, width = own.shape
    length = 2 * patches
    slots = length // 4
    sections, copies = len(weights), len(weights[0])
    part_rows, group_cols = weights[0][0].shape
    pieces = group_cols // head_dim
    flat = [w for parts in weights for w in parts]

    def body(own_ref, other_ref, gain_ref, bias_ref, *refs):
        w_refs, (out_ref, x, n) = refs[: len(flat)], refs[len(flat) :]
        section = lax.axis_index("section")
        put_rows(x, 0, own_ref[...].astype(f32))
        put_rows(x, patches, other_ref[...].astype(f32))
        gain, bias = gain_ref[...].reshape(1, width), bias_ref[...].reshape(1, width)
        for j in range(4):
            rows, _ = normalize(every_fourth(x, j, slots))
            rows = (rows * gain + bias).astype(bf16)
            for t in range(sections):
                n[t, j * slots : (j + 1) * slots, :] = rows[:, t * part_rows : (t + 1) * part_rows]
        for p in range(copies):
            total = sum(
                dot(n[section ^ k], w_refs[k * copies + p][:, :group_cols])
                for k in range(sections)
            ).T
            for c in range(pieces):
                out_ref[p, c] = total[c * head_dim : (c + 1) * head_dim].astype(bf16)

    shape = (copies, pieces, head_dim, length)
    return run_kernel(
        body,
        (1,),
        [whole(x) for x in (own, other, gain, bias, *flat)],
        pl.BlockSpec(shape, lambda i, *_: (0, 0, 0, 0)),
        struct(shape, bf16),
        [
            pltpu.VMEM((width // LANES, length, LANES), f32),
            pltpu.VMEM((sections, length, part_rows), bf16),
        ],
        limit=30,
    )(own, other, gain, bias, *flat)


def attention_back(
    image_rows, own, other, gain, mine, theirs, proj_weight, projected, weights, head_dim
):
    patches, width = own.shape
    length = 2 * patches
    slots = length // 4
    half = slots // 2
    images = image_rows.shape[0]
    sections, copies = len(weights), len(weights[0])
    part_rows, group_cols = weights[0][0].shape
    group_heads = group_cols // (3 * head_dim)
    part_heads = part_rows // head_dim
    shard_sections = copies * group_heads // part_heads
    flat = [w for parts in weights for w in parts]
    chunks = len(mine)
    per_chunk = 4 // chunks
    score_scale = head_dim ** (-0.5)

    def body(image_ref, own_ref, other_ref, gain_ref, *refs):
        gain = gain_ref[...].reshape(1, width)
        mine_refs, refs = refs[:chunks], refs[chunks:]
        theirs_refs, refs = refs[:chunks], refs[chunks:]
        proj_ref, projected_ref, refs = refs[0], refs[1], refs[2:]
        w_refs, refs = refs[: len(flat)], refs[len(flat) :]
        own_out, other_out, grad_out, x, og, og_parts, heads, acc = refs
        section, shard, copy = (lax.axis_index(name) for name in ("section", "vit", "dp"))
        ends = image_ends(image_ref, images)
        put_rows(x, 0, own_ref[...].astype(f32))
        put_rows(x, patches, other_ref[...].astype(f32))
        for j in range(4):
            rows, inverse = normalize(every_fourth(x, j, slots))
            cols = slice(j % per_chunk * width, (j % per_chunk + 1) * width)
            there = theirs_refs[j // per_chunk][:, cols]
            there = jnp.concatenate([there[half:], there[:half]], axis=0)
            upstream = mine_refs[j // per_chunk][:, cols].astype(f32) + there.astype(f32)
            result = normalize_back(upstream, rows, inverse, gain).astype(bf16)
            og[j * slots : (j + 1) * slots, :] = result
            grad_out[j] = result[:half]
            for t in range(sections):
                og_parts[t, j * slots : (j + 1) * slots, :] = result[
                    :, t * part_rows : (t + 1) * part_rows
                ]

        def put_heads(part, cols):
            for h in range(part_heads):
                heads[part * part_heads + h] = cols[h * head_dim : (h + 1) * head_dim].astype(bf16)

        for i in range(shard_sections):
            relation = section ^ (shard * shard_sections + i)
            for k in range(sections):

                @pl.when(relation == k)
                def _(i=i, k=k):
                    if k == 0:
                        put_heads(i, dot(proj_ref[...], og[...], 1, 1))
                    else:
                        fetched = [
                            w_refs[k * copies + p][:, group_cols : group_cols + part_rows]
                            for p in range(copies)
                        ]
                        put_heads(
                            i, sum(dot(w, og_parts[copy ^ p], 1, 1) for p, w in enumerate(fetched))
                        )

        def image_of(axis):
            index = lax.broadcasted_iota(jnp.int32, (length, length), axis) % slots
            position = ((index // half) ^ shard) * half + index % half
            image = jnp.zeros((length, length), jnp.int32)
            for e in range(images):
                image += (position >= ends[e]).astype(jnp.int32)
            return image

        image = image_of(0)
        allowed = (image == image_of(1)) & (image < images)
        dead = (image_of(1)[:1] == images).astype(f32)
        for p in range(copies):
            grads = [[], [], []]
            for h in range(group_heads):
                query, key, value = (projected_ref[p, c * group_heads + h] for c in range(3))
                grad = heads[(copy ^ p) * group_heads + h]
                scores = dot(key, query, 0, 0) * score_scale
                exponent = jnp.where(allowed, jnp.exp(scores), 0.0)
                denominator = jnp.sum(exponent, axis=0, keepdims=True) + dead
                softmax_weights = (exponent / denominator).astype(bf16)
                prob_grad = dot(value, grad, 0, 0)
                weighted = softmax_weights.astype(f32)
                row_dot = jnp.sum(weighted * prob_grad, axis=0, keepdims=True)
                score_grad = (weighted * (prob_grad - row_dot) * score_scale).astype(bf16)
                grads[0].append(dot(key, score_grad))
                grads[1].append(dot(query, score_grad, 1, 1))
                grads[2].append(dot(grad, softmax_weights, 1, 1))
            group_grad = jnp.concatenate([g for gs in grads for g in gs], axis=0).astype(bf16)
            for k in range(sections):
                term = dot(w_refs[k * copies + p][:, :group_cols], group_grad)
                acc[k] = term if p == 0 else acc[k] + term

        result = jnp.concatenate([acc[section ^ t] for t in range(sections)], axis=0).T
        for j in range(4):
            own_out[j] = result[j * slots : j * slots + half]
            other_out[j] = result[j * slots + half : (j + 1) * slots].astype(bf16)

    shape = (4, half, width)
    operands = (own, other, gain, *mine, *theirs, proj_weight, projected, *flat)
    return run_kernel(
        body,
        (1,),
        [whole(x) for x in operands],
        [pl.BlockSpec(shape, lambda i, *_: (0, 0, 0))] * 3,
        [struct(shape, f32), struct(shape, bf16), struct(shape, bf16)],
        [
            pltpu.VMEM((width // LANES, length, LANES), f32),
            pltpu.VMEM((length, width), bf16),
            pltpu.VMEM((sections, length, part_rows), bf16),
            pltpu.VMEM((copies * group_heads, head_dim, length), bf16),
            pltpu.VMEM((sections, part_rows, length), f32),
        ],
        prefetch=1,
        limit=40,
    )(image_rows, *operands)


def finish(own, gain, mine, theirs, out_grad):
    patches, width = own.shape

    def body(own_ref, gain_ref, mine_ref, theirs_ref, grad_ref, out_ref, x):
        gain = gain_ref[...].reshape(1, width)
        put_rows(x, 0, own_ref[...].astype(f32))
        for j in range(4):
            rows, inverse = normalize(every_fourth(x, j, patches // 4))
            upstream = mine_ref[j] + theirs_ref[j].astype(f32)
            result = grad_ref[j].astype(f32) + normalize_back(
                upstream, rows, inverse, gain
            )
            for c in range(x.shape[0]):
                x[c, pl.ds(j, patches // 4, stride=4), :] = result[:, c * LANES : (c + 1) * LANES]
        out_ref[...] = jnp.concatenate([x[c] for c in range(x.shape[0])], axis=1).astype(bf16)

    operands = (own, gain, mine, theirs, out_grad)
    return run_kernel(
        body,
        (1,),
        [whole(x) for x in operands],
        pl.BlockSpec((patches, width), lambda i, *_: (0, 0)),
        struct((patches, width), bf16),
        [pltpu.VMEM((width // LANES, patches, LANES), f32)],
    )(*operands)


def local_paired(
    grad_llm,
    vis_slot,
    image_rows,
    section_layer,
    vit_in,
    vit_out,
    ln_gain,
    ln_bias,
    qkv_weight,
    proj_weight,
    merge_gain,
    merge_bias,
    fc1_weight,
    fc1_bias,
    fc2_weight,
):
    sections = lax.axis_size("section")
    shards = lax.axis_size("vit")
    copies = lax.axis_size("dp")
    section_index = lax.axis_index("section")
    shard_index = lax.axis_index("vit")
    copy_index = lax.axis_index("dp")
    llm_width = grad_llm.shape[2]
    vit_width = vit_in.shape[1]
    head_dim = vit_width // HEADS
    part_rows = qkv_weight.shape[0]
    group_heads = HEADS // (shards * copies)
    group_rows = grad_llm.shape[1] // sections

    def own_group(p, source):
        first = (shard_index * copies + (copy_index ^ p)) * group_heads * head_dim
        return [
            lax.dynamic_slice_in_dim(source, c * vit_width + first, group_heads * head_dim, 1)
            for c in range(3)
        ]

    image_rows = image_rows.T

    outgoing = grad_llm[0].reshape(sections, group_rows, llm_width)
    arrived = {
        k: swap(
            lax.dynamic_index_in_dim(outgoing, section_index ^ k, 0, keepdims=False), "section", k
        )
        for k in range(1, sections)
    }
    vit_out_other = swap(vit_out, "vit", 1)
    proj_cols = lax.dynamic_slice_in_dim(proj_weight, copy_index * part_rows, part_rows, 1)
    own_parts = [jnp.concatenate(own_group(p, qkv_weight), axis=1) for p in range(copies)]
    piece = jnp.concatenate([own_parts[0], proj_cols], axis=1)
    near = swap(piece, "section", 1)
    far = swap(piece, "section", 2)
    vit_in_other = swap(vit_in, "vit", 1)
    slope = slope_of(vit_out, vit_out_other, merge_gain, merge_bias, fc1_weight, fc1_bias)
    arrived, slope = lax.optimization_barrier((arrived, slope))

    summed = weighted_sum(section_layer, grad_llm, [arrived[k] for k in range(1, sections)])
    summed_other = swap(summed, "vit", 1)
    near, summed = lax.optimization_barrier((near, summed))
    near_chip = swap(near, "dp", 2)
    near_core = swap(near, "dp", 1)

    pre_grad = pre_grad_of(image_rows, vis_slot, summed, summed_other, fc2_weight, slope)
    far, near_chip, pre_grad = lax.optimization_barrier((far, near_chip, pre_grad))
    cross = swap(far, "section", 1)
    far_chip = swap(far, "dp", 2)
    near_diagonal = swap(near_chip, "dp", 1)
    far_core = swap(far, "dp", 1)
    first = merge_part(pre_grad, fc1_weight, 0, 2)
    first_theirs = swap(first, "vit", 1)
    far_chip, pre_grad, first, cross = lax.optimization_barrier((far_chip, pre_grad, first, cross))
    cross_chip = swap(cross, "dp", 2)
    far_diagonal = swap(far_chip, "dp", 1)
    cross_core = swap(cross, "dp", 1)
    second = merge_part(pre_grad, fc1_weight, 1, 2)
    second_theirs = swap(second, "vit", 1)
    second, cross_chip = lax.optimization_barrier((second, cross_chip))
    cross_diagonal = swap(cross_chip, "dp", 1)
    weights = [
        own_parts,
        [near, near_core, near_chip, near_diagonal],
        [far, far_core, far_chip, far_diagonal],
        [cross, cross_core, cross_chip, cross_diagonal],
    ]

    projected = project(vit_in, vit_in_other, ln_gain, ln_bias, weights, head_dim)
    normed_mine, normed_sent, out_grad = attention_back(
        image_rows,
        vit_out,
        vit_out_other,
        merge_gain,
        [first, second],
        [first_theirs, second_theirs],
        proj_weight,
        projected,
        weights,
        head_dim,
    )
    normed_theirs = swap(normed_sent, "vit", 1)
    return finish(vit_in, ln_gain, normed_mine, normed_theirs, out_grad)


def solution(mesh):
    paired = fits(mesh)

    def chosen_form(*arguments):
        return (local_paired if paired else local)(*arguments)

    placed = (
        P("section", ("dp", "vit"), None),
        P("dp", None),
        P("dp", None),
        P(),
        P(("dp", "section", "vit"), None),
        P(("dp", "section", "vit"), None),
        P(),
        P(),
        P("section", None),
        P("section", None),
        P(),
        P(),
        P(None, "vit"),
        P("vit"),
        P("vit", None),
    )
    return jax.shard_map(
        chosen_form,
        mesh=mesh,
        in_specs=placed,
        out_specs=P(("dp", "section", "vit"), None),
        check_vma=False,
    )
```

profile of v0, /device:TPU:20, one launch (start us, length us, event | category | flops | bytes accessed | tf_op | source)
XLA Modules:
  0.0 121.9 jit_solution(15883866371804774616)
XLA Ops:
  0.0 1.6 %collective-permute-start = (bf16[128,1152]{1,0:T(8,128)(2,1)}, bf16[128,1152]{1,0:T(8,128)(2,1)S(1)}, u32[]{:S(2)}, u32[]{:S(2)}) collective-permute-start(bf16[128,1152]{1,0:T(8,128)(2,1)} %own_ref.6), channel_id=1, source_target_pairs={{0,4},{4,0},{1,5},{5,1},{2,6},{6,2},{3,7},{7,3},{8,12},{12,8},{9,1... | collective-permute-start | bytes 884744 | tf_op jit(solution)/shard_map/ppermute | solution.py:212
  1.6 1.1 constant_dynamic-slice_fusion.9
  2.7 3.5 %constant_dynamic-slice_fusion.2 = (bf16[288,144]{1,0:T(8,128)(2,1)S(1)}, bf16[288,144]{1,0:T(8,128)(2,1)S(1)}, bf16[288,144]{1,0:T(8,128)(2,1)S(1)}, bf16[288,1...) fusion(bf16[288,3456]{1,0:T(8,128)(2,1)} %param.23, ...), kind=kLoop, calls=%fused_computation.10 | loop fusion | bytes 1990704 | tf_op jit(solution)/shard_map/dynamic_slice | solution.py:640
  6.1 1.1 pad_maximum_fusion
  7.2 1.6 %collective-permute-start.2 = (bf16[288,720]{1,0:T(8,128)(2,1)}, bf16[288,720]{1,0:T(8,128)(2,1)S(1)}, u32[]{:S(2)}, u32[]{:S(2)}) collective-permute-start(bf16[288,720]{1,0:T(8,128)(2,1)} %pad_maximum_fusion), channel_id=1, source_target_pairs={{0,8},{8,0},{16,24},{24,16},{1,9},{9,1},{17,25},{25,17},{2,10},{10... | collective-permute-start | bytes 1244168 | tf_op jit(solution)/shard_map/ppermute | solution.py:212
  8.8 1.2 dynamic-slice_bitcast_fusion
  9.9 0.1 collective-permute-start.5
  10.0 2.8 %collective-permute-start.4 = (bf16[32,4096]{1,0:T(8,128)(2,1)S(1)}, bf16[32,4096]{1,0:T(8,128)(2,1)S(1)}, u32[]{:S(2)}, u32[]{:S(2)}) collective-permute-start(bf16[32,4096]{1,0:T(8,128)(2,1)S(1)} %get-tuple-element.54), channel_id=1, source_target_pairs={{0,16},{8,24},{16,0},{24,8},{1,17},{9,25},{17,1},{25,9},{2,18},{10... | collective-permute-start | bytes 786440 | tf_op jit(solution)/shard_map/ppermute | solution.py:212
  12.8 0.7 collective-permute-start.3
  13.5 1.2 %collective-permute-start.1 = (bf16[288,720]{1,0:T(8,128)(2,1)}, bf16[288,720]{1,0:T(8,128)(2,1)S(1)}, u32[]{:S(2)}, u32[]{:S(2)}) collective-permute-start(bf16[288,720]{1,0:T(8,128)(2,1)} %pad_maximum_fusion), channel_id=1, source_target_pairs={{0,16},{8,24},{16,0},{24,8},{1,17},{9,25},{17,1},{25,9},{2,18},{10... | collective-permute-start | bytes 1244168 | tf_op jit(solution)/shard_map/ppermute | solution.py:212
  14.7 7.0 %copy-done = bf16[4608,2304]{1,0:T(8,128)(2,1)S(1)} copy-done((bf16[4608,2304]{1,0:T(8,128)(2,1)S(1)}, bf16[4608,2304]{1,0:T(8,128)(2,1)}, u32[]{:S(2)}) %copy-start) | copy-done | bytes 21233688
  21.8 1.0 copy-done.5
  22.7 0.7 copy-done.7
  23.4 0.7 copy-done.10
  24.1 0.7 copy-done.11
  24.8 5.5 %shard_map.145.slope_ref = f32[64,2304]{1,0:T(8,128)S(1)} custom-call(bf16[128,1152]{1,0:T(8,128)(2,1)S(1)} %copy-done.5, bf16[128,1152]{1,0:T(8,128)(2,1)S(1)} %collective-permute-done.other_ref, f32[1152]{0:T(1024)S(1)} %copy-done.7, f32[1152]{0:T(1024)S(1)} %copy-done.11, f32[2304]{0:T(1024)S(1)} %copy-done.10, bf16[4608,2304]{1,0:T(8,128)(2,1)S(1)} %copy-done), custom_call_target="tpu_custom_call" | custom-call | tf_op jit(solution)/shard_map/pallas_call | solution.py:330
  30.3 3.4 %collective-permute-done.4.refs_1_ = bf16[32,4096]{1,0:T(8,128)(2,1)S(1)} collective-permute-done((bf16[32,4096]{1,0:T(8,128)(2,1)S(1)}, bf16[32,4096]{1,0:T(8,128)(2,1)S(1)}, u32[]{:S(2)}, u32[]{:S(2)}) %collective-permute-start.4) | collective-permute-done | bytes 262176 | tf_op jit(solution)/shard_map/ppermute | solution.py:212
  33.7 3.6 %collective-permute-done.3.refs_0_ = bf16[32,4096]{1,0:T(8,128)(2,1)S(1)} collective-permute-done((bf16[32,4096]{1,0:T(8,128)(2,1)S(1)}, bf16[32,4096]{1,0:T(8,128)(2,1)S(1)}, u32[]{:S(2)}, u32[]{:S(2)}) %collective-permute-start.3) | collective-permute-done | bytes 262176 | tf_op jit(solution)/shard_map/ppermute | solution.py:212
  37.4 0.9 shard_map.146.own_ref
  38.2 0.5 collective-permute-start.6
  38.8 0.6 collective-permute-start.7
  39.3 5.8 %collective-permute-done.7.other_ref = bf16[32,4096]{1,0:T(8,128)(2,1)S(1)} collective-permute-done((bf16[32,4096]{1,0:T(8,128)(2,1)S(1)}, bf16[32,4096]{1,0:T(8,128)(2,1)S(1)}, u32[]{:S(2)}, u32[]{:S(2)}) %collective-permute-start.7) | collective-permute-done | bytes 262176 | tf_op jit(solution)/shard_map/ppermute | solution.py:212
  45.1 6.4 %copy-done.1 = bf16[2304,4096]{1,0:T(8,128)(2,1)S(1)} copy-done((bf16[2304,4096]{1,0:T(8,128)(2,1)S(1)}, bf16[2304,4096]{1,0:T(8,128)(2,1)}, u32[]{:S(2)}) %copy-start.1) | copy-done | bytes 18874392
  51.5 7.9 %shard_map.147.pre_ref = bf16[64,2304]{1,0:T(8,128)(2,1)S(1)} custom-call(s32[2,4]{1,0:T(2,128)S(1)} %bitcast.11, s32[2,128]{1,0:T(2,128)S(1)} %copy-done.14, bf16[32,4096]{1,0:T(8,128)(2,1)S(1)} %shard_map.146.own_ref, bf16[32,4096]{1,0:T(8,128)(2,1)S(1)} %collective-permute-done.7.other_ref, f32[64,2304]{1,0:T(8,128)S(1)} %shard_map.145.slope_ref, ...), custom_call_target="tpu_custom_call" | custom-call | tf_op jit(solution)/shard_map/pallas_call | solution.py:379
  59.5 9.8 %collective-permute-start.9 = (bf16[288,720]{1,0:T(8,128)(2,1)S(1)}, bf16[288,720]{1,0:T(8,128)(2,1)S(1)}, u32[]{:S(2)}, u32[]{:S(2)}) collective-permute-start(bf16[288,720]{1,0:T(8,128)(2,1)S(1)} %collective-permute-done.1.refs_8_.refs_14_), channel_id=1, source_target_pairs={{0,8},{8,0},{16,24},{24,16},{1,9},{9,1},{17,25},{25,17},{2,10},{10... | collective-permute-start | bytes 1244168 | tf_op jit(solution)/shard_map/ppermute | solution.py:212
  69.3 1.5 %collective-permute-start.8 = (bf16[288,720]{1,0:T(8,128)(2,1)S(1)}, bf16[288,720]{1,0:T(8,128)(2,1)S(1)}, u32[]{:S(2)}, u32[]{:S(2)}) collective-permute-start(bf16[288,720]{1,0:T(8,128)(2,1)S(1)} %collective-permute-done.1.refs_8_.refs_14_), channel_id=1, source_target_pairs={{0,2},{1,3},{2,0},{3,1},{4,6},{5,7},{6,4},{7,5},{8,10},{9,11},{10,... | collective-permute-start | bytes 1244168 | tf_op jit(solution)/shard_map/ppermute | solution.py:212
  70.9 4.5 %shard_map.148.refs_0_ = bf16[64,2304]{1,0:T(8,128)(2,1)S(1)} custom-call(bf16[64,2304]{1,0:T(8,128)(2,1)S(1)} %shard_map.147.pre_ref, bf16[4608,2304]{1,0:T(8,128)(2,1)S(1)} %bitcast.9), custom_call_target="tpu_custom_call" | custom-call | tf_op jit(solution)/shard_map/pallas_call | solution.py:407
  75.4 0.1 collective-permute-done.9.refs_12_.refs_18_
  75.6 2.0 %collective-permute-done.8.refs_10_.refs_16_ = bf16[288,720]{1,0:T(8,128)(2,1)S(1)} collective-permute-done((bf16[288,720]{1,0:T(8,128)(2,1)S(1)}, bf16[288,720]{1,0:T(8,128)(2,1)S(1)}, u32[]{:S(2)}, u32[]{:S(2)}) %collective-permute-start.8) | collective-permute-done | bytes 414752 | tf_op jit(solution)/shard_map/ppermute | solution.py:212
  77.6 1.5 %collective-permute-start.10 = (bf16[288,720]{1,0:T(8,128)(2,1)S(1)}, bf16[288,720]{1,0:T(8,128)(2,1)S(1)}, u32[]{:S(2)}, u32[]{:S(2)}) collective-permute-start(bf16[288,720]{1,0:T(8,128)(2,1)S(1)} %collective-permute-done.9.refs_12_.refs_18_), channel_id=1, source_target_pairs={{0,2},{1,3},{2,0},{3,1},{4,6},{5,7},{6,4},{7,5},{8,10},{9,11},{10,... | collective-permute-start | bytes 1244168 | tf_op jit(solution)/shard_map/ppermute | solution.py:212
  79.1 0.6 collective-permute-start.13
  79.7 0.2 collective-permute-start.15
  79.9 0.3 collective-permute-start.16
  80.2 4.5 %shard_map.149.refs_1_ = bf16[64,2304]{1,0:T(8,128)(2,1)S(1)} custom-call(bf16[64,2304]{1,0:T(8,128)(2,1)S(1)} %shard_map.147.pre_ref, bf16[4608,2304]{1,0:T(8,128)(2,1)S(1)} %bitcast.9), custom_call_target="tpu_custom_call" | custom-call | tf_op jit(solution)/shard_map/pallas_call | solution.py:407
  84.7 1.2 collective-permute-done.10.refs_14_.refs_20_
  85.9 2.6 %collective-permute-done.13.other_ref = bf16[128,1152]{1,0:T(8,128)(2,1)S(1)} collective-permute-done((bf16[128,1152]{1,0:T(8,128)(2,1)S(1)}, bf16[128,1152]{1,0:T(8,128)(2,1)S(1)}, u32[]{:S(2)}, u32[]{:S(2)}) %collective-permute-start.13) | collective-permute-done | bytes 294944 | tf_op jit(solution)/shard_map/ppermute | solution.py:212
  88.5 0.5 collective-permute-start.19
  89.1 0.6 collective-permute-start.11
  89.6 1.5 %collective-permute-start.12 = (bf16[64,2304]{1,0:T(8,128)(2,1)S(1)}, bf16[64,2304]{1,0:T(8,128)(2,1)S(1)}, u32[]{:S(2)}, u32[]{:S(2)}) collective-permute-start(bf16[64,2304]{1,0:T(8,128)(2,1)S(1)} %shard_map.149.refs_1_), channel_id=1, source_target_pairs={{0,4},{4,0},{1,5},{5,1},{2,6},{6,2},{3,7},{7,3},{8,12},{12,8},{9,1... | collective-permute-start | bytes 884744 | tf_op jit(solution)/shard_map/ppermute | solution.py:212
  91.1 0.3 pad_maximum_fusion.1
  91.4 0.3 pad_maximum_fusion.3
  91.8 3.0 %shard_map.150.refs_5_ = bf16[4,6,72,256]{3,2,1,0:T(8,128)(2,1)S(1)} custom-call(bf16[128,1152]{1,0:T(8,128)(2,1)S(1)} %copy-done.4, bf16[128,1152]{1,0:T(8,128)(2,1)S(1)} %collective-permute-done.13.other_ref, f32[1152]{0:T(1024)S(1)} %copy-done.9, f32[1152]{0:T(1024)S(1)} %copy-done.12, bf16[288,432]{1,0:T(8,128)(2,1)S(1)} %get-tuple-element.56.refs_0_.refs_6_, ...), custom_call_target="tpu_custom_call" | custom-call | tf_op jit(solution)/shard_map/pallas_call | solution.py:445
  94.9 4.1 %collective-permute-done.11.refs_2_ = bf16[64,2304]{1,0:T(8,128)(2,1)S(1)} collective-permute-done((bf16[64,2304]{1,0:T(8,128)(2,1)S(1)}, bf16[64,2304]{1,0:T(8,128)(2,1)S(1)}, u32[]{:S(2)}, u32[]{:S(2)}) %collective-permute-start.11) | collective-permute-done | bytes 294944 | tf_op jit(solution)/shard_map/ppermute | solution.py:212
  98.9 5.4 %collective-permute-done.12.refs_3_ = bf16[64,2304]{1,0:T(8,128)(2,1)S(1)} collective-permute-done((bf16[64,2304]{1,0:T(8,128)(2,1)S(1)}, bf16[64,2304]{1,0:T(8,128)(2,1)S(1)}, u32[]{:S(2)}, u32[]{:S(2)}) %collective-permute-start.12) | collective-permute-done | bytes 294944 | tf_op jit(solution)/shard_map/ppermute | solution.py:212
  104.4 8.1 %shard_map.151 = (f32[4,32,1152]{2,1,0:T(8,128)S(1)}, bf16[4,32,1152]{2,1,0:T(8,128)(2,1)S(1)}, bf16[4,32,1152]{2,1,0:T(8,128)(2,1)S(1)}) custom-call(s32[2,4]{1,0:T(2,128)S(1)} %bitcast.12, bf16[128,1152]{1,0:T(8,128)(2,1)S(1)} %copy-done.6, bf16[128,1152]{1,0:T(8,128)(2,1)S(1)} %collective-permute-done.other_ref, f32[1152]{0:T(1024)S(1)} %copy-done.8, ...), custom_call_target="tpu_custom_call" | custom-call | tf_op jit(solution)/shard_map/pallas_call | solution.py:562
  112.5 0.5 collective-permute-start.20
  112.9 7.7 %collective-permute-done.20.theirs_ref = bf16[4,32,1152]{2,1,0:T(8,128)(2,1)S(1)} collective-permute-done((bf16[4,32,1152]{2,1,0:T(8,128)(2,1)S(1)}, bf16[4,32,1152]{2,1,0:T(8,128)(2,1)S(1)}, u32[]{:S(2)}, u32[]{:S(2)}) %collective-permute-start.20) | collective-permute-done | bytes 294944 | tf_op jit(solution)/shard_map/ppermute | solution.py:212
  120.6 1.3 %shard_map.152 = bf16[128,1152]{1,0:T(8,128)(2,1)} custom-call(bf16[128,1152]{1,0:T(8,128)(2,1)S(1)} %copy-done.4, f32[1152]{0:T(1024)S(1)} %copy-done.9, f32[4,32,1152]{2,1,0:T(8,128)S(1)} %get-tuple-element.38.mine_ref, bf16[4,32,1152]{2,1,0:T(8,128)(2,1)S(1)} %collective-permute-done.20.theirs_ref, bf16[4,32,1152]{2,1,0:T(8,128)(2,1)S(1)} %get-tuple-element.40.grad_ref), custom_call_target="tpu_custom_call" | custom-call | tf_op jit(solution)/shard_map/pallas_call | solution.py:597
  (55 shorter events, 0.1 us)
Async XLA Ops:
  0.0 37.3 %copy-start.2 = (bf16[1,128,4096]{2,1,0:T(8,128)(2,1)S(1)}, bf16[1,128,4096]{2,1,0:T(8,128)(2,1)}, u32[]{:S(2)}) copy-start(bf16[1,128,4096]{2,1,0:T(8,128)(2,1)} %grad_ref.1) | copy-start | bytes 3145732
  0.0 37.3 %copy-start.15 = (s32[4]{0:T(128)S(1)}, s32[4]{0:T(128)}, u32[]{:S(2)}) copy-start(s32[4]{0:T(128)} %layer_ref.1) | copy-start | bytes 52
  0.0 45.1 %copy-start.13 = (s32[4,2]{0,1:T(2,128)S(1)}, s32[4,2]{0,1:T(2,128)}, u32[]{:S(2)}) copy-start(s32[4,2]{0,1:T(2,128)} %param.17) | copy-start | bytes 100
  0.0 45.1 %copy-start.14 = (s32[2,128]{1,0:T(2,128)S(1)}, s32[2,128]{1,0:T(2,128)}, u32[]{:S(2)}) copy-start(s32[2,128]{1,0:T(2,128)} %slot_ref.1) | copy-start | bytes 3076
  0.0 13.5 %collective-permute-start = (bf16[128,1152]{1,0:T(8,128)(2,1)}, bf16[128,1152]{1,0:T(8,128)(2,1)S(1)}, u32[]{:S(2)}, u32[]{:S(2)}) collective-permute-start(bf16[128,1152]{1,0:T(8,128)(2,1)} %own_ref.6), channel_id=1, source_target_pairs={{0,4},{4,0},{1,5},{5,1},{2,6},{6,2},{3,7},{7,3},{8,12},{12,8},{9,1... | collective-permute-start | bytes 884744 | tf_op jit(solution)/shard_map/ppermute | solution.py:212
  7.2 31.0 %collective-permute-start.2 = (bf16[288,720]{1,0:T(8,128)(2,1)}, bf16[288,720]{1,0:T(8,128)(2,1)S(1)}, u32[]{:S(2)}, u32[]{:S(2)}) collective-permute-start(bf16[288,720]{1,0:T(8,128)(2,1)} %pad_maximum_fusion), channel_id=1, source_target_pairs={{0,8},{8,0},{16,24},{24,16},{1,9},{9,1},{17,25},{25,17},{2,10},{10... | collective-permute-start | bytes 1244168 | tf_op jit(solution)/shard_map/ppermute | solution.py:212
  9.9 20.4 %collective-permute-start.5 = (bf16[32,4096]{1,0:T(8,128)(2,1)S(1)}, bf16[32,4096]{1,0:T(8,128)(2,1)S(1)}, u32[]{:S(2)}, u32[]{:S(2)}) collective-permute-start(bf16[32,4096]{1,0:T(8,128)(2,1)S(1)} %get-tuple-element.53), channel_id=1, source_target_pairs={{0,24},{8,16},{16,8},{24,0},{1,25},{9,17},{17,9},{25,1},{2,26},{10... | collective-permute-start | bytes 786440 | tf_op jit(solution)/shard_map/ppermute | solution.py:212
  10.0 23.7 %collective-permute-start.4 = (bf16[32,4096]{1,0:T(8,128)(2,1)S(1)}, bf16[32,4096]{1,0:T(8,128)(2,1)S(1)}, u32[]{:S(2)}, u32[]{:S(2)}) collective-permute-start(bf16[32,4096]{1,0:T(8,128)(2,1)S(1)} %get-tuple-element.54), channel_id=1, source_target_pairs={{0,16},{8,24},{16,0},{24,8},{1,17},{9,25},{17,1},{25,9},{2,18},{10... | collective-permute-start | bytes 786440 | tf_op jit(solution)/shard_map/ppermute | solution.py:212
  12.8 24.5 %collective-permute-start.3 = (bf16[32,4096]{1,0:T(8,128)(2,1)S(1)}, bf16[32,4096]{1,0:T(8,128)(2,1)S(1)}, u32[]{:S(2)}, u32[]{:S(2)}) collective-permute-start(bf16[32,4096]{1,0:T(8,128)(2,1)S(1)} %get-tuple-element.55), channel_id=1, source_target_pairs={{0,8},{8,0},{16,24},{24,16},{1,9},{9,1},{17,25},{25,17},{2,10},{10... | collective-permute-start | bytes 786440 | tf_op jit(solution)/shard_map/ppermute | solution.py:212
  13.5 46.0 %collective-permute-start.1 = (bf16[288,720]{1,0:T(8,128)(2,1)}, bf16[288,720]{1,0:T(8,128)(2,1)S(1)}, u32[]{:S(2)}, u32[]{:S(2)}) collective-permute-start(bf16[288,720]{1,0:T(8,128)(2,1)} %pad_maximum_fusion), channel_id=1, source_target_pairs={{0,16},{8,24},{16,0},{24,8},{1,17},{9,25},{17,1},{25,9},{2,18},{10... | collective-permute-start | bytes 1244168 | tf_op jit(solution)/shard_map/ppermute | solution.py:212
  14.7 7.0 %copy-start = (bf16[4608,2304]{1,0:T(8,128)(2,1)S(1)}, bf16[4608,2304]{1,0:T(8,128)(2,1)}, u32[]{:S(2)}) copy-start(bf16[4608,2304]{1,0:T(8,128)(2,1)} %fc1_ref.5) | copy-start | bytes 63700996
  21.8 1.0 copy-start.5
  22.7 0.7 copy-start.7
  23.4 0.7 copy-start.10
  24.1 0.7 copy-start.11
  24.8 46.0 %slice-start = ((s8[21233664]{0:T(1024)(128)(4,1)}), s8[262144]{0:T(1024)(128)(4,1)S(1)}, s32[]{:S(2)}) async-start(s8[21233664]{0:T(1024)(128)(4,1)} %bitcast.8), calls=%async_computation | async-start | bytes 524288
  24.8 46.0 %slice-start.1 = ((s8[21233664]{0:T(1024)(128)(4,1)}), s8[4194304]{0:T(1024)(128)(4,1)S(1)}, s32[]{:S(2)}) async-start(s8[21233664]{0:T(1024)(128)(4,1)} %bitcast.8), calls=%async_computation.1 | async-start | bytes 8388608
  24.8 46.0 %slice-start.2 = ((s8[21233664]{0:T(1024)(128)(4,1)}), s8[4194304]{0:T(1024)(128)(4,1)S(1)}, s32[]{:S(2)}) async-start(s8[21233664]{0:T(1024)(128)(4,1)} %bitcast.8), calls=%async_computation.2 | async-start | bytes 8388608
  24.8 46.0 %slice-start.3 = ((s8[21233664]{0:T(1024)(128)(4,1)}), s8[4194304]{0:T(1024)(128)(4,1)S(1)}, s32[]{:S(2)}) async-start(s8[21233664]{0:T(1024)(128)(4,1)} %bitcast.8), calls=%async_computation.3 | async-start | bytes 8388608
  38.2 21.3 %collective-permute-start.6 = (bf16[288,720]{1,0:T(8,128)(2,1)S(1)}, bf16[288,720]{1,0:T(8,128)(2,1)S(1)}, u32[]{:S(2)}, u32[]{:S(2)}) collective-permute-start(bf16[288,720]{1,0:T(8,128)(2,1)S(1)} %collective-permute-done.2.refs_4_.refs_10_), channel_id=1, source_target_pairs={{0,2},{1,3},{2,0},{3,1},{4,6},{5,7},{6,4},{7,5},{8,10},{9,11},{10,... | collective-permute-start | bytes 1244168 | tf_op jit(solution)/shard_map/ppermute | solution.py:212
  38.8 6.4 %collective-permute-start.7 = (bf16[32,4096]{1,0:T(8,128)(2,1)S(1)}, bf16[32,4096]{1,0:T(8,128)(2,1)S(1)}, u32[]{:S(2)}, u32[]{:S(2)}) collective-permute-start(bf16[32,4096]{1,0:T(8,128)(2,1)S(1)} %shard_map.146.own_ref), channel_id=1, source_target_pairs={{0,4},{4,0},{1,5},{5,1},{2,6},{6,2},{3,7},{7,3},{8,12},{12,8},{9,1... | collective-permute-start | bytes 786440 | tf_op jit(solution)/shard_map/ppermute | solution.py:212
  45.1 6.4 %copy-start.1 = (bf16[2304,4096]{1,0:T(8,128)(2,1)S(1)}, bf16[2304,4096]{1,0:T(8,128)(2,1)}, u32[]{:S(2)}) copy-start(bf16[2304,4096]{1,0:T(8,128)(2,1)} %fc2_ref.1) | copy-start | bytes 56623108
  51.5 19.3 %slice-start.4 = ((s8[21233664]{0:T(1024)(128)(4,1)}), s8[4194304]{0:T(1024)(128)(4,1)S(1)}, s32[]{:S(2)}) async-start(s8[21233664]{0:T(1024)(128)(4,1)} %bitcast.8), calls=%async_computation.4 | async-start | bytes 8388608
  51.5 19.3 %slice-start.5 = ((s8[21233664]{0:T(1024)(128)(4,1)}), s8[4194304]{0:T(1024)(128)(4,1)S(1)}, s32[]{:S(2)}) async-start(s8[21233664]{0:T(1024)(128)(4,1)} %bitcast.8), calls=%async_computation.5 | async-start | bytes 8388608
  51.5 27.6 %copy-start.4 = (bf16[128,1152]{1,0:T(8,128)(2,1)S(1)}, bf16[128,1152]{1,0:T(8,128)(2,1)}, u32[]{:S(2)}) copy-start(bf16[128,1152]{1,0:T(8,128)(2,1)} %own_ref.7) | copy-start | bytes 884740
  59.4 31.6 %copy-start.16 = (bf16[288,144]{1,0:T(8,128)(2,1)S(1)}, bf16[288,144]{1,0:T(8,128)(2,1)}, u32[]{:S(2)}) copy-start(bf16[288,144]{1,0:T(8,128)(2,1)} %get-tuple-element.47) | copy-start | bytes 248836
  59.5 32.4 %copy-start.9 = (f32[1152]{0:T(1024)S(1)}, f32[1152]{0:T(1024)}, u32[]{:S(2)}) copy-start(f32[1152]{0:T(1024)} %gain_ref.7) | copy-start | bytes 13828
  59.5 32.4 %copy-start.12 = (f32[1152]{0:T(1024)S(1)}, f32[1152]{0:T(1024)}, u32[]{:S(2)}) copy-start(f32[1152]{0:T(1024)} %bias_ref.3) | copy-start | bytes 13828
  59.5 16.1 %collective-permute-start.9 = (bf16[288,720]{1,0:T(8,128)(2,1)S(1)}, bf16[288,720]{1,0:T(8,128)(2,1)S(1)}, u32[]{:S(2)}, u32[]{:S(2)}) collective-permute-start(bf16[288,720]{1,0:T(8,128)(2,1)S(1)} %collective-permute-done.1.refs_8_.refs_14_), channel_id=1, source_target_pairs={{0,8},{8,0},{16,24},{24,16},{1,9},{9,1},{17,25},{25,17},{2,10},{10... | collective-permute-start | bytes 1244168 | tf_op jit(solution)/shard_map/ppermute | solution.py:212
  69.3 8.3 %collective-permute-start.8 = (bf16[288,720]{1,0:T(8,128)(2,1)S(1)}, bf16[288,720]{1,0:T(8,128)(2,1)S(1)}, u32[]{:S(2)}, u32[]{:S(2)}) collective-permute-start(bf16[288,720]{1,0:T(8,128)(2,1)S(1)} %collective-permute-done.1.refs_8_.refs_14_), channel_id=1, source_target_pairs={{0,2},{1,3},{2,0},{3,1},{4,6},{5,7},{6,4},{7,5},{8,10},{9,11},{10,... | collective-permute-start | bytes 1244168 | tf_op jit(solution)/shard_map/ppermute | solution.py:212
  75.4 29.0 %copy-start.3 = (bf16[288,1152]{1,0:T(8,128)(2,1)S(1)}, bf16[288,1152]{1,0:T(8,128)(2,1)}, u32[]{:S(2)}) copy-start(bf16[288,1152]{1,0:T(8,128)(2,1)} %refs_4_.1) | copy-start | bytes 1990660
  75.4 29.0 %copy-start.6 = (bf16[128,1152]{1,0:T(8,128)(2,1)S(1)}, bf16[128,1152]{1,0:T(8,128)(2,1)}, u32[]{:S(2)}) copy-start(bf16[128,1152]{1,0:T(8,128)(2,1)} %own_ref.6) | copy-start | bytes 884740
  75.4 28.9 %copy-start.8 = (f32[1152]{0:T(1024)S(1)}, f32[1152]{0:T(1024)}, u32[]{:S(2)}) copy-start(f32[1152]{0:T(1024)} %gain_ref.6) | copy-start | bytes 13828
  77.6 8.3 %collective-permute-start.10 = (bf16[288,720]{1,0:T(8,128)(2,1)S(1)}, bf16[288,720]{1,0:T(8,128)(2,1)S(1)}, u32[]{:S(2)}, u32[]{:S(2)}) collective-permute-start(bf16[288,720]{1,0:T(8,128)(2,1)S(1)} %collective-permute-done.9.refs_12_.refs_18_), channel_id=1, source_target_pairs={{0,2},{1,3},{2,0},{3,1},{4,6},{5,7},{6,4},{7,5},{8,10},{9,11},{10,... | collective-permute-start | bytes 1244168 | tf_op jit(solution)/shard_map/ppermute | solution.py:212
  79.1 9.4 %collective-permute-start.14 = (bf16[288,720]{1,0:T(8,128)(2,1)S(1)}, bf16[288,720]{1,0:T(8,128)(2,1)S(1)}, u32[]{:S(2)}, u32[]{:S(2)}) collective-permute-start(bf16[288,720]{1,0:T(8,128)(2,1)S(1)} %collective-permute-done.2.refs_4_.refs_10_), channel_id=1, source_target_pairs={{0,1},{1,0},{2,3},{3,2},{4,5},{5,4},{6,7},{7,6},{8,9},{9,8},{10,11... | collective-permute-start | bytes 1244168 | tf_op jit(solution)/shard_map/ppermute | solution.py:212
  79.1 9.4 %collective-permute-start.13 = (bf16[128,1152]{1,0:T(8,128)(2,1)S(1)}, bf16[128,1152]{1,0:T(8,128)(2,1)S(1)}, u32[]{:S(2)}, u32[]{:S(2)}) collective-permute-start(bf16[128,1152]{1,0:T(8,128)(2,1)S(1)} %copy-done.4), channel_id=1, source_target_pairs={{0,4},{4,0},{1,5},{5,1},{2,6},{6,2},{3,7},{7,3},{8,12},{12,8},{9,1... | collective-permute-start | bytes 884744 | tf_op jit(solution)/shard_map/ppermute | solution.py:212
  79.7 9.4 %collective-permute-start.15 = (bf16[288,720]{1,0:T(8,128)(2,1)S(1)}, bf16[288,720]{1,0:T(8,128)(2,1)S(1)}, u32[]{:S(2)}, u32[]{:S(2)}) collective-permute-start(bf16[288,720]{1,0:T(8,128)(2,1)S(1)} %collective-permute-done.6.refs_6_.refs_12_), channel_id=1, source_target_pairs={{0,1},{1,0},{2,3},{3,2},{4,5},{5,4},{6,7},{7,6},{8,9},{9,8},{10,11... | collective-permute-start | bytes 1244168 | tf_op jit(solution)/shard_map/ppermute | solution.py:212
  79.9 9.7 %collective-permute-start.16 = (bf16[288,720]{1,0:T(8,128)(2,1)S(1)}, bf16[288,720]{1,0:T(8,128)(2,1)S(1)}, u32[]{:S(2)}, u32[]{:S(2)}) collective-permute-start(bf16[288,720]{1,0:T(8,128)(2,1)S(1)} %collective-permute-done.1.refs_8_.refs_14_), channel_id=1, source_target_pairs={{0,1},{1,0},{2,3},{3,2},{4,5},{5,4},{6,7},{7,6},{8,9},{9,8},{10,11... | collective-permute-start | bytes 1244168 | tf_op jit(solution)/shard_map/ppermute | solution.py:212
  85.9 5.9 %collective-permute-start.18 = (bf16[288,720]{1,0:T(8,128)(2,1)S(1)}, bf16[288,720]{1,0:T(8,128)(2,1)S(1)}, u32[]{:S(2)}, u32[]{:S(2)}) collective-permute-start(bf16[288,720]{1,0:T(8,128)(2,1)S(1)} %collective-permute-done.9.refs_12_.refs_18_), channel_id=1, source_target_pairs={{0,1},{1,0},{2,3},{3,2},{4,5},{5,4},{6,7},{7,6},{8,9},{9,8},{10,11... | collective-permute-start | bytes 1244168 | tf_op jit(solution)/shard_map/ppermute | solution.py:212
  88.5 3.2 %collective-permute-start.17 = (bf16[288,720]{1,0:T(8,128)(2,1)S(1)}, bf16[288,720]{1,0:T(8,128)(2,1)S(1)}, u32[]{:S(2)}, u32[]{:S(2)}) collective-permute-start(bf16[288,720]{1,0:T(8,128)(2,1)S(1)} %collective-permute-done.8.refs_10_.refs_16_), channel_id=1, source_target_pairs={{0,1},{1,0},{2,3},{3,2},{4,5},{5,4},{6,7},{7,6},{8,9},{9,8},{10,11... | collective-permute-start | bytes 1244168 | tf_op jit(solution)/shard_map/ppermute | solution.py:212
  88.5 3.3 %collective-permute-start.19 = (bf16[288,720]{1,0:T(8,128)(2,1)S(1)}, bf16[288,720]{1,0:T(8,128)(2,1)S(1)}, u32[]{:S(2)}, u32[]{:S(2)}) collective-permute-start(bf16[288,720]{1,0:T(8,128)(2,1)S(1)} %collective-permute-done.10.refs_14_.refs_20_), channel_id=1, source_target_pairs={{0,1},{1,0},{2,3},{3,2},{4,5},{5,4},{6,7},{7,6},{8,9},{9,8},{10,11... | collective-permute-start | bytes 1244168 | tf_op jit(solution)/shard_map/ppermute | solution.py:212
  89.1 9.9 %collective-permute-start.11 = (bf16[64,2304]{1,0:T(8,128)(2,1)S(1)}, bf16[64,2304]{1,0:T(8,128)(2,1)S(1)}, u32[]{:S(2)}, u32[]{:S(2)}) collective-permute-start(bf16[64,2304]{1,0:T(8,128)(2,1)S(1)} %shard_map.148.refs_0_), channel_id=1, source_target_pairs={{0,4},{4,0},{1,5},{5,1},{2,6},{6,2},{3,7},{7,3},{8,12},{12,8},{9,1... | collective-permute-start | bytes 884744 | tf_op jit(solution)/shard_map/ppermute | solution.py:212
  89.6 14.7 %collective-permute-start.12 = (bf16[64,2304]{1,0:T(8,128)(2,1)S(1)}, bf16[64,2304]{1,0:T(8,128)(2,1)S(1)}, u32[]{:S(2)}, u32[]{:S(2)}) collective-permute-start(bf16[64,2304]{1,0:T(8,128)(2,1)S(1)} %shard_map.149.refs_1_), channel_id=1, source_target_pairs={{0,4},{4,0},{1,5},{5,1},{2,6},{6,2},{3,7},{7,3},{8,12},{12,8},{9,1... | collective-permute-start | bytes 884744 | tf_op jit(solution)/shard_map/ppermute | solution.py:212
  112.5 8.2 %collective-permute-start.20 = (bf16[4,32,1152]{2,1,0:T(8,128)(2,1)S(1)}, bf16[4,32,1152]{2,1,0:T(8,128)(2,1)S(1)}, u32[]{:S(2)}, u32[]{:S(2)}) collective-permute-start(bf16[4,32,1152]{2,1,0:T(8,128)(2,1)S(1)} %get-tuple-element.39), channel_id=1, source_target_pairs={{0,4},{4,0},{1,5},{5,1},{2,6},{6,2},{3,7},{7,3},{8,12},{12,8},{9,1... | collective-permute-start | bytes 884744 | tf_op jit(solution)/shard_map/ppermute | solution.py:212
where the time goes:
time: 122 us
  waiting for transfers between devices  36 us (30%)
  Pallas kernels  35.7 us (29%)
  starting transfers between devices  25.9 us (21%)
  local copies, waits for them, and re-layouts  22.2 us (18%)
  other arithmetic  1.76 us (1%)
    ppermute x21, waiting for transfers between devices, swap(): return lax.ppermute(values, axis, [(i, i ^ bit) for i in range(count)])  36 us
    ppermute x21, starting transfers between devices, swap(): return lax.ppermute(values, axis, [(i, i ^ bit) for i in range(count)])  25.9 us
    unnamed x46, local copies, waits for them, and re-layouts  16.5 us
    pallas_call x2, Pallas kernels, merge_part(): run_kernel(body, (1,), [whole(pre_grad), RESIDENT], pl.BlockSpec((slots,...  9.05 us
    pallas_call x1, Pallas kernels, attention_back(): run_kernel(body, (1,), [whole(x) for x in operands], [pl.BlockSpec(shape,...  8.07 us
    pallas_call x1, Pallas kernels, pre_grad_of(): run_kernel(body, (1,), [whole(x) for x in (vis_slot, own, other, slope)]...  7.93 us
    pallas_call x1, Pallas kernels, slope_of(): run_kernel(body, (1,), [whole(x) for x in (own, other, gain, bias, fc1_bi...  5.47 us
    dynamic_slice x1, local copies, waits for them, and re-layouts, own_group(): lax.dynamic_slice_in_dim(source, c * vit_width + first, group_heads * hea...  3.46 us
  transfers between devices with their start and end apart: 21, of which 10 were waited for; matrix products, arithmetic and copies ran while one was open for 6% of the time, Pallas kernels for 22%

commit v1 on v0

--- a/solution.py
+++ b/solution.py
@@ -225,7 +225,7 @@
     return max(b for b in range(128, limit + 1, 128) if size % b == 0)
 
 
-def run_kernel(body, grid, in_specs, out_specs, out_shape, scratch=(), prefetch=0, limit=10):
+def run_kernel(body, grid, in_specs, out_specs, out_shape, scratch=(), prefetch=0, limit=10, cost=0):
     return pl.pallas_call(
         body,
         grid_spec=pltpu.PrefetchScalarGridSpec(
@@ -236,6 +236,9 @@
             scratch_shapes=list(scratch),
         ),
         out_shape=out_shape,
+        cost_estimate=pl.CostEstimate(flops=cost, transcendentals=0, bytes_accessed=0)
+        if cost
+        else None,
         compiler_params=pltpu.CompilerParams(
             dimension_semantics=("arbitrary",) * len(grid), vmem_limit_bytes=limit << 20
         ),
@@ -254,6 +257,7 @@
 
 
 LANES = 128
+COST = 8_000_000_000
 
 
 def put_rows(ref, first, values):
@@ -301,7 +305,42 @@
         struct((rows, width), bf16),
         [pltpu.VMEM((rows, width), bf16), pltpu.SemaphoreType.DMA],
         prefetch=1,
+        limit=4,
     )(section_layer, grad_llm, *arrived)
+
+
+def own_columns(qkv_weight, proj_weight, shards, copies):
+    part_rows, width = proj_weight.shape
+    group = qkv_weight.shape[1] // (3 * shards * copies)
+
+    def body(qkv_ref, proj_ref, piece_ref, *part_refs):
+        place = lax.axis_index("vit") * copies + lax.axis_index("dp")
+        for v in range(shards):
+            for q in range(copies):
+
+                @pl.when(place == v * copies + q)
+                def _(v=v, q=q):
+                    for p in range(copies):
+                        first = (v * copies + (q ^ p)) * group
+                        cols = jnp.concatenate(
+                            [qkv_ref[:, c * width + first : c * width + first + group] for c in range(3)],
+                            axis=1,
+                        )
+                        part_refs[p][...] = cols
+                        if p == 0:
+                            columns = proj_ref[:, q * part_rows : (q + 1) * part_rows]
+                            piece_ref[...] = jnp.concatenate([cols, columns], axis=1)
+
+    shapes = [(part_rows, 3 * group + part_rows)] + [(part_rows, 3 * group)] * copies
+    return run_kernel(
+        body,
+        (1,),
+        [whole(qkv_weight), whole(proj_weight)],
+        [pl.BlockSpec(shape, lambda i, *_: (0, 0)) for shape in shapes],
+        [struct(shape, bf16) for shape in shapes],
+        limit=16,
+        cost=COST,
+    )(qkv_weight, proj_weight)
 
 
 def slope_of(own, other, gain, bias, fc1_weight, fc1_bias):
@@ -338,6 +377,8 @@
             pltpu.VMEM((width // LANES, 2 * patches, LANES), f32),
             pltpu.VMEM((slots, depth), bf16),
         ],
+        cost=COST,
+        limit=5,
     )(own, other, gain, bias, fc1_bias, fc1_weight)
 
 
@@ -350,7 +391,15 @@
     block = block_of(hidden, 256)
     steps = hidden // block
 
-    def body(image_ref, slot_ref, own_ref, other_ref, slope_ref, fc2_ref, out_ref, merged):
+    def body(
+        image_ref, slot_ref, own_ref, other_ref, slope_ref, fc2_ref, out_ref, merged, buffer, sems
+    ):
+        def fetch(i):
+            rows_here = pl.ds(pl.multiple_of(i * block, LANES), block)
+            return pltpu.make_async_copy(fc2_ref.at[rows_here, :], buffer.at[i], sems.at[i])
+
+        for i in range(steps):
+            fetch(i).start()
         section, shard = lax.axis_index("section"), lax.axis_index("vit")
         index = lax.broadcasted_iota(jnp.int32, (slots, llm_rows), 0)
         position = ((index // half) ^ shard) * half + index % half
@@ -370,7 +419,8 @@
 
         def step(i, carry):
             window = pl.ds(pl.multiple_of(i * block, LANES), block)
-            hidden_grad = dot(merged[...], fc2_ref[window, :], 1, 1)
+            fetch(i).wait()
+            hidden_grad = dot(merged[...], buffer[i], 1, 1)
             out_ref[:, window] = (hidden_grad * slope_ref[:, window]).astype(bf16)
             return carry
 
@@ -379,14 +429,24 @@
     return run_kernel(
         body,
         (1,),
-        [whole(x) for x in (vis_slot, own, other, slope)] + [RESIDENT],
+        [whole(x) for x in (vis_slot, own, other, slope)] + [pl.BlockSpec(memory_space=pltpu.HBM)],
         pl.BlockSpec((slots, hidden), lambda i, *_: (0, 0)),
         struct((slots, hidden), bf16),
         [
             pltpu.VMEM((slots, width), bf16),
+            pltpu.VMEM((steps, block, width), bf16),
+            pltpu.SemaphoreType.DMA((steps,)),
         ],
         prefetch=1,
-    )(image_rows, vis_slot, own, other, slope, fc2_weight)
+        limit=22,
+    )(
+        image_rows,
+        vis_slot,
+        own,
+        other,
+        slope,
+        pltpu.with_memory_space_constraint(fc2_weight, pltpu.HBM),
+    )
 
 
 def merge_part(pre_grad, fc1_weight, part, parts):
@@ -410,6 +470,7 @@
         [whole(pre_grad), RESIDENT],
         pl.BlockSpec((slots, columns), lambda i, *_: (0, 0)),
         struct((slots, columns), bf16),
+        limit=2,
     )(pre_grad, fc1_weight)
 
 
@@ -625,22 +686,10 @@
     shards = lax.axis_size("vit")
     copies = lax.axis_size("dp")
     section_index = lax.axis_index("section")
-    shard_index = lax.axis_index("vit")
-    copy_index = lax.axis_index("dp")
     llm_width = grad_llm.shape[2]
     vit_width = vit_in.shape[1]
     head_dim = vit_width // HEADS
-    part_rows = qkv_weight.shape[0]
-    group_heads = HEADS // (shards * copies)
     group_rows = grad_llm.shape[1] // sections
-
-    def own_group(p, source):
-        first = (shard_index * copies + (copy_index ^ p)) * group_heads * head_dim
-        return [
-            lax.dynamic_slice_in_dim(source, c * vit_width + first, group_heads * head_dim, 1)
-            for c in range(3)
-        ]
-
     image_rows = image_rows.T
 
     outgoing = grad_llm[0].reshape(sections, group_rows, llm_width)
@@ -651,9 +700,7 @@
         for k in range(1, sections)
     }
     vit_out_other = swap(vit_out, "vit", 1)
-    proj_cols = lax.dynamic_slice_in_dim(proj_weight, copy_index * part_rows, part_rows, 1)
-    own_parts = [jnp.concatenate(own_group(p, qkv_weight), axis=1) for p in range(copies)]
-    piece = jnp.concatenate([own_parts[0], proj_cols], axis=1)
+    piece, *own_parts = own_columns(qkv_weight, proj_weight, shards, copies)
     near = swap(piece, "section", 1)
     far = swap(piece, "section", 2)
     vit_in_other = swap(vit_in, "vit", 1)
@@ -662,7 +709,7 @@
 
     summed = weighted_sum(section_layer, grad_llm, [arrived[k] for k in range(1, sections)])
     summed_other = swap(summed, "vit", 1)
-    near, summed = lax.optimization_barrier((near, summed))
+    near, summed_other = lax.optimization_barrier((near, summed_other))
     near_chip = swap(near, "dp", 2)
     near_core = swap(near, "dp", 1)
 

time: 122 us -> 109 us (0.89)
  the two profiles are of different devices: /device:TPU:20 before, /device:TPU:0 now
where the time goes in v1:
time: 109 us
  waiting for transfers between devices  45.8 us (42%)
  Pallas kernels  37.5 us (34%)
  starting transfers between devices  21.3 us (20%)
  local copies, waits for them, and re-layouts  4.53 us (4%)
    ppermute x21, waiting for transfers between devices, swap(): return lax.ppermute(values, axis, [(i, i ^ bit) for i in range(count)])  45.8 us
    ppermute x21, starting transfers between devices, swap(): return lax.ppermute(values, axis, [(i, i ^ bit) for i in range(count)])  21.3 us
    pallas_call x1, Pallas kernels, pre_grad_of(): run_kernel(body, (1,), [whole(x) for x in (vis_slot, own, other, slope)]...  9.4 us
    pallas_call x2, Pallas kernels, merge_part(): run_kernel(body, (1,), [whole(pre_grad), RESIDENT], pl.BlockSpec((slots,...  9.05 us
    pallas_call x1, Pallas kernels, attention_back(): run_kernel(body, (1,), [whole(x) for x in operands], [pl.BlockSpec(shape,...  7.91 us
    pallas_call x1, Pallas kernels, slope_of(): run_kernel(body, (1,), [whole(x) for x in (own, other, gain, bias, fc1_bi...  5.47 us
    unnamed x30, local copies, waits for them, and re-layouts  3.22 us
    pallas_call x1, Pallas kernels, project(): run_kernel(body, (1,), [whole(x) for x in (own, other, gain, bias, *flat)...  3.03 us
  transfers between devices with their start and end apart: 21, of which 10 were waited for; matrix products, arithmetic and copies ran while one was open for 1% of the time, Pallas kernels for 26%

profile of v1, /device:TPU:0, one launch (start us, length us, event | category | flops | bytes accessed | tf_op | source)
XLA Modules:
  0.0 109.3 jit_solution(13765135151894735052)
XLA Ops:
  0.0 3.0 %collective-permute-start = (bf16[128,1152]{1,0:T(8,128)(2,1)}, bf16[128,1152]{1,0:T(8,128)(2,1)S(1)}, u32[]{:S(2)}, u32[]{:S(2)}) collective-permute-start(bf16[128,1152]{1,0:T(8,128)(2,1)} %own_ref.6), channel_id=1, source_target_pairs={{0,4},{4,0},{1,5},{5,1},{2,6},{6,2},{3,7},{7,3},{8,12},{12,8},{9,1... | collective-permute-start | bytes 884744 | tf_op jit(solution)/shard_map/ppermute | solution.py:212
  3.0 1.3 %dynamic-slice_bitcast_fusion = (bf16[32,4096]{1,0:T(8,128)(2,1)S(1)}, bf16[32,4096]{1,0:T(8,128)(2,1)S(1)}, bf16[32,4096]{1,0:T(8,128)(2,1)S(1)}) fusion(bf16[4,32,4096]{2,1,0:T(8,128)(2,1)} %bitcast.8, s32[]{:T(128)S(6)} %select_n.12, s32[]{:T(128)S(6)} %select_n.11, s32[]{:T(128)S(6)} %select_n.10), kind=kLoop, calls=%fused_computation | loop fusion | bytes 1572876 | tf_op jit(solution)/shard_map/jit(dynamic_index_in_dim)/squeeze | solution.py:698
  4.4 3.7 %collective-permute-start.5 = (bf16[32,4096]{1,0:T(8,128)(2,1)S(1)}, bf16[32,4096]{1,0:T(8,128)(2,1)S(1)}, u32[]{:S(2)}, u32[]{:S(2)}) collective-permute-start(bf16[32,4096]{1,0:T(8,128)(2,1)S(1)} %get-tuple-element.51), channel_id=1, source_target_pairs={{0,24},{8,16},{16,8},{24,0},{1,25},{9,17},{17,9},{25,1},{2,26},{10... | collective-permute-start | bytes 786440 | tf_op jit(solution)/shard_map/ppermute | solution.py:212
  8.0 0.0 collective-permute-start.4
  8.0 0.8 collective-permute-start.3
  8.8 1.6 %copy-done.3 = bf16[288,1152]{1,0:T(8,128)(2,1)S(1)} copy-done((bf16[288,1152]{1,0:T(8,128)(2,1)S(1)}, bf16[288,1152]{1,0:T(8,128)(2,1)}, u32[]{:S(2)}) %copy-start.3) | copy-done | bytes 663576
  10.4 1.6 %copy-done.12 = bf16[288,3456]{1,0:T(8,128)(2,1)S(1)} copy-done((bf16[288,3456]{1,0:T(8,128)(2,1)S(1)}, bf16[288,3456]{1,0:T(8,128)(2,1)}, u32[]{:S(2)}) %copy-start.12) | copy-done | bytes 1990680
  12.0 0.5 shard_map.145
  12.5 0.0 copy-start.1
  12.5 0.0 copy-start.11
  12.5 0.0 copy-start.9
  12.5 0.0 copy-start.10
  12.5 1.6 %collective-permute-start.2 = (bf16[288,720]{1,0:T(8,128)(2,1)S(1)}, bf16[288,720]{1,0:T(8,128)(2,1)S(1)}, u32[]{:S(2)}, u32[]{:S(2)}) collective-permute-start(bf16[288,720]{1,0:T(8,128)(2,1)S(1)} %get-tuple-element.28), channel_id=1, source_target_pairs={{0,8},{8,0},{16,24},{24,16},{1,9},{9,1},{17,25},{25,17},{2,10},{10... | collective-permute-start | bytes 1244168 | tf_op jit(solution)/shard_map/ppermute | solution.py:212
  14.1 0.0 collective-permute-done.other_ref
  14.1 5.5 %shard_map.146.slope_ref = f32[64,2304]{1,0:T(8,128)S(1)} custom-call(bf16[128,1152]{1,0:T(8,128)(2,1)S(1)} %copy-done.5, bf16[128,1152]{1,0:T(8,128)(2,1)S(1)} %collective-permute-done.other_ref, f32[1152]{0:T(1024)S(1)} %copy-done.7, f32[1152]{0:T(1024)S(1)} %copy-done.14, f32[2304]{0:T(1024)S(1)} %copy-done.13, bf16[4608,2304]{1,0:T(8,128)(2,1)S(1)} %copy-done), custom_call_target="tpu_custom_call" | custom-call | flops 8000000000 | tf_op jit(solution)/shard_map/pallas_call | solution.py:369
  19.6 10.5 %collective-permute-done.4.refs_1_ = bf16[32,4096]{1,0:T(8,128)(2,1)S(1)} collective-permute-done((bf16[32,4096]{1,0:T(8,128)(2,1)S(1)}, bf16[32,4096]{1,0:T(8,128)(2,1)S(1)}, u32[]{:S(2)}, u32[]{:S(2)}) %collective-permute-start.4) | collective-permute-done | bytes 262176 | tf_op jit(solution)/shard_map/ppermute | solution.py:212
  30.2 0.0 collective-permute-done.3.refs_0_
  30.2 0.9 shard_map.147.own_ref
  31.0 0.6 collective-permute-start.6
  31.6 4.1 %collective-permute-done.2.refs_4_.refs_10_ = bf16[288,720]{1,0:T(8,128)(2,1)S(1)} collective-permute-done((bf16[288,720]{1,0:T(8,128)(2,1)S(1)}, bf16[288,720]{1,0:T(8,128)(2,1)S(1)}, u32[]{:S(2)}, u32[]{:S(2)}) %collective-permute-start.2) | collective-permute-done | bytes 414752 | tf_op jit(solution)/shard_map/ppermute | solution.py:212
  35.8 2.7 %collective-permute-done.6.other_ref = bf16[32,4096]{1,0:T(8,128)(2,1)S(1)} collective-permute-done((bf16[32,4096]{1,0:T(8,128)(2,1)S(1)}, bf16[32,4096]{1,0:T(8,128)(2,1)S(1)}, u32[]{:S(2)}, u32[]{:S(2)}) %collective-permute-start.6) | collective-permute-done | bytes 262176 | tf_op jit(solution)/shard_map/ppermute | solution.py:212
  38.4 1.5 %collective-permute-start.7 = (bf16[288,720]{1,0:T(8,128)(2,1)S(1)}, bf16[288,720]{1,0:T(8,128)(2,1)S(1)}, u32[]{:S(2)}, u32[]{:S(2)}) collective-permute-start(bf16[288,720]{1,0:T(8,128)(2,1)S(1)} %collective-permute-done.2.refs_4_.refs_10_), channel_id=1, source_target_pairs={{0,2},{1,3},{2,0},{3,1},{4,6},{5,7},{6,4},{7,5},{8,10},{9,11},{10,... | collective-permute-start | bytes 1244168 | tf_op jit(solution)/shard_map/ppermute | solution.py:212
  40.0 9.4 %shard_map.148.pre_ref = bf16[64,2304]{1,0:T(8,128)(2,1)S(1)} custom-call(s32[2,4]{1,0:T(2,128)S(1)} %bitcast.9, s32[2,128]{1,0:T(2,128)S(1)} %copy-done.10, bf16[32,4096]{1,0:T(8,128)(2,1)S(1)} %shard_map.147.own_ref, bf16[32,4096]{1,0:T(8,128)(2,1)S(1)} %collective-permute-done.6.other_ref, f32[64,2304]{1,0:T(8,128)S(1)} %shard_map.146.slope_ref, ...), custom_call_target="tpu_custom_call" | custom-call | tf_op jit(solution)/shard_map/pallas_call | solution.py:429
  49.4 0.0 copy-start.6
  49.4 0.0 copy-start.8
  49.4 3.3 %collective-permute-done.1.refs_8_.refs_14_ = bf16[288,720]{1,0:T(8,128)(2,1)S(1)} collective-permute-done((bf16[288,720]{1,0:T(8,128)(2,1)S(1)}, bf16[288,720]{1,0:T(8,128)(2,1)S(1)}, u32[]{:S(2)}, u32[]{:S(2)}) %collective-permute-start.1) | collective-permute-done | bytes 414752 | tf_op jit(solution)/shard_map/ppermute | solution.py:212
  52.7 1.5 %collective-permute-start.8 = (bf16[288,720]{1,0:T(8,128)(2,1)S(1)}, bf16[288,720]{1,0:T(8,128)(2,1)S(1)}, u32[]{:S(2)}, u32[]{:S(2)}) collective-permute-start(bf16[288,720]{1,0:T(8,128)(2,1)S(1)} %collective-permute-done.1.refs_8_.refs_14_), channel_id=1, source_target_pairs={{0,2},{1,3},{2,0},{3,1},{4,6},{5,7},{6,4},{7,5},{8,10},{9,11},{10,... | collective-permute-start | bytes 1244168 | tf_op jit(solution)/shard_map/ppermute | solution.py:212
  54.2 4.5 %shard_map.149.refs_0_ = bf16[64,2304]{1,0:T(8,128)(2,1)S(1)} custom-call(bf16[64,2304]{1,0:T(8,128)(2,1)S(1)} %shard_map.148.pre_ref, bf16[4608,2304]{1,0:T(8,128)(2,1)S(1)} %copy-done), custom_call_target="tpu_custom_call" | custom-call | tf_op jit(solution)/shard_map/pallas_call | solution.py:467
  58.8 0.0 copy-start.4
  58.8 5.0 %collective-permute-done.9.refs_12_.refs_18_ = bf16[288,720]{1,0:T(8,128)(2,1)S(1)} collective-permute-done((bf16[288,720]{1,0:T(8,128)(2,1)S(1)}, bf16[288,720]{1,0:T(8,128)(2,1)S(1)}, u32[]{:S(2)}, u32[]{:S(2)}) %collective-permute-start.9) | collective-permute-done | bytes 414752 | tf_op jit(solution)/shard_map/ppermute | solution.py:212
  63.8 0.0 collective-permute-done.8.refs_10_.refs_16_
  63.8 1.5 %collective-permute-start.10 = (bf16[288,720]{1,0:T(8,128)(2,1)S(1)}, bf16[288,720]{1,0:T(8,128)(2,1)S(1)}, u32[]{:S(2)}, u32[]{:S(2)}) collective-permute-start(bf16[288,720]{1,0:T(8,128)(2,1)S(1)} %collective-permute-done.9.refs_12_.refs_18_), channel_id=1, source_target_pairs={{0,2},{1,3},{2,0},{3,1},{4,6},{5,7},{6,4},{7,5},{8,10},{9,11},{10,... | collective-permute-start | bytes 1244168 | tf_op jit(solution)/shard_map/ppermute | solution.py:212
  65.4 2.1 %collective-permute-start.13 = (bf16[128,1152]{1,0:T(8,128)(2,1)S(1)}, bf16[128,1152]{1,0:T(8,128)(2,1)S(1)}, u32[]{:S(2)}, u32[]{:S(2)}) collective-permute-start(bf16[128,1152]{1,0:T(8,128)(2,1)S(1)} %copy-done.2), channel_id=1, source_target_pairs={{0,4},{4,0},{1,5},{5,1},{2,6},{6,2},{3,7},{7,3},{8,12},{12,8},{9,1... | collective-permute-start | bytes 884744 | tf_op jit(solution)/shard_map/ppermute | solution.py:212
  67.5 0.2 collective-permute-start.15
  67.7 0.3 collective-permute-start.16
  68.0 4.5 %shard_map.150.refs_1_ = bf16[64,2304]{1,0:T(8,128)(2,1)S(1)} custom-call(bf16[64,2304]{1,0:T(8,128)(2,1)S(1)} %shard_map.148.pre_ref, bf16[4608,2304]{1,0:T(8,128)(2,1)S(1)} %copy-done), custom_call_target="tpu_custom_call" | custom-call | tf_op jit(solution)/shard_map/pallas_call | solution.py:467
  72.5 1.6 %collective-permute-done.10.refs_14_.refs_20_ = bf16[288,720]{1,0:T(8,128)(2,1)S(1)} collective-permute-done((bf16[288,720]{1,0:T(8,128)(2,1)S(1)}, bf16[288,720]{1,0:T(8,128)(2,1)S(1)}, u32[]{:S(2)}, u32[]{:S(2)}) %collective-permute-start.10) | collective-permute-done | bytes 414752 | tf_op jit(solution)/shard_map/ppermute | solution.py:212
  74.1 1.0 collective-permute-done.13.other_ref
  75.2 0.5 collective-permute-start.19
  75.7 1.9 %collective-permute-start.11 = (bf16[64,2304]{1,0:T(8,128)(2,1)S(1)}, bf16[64,2304]{1,0:T(8,128)(2,1)S(1)}, u32[]{:S(2)}, u32[]{:S(2)}) collective-permute-start(bf16[64,2304]{1,0:T(8,128)(2,1)S(1)} %shard_map.149.refs_0_), channel_id=1, source_target_pairs={{0,4},{4,0},{1,5},{5,1},{2,6},{6,2},{3,7},{7,3},{8,12},{12,8},{9,1... | collective-permute-start | bytes 884744 | tf_op jit(solution)/shard_map/ppermute | solution.py:212
  77.5 0.2 collective-permute-start.12
  77.7 3.0 %shard_map.151.refs_5_ = bf16[4,6,72,256]{3,2,1,0:T(8,128)(2,1)S(1)} custom-call(bf16[128,1152]{1,0:T(8,128)(2,1)S(1)} %copy-done.2, bf16[128,1152]{1,0:T(8,128)(2,1)S(1)} %collective-permute-done.13.other_ref, f32[1152]{0:T(1024)S(1)} %copy-done.6, f32[1152]{0:T(1024)S(1)} %copy-done.8, bf16[288,432]{1,0:T(8,128)(2,1)S(1)} %get-tuple-element.41.refs_0_.refs_6_, ...), custom_call_target="tpu_custom_call" | custom-call | tf_op jit(solution)/shard_map/pallas_call | solution.py:506
  80.8 4.8 %collective-permute-done.11.refs_2_ = bf16[64,2304]{1,0:T(8,128)(2,1)S(1)} collective-permute-done((bf16[64,2304]{1,0:T(8,128)(2,1)S(1)}, bf16[64,2304]{1,0:T(8,128)(2,1)S(1)}, u32[]{:S(2)}, u32[]{:S(2)}) %collective-permute-start.11) | collective-permute-done | bytes 294944 | tf_op jit(solution)/shard_map/ppermute | solution.py:212
  85.5 5.9 %collective-permute-done.12.refs_3_ = bf16[64,2304]{1,0:T(8,128)(2,1)S(1)} collective-permute-done((bf16[64,2304]{1,0:T(8,128)(2,1)S(1)}, bf16[64,2304]{1,0:T(8,128)(2,1)S(1)}, u32[]{:S(2)}, u32[]{:S(2)}) %collective-permute-start.12) | collective-permute-done | bytes 294944 | tf_op jit(solution)/shard_map/ppermute | solution.py:212
  91.4 7.9 %shard_map.152 = (f32[4,32,1152]{2,1,0:T(8,128)S(1)}, bf16[4,32,1152]{2,1,0:T(8,128)(2,1)S(1)}, bf16[4,32,1152]{2,1,0:T(8,128)(2,1)S(1)}) custom-call(s32[2,4]{1,0:T(2,128)S(1)} %bitcast.10, bf16[128,1152]{1,0:T(8,128)(2,1)S(1)} %copy-done.5, bf16[128,1152]{1,0:T(8,128)(2,1)S(1)} %collective-permute-done.other_ref, f32[1152]{0:T(1024)S(1)} %copy-done.7, ...), custom_call_target="tpu_custom_call" | custom-call | tf_op jit(solution)/shard_map/pallas_call | solution.py:623
  99.4 1.9 %collective-permute-start.20 = (bf16[4,32,1152]{2,1,0:T(8,128)(2,1)S(1)}, bf16[4,32,1152]{2,1,0:T(8,128)(2,1)S(1)}, u32[]{:S(2)}, u32[]{:S(2)}) collective-permute-start(bf16[4,32,1152]{2,1,0:T(8,128)(2,1)S(1)} %get-tuple-element.49), channel_id=1, source_target_pairs={{0,4},{4,0},{1,5},{5,1},{2,6},{6,2},{3,7},{7,3},{8,12},{12,8},{9,1... | collective-permute-start | bytes 884744 | tf_op jit(solution)/shard_map/ppermute | solution.py:212
  101.3 6.8 %collective-permute-done.20.theirs_ref = bf16[4,32,1152]{2,1,0:T(8,128)(2,1)S(1)} collective-permute-done((bf16[4,32,1152]{2,1,0:T(8,128)(2,1)S(1)}, bf16[4,32,1152]{2,1,0:T(8,128)(2,1)S(1)}, u32[]{:S(2)}, u32[]{:S(2)}) %collective-permute-start.20) | collective-permute-done | bytes 294944 | tf_op jit(solution)/shard_map/ppermute | solution.py:212
  108.1 1.3 %shard_map.153 = bf16[128,1152]{1,0:T(8,128)(2,1)} custom-call(bf16[128,1152]{1,0:T(8,128)(2,1)S(1)} %copy-done.2, f32[1152]{0:T(1024)S(1)} %copy-done.6, f32[4,32,1152]{2,1,0:T(8,128)S(1)} %get-tuple-element.48.mine_ref, bf16[4,32,1152]{2,1,0:T(8,128)(2,1)S(1)} %collective-permute-done.20.theirs_ref, bf16[4,32,1152]{2,1,0:T(8,128)(2,1)S(1)} %get-tuple-element.50.grad_ref), custom_call_target="tpu_custom_call" | custom-call | tf_op jit(solution)/shard_map/pallas_call | solution.py:658
  (34 shorter events, 0.1 us)
Async XLA Ops:
  0.0 14.1 %copy-start.7 = (f32[1152]{0:T(1024)S(1)}, f32[1152]{0:T(1024)}, u32[]{:S(2)}) copy-start(f32[1152]{0:T(1024)} %gain_ref.6) | copy-start | bytes 13828
  0.0 14.1 %copy-start.13 = (f32[2304]{0:T(1024)S(1)}, f32[2304]{0:T(1024)}, u32[]{:S(2)}) copy-start(f32[2304]{0:T(1024)} %fc1b_ref.1) | copy-start | bytes 27652
  0.0 14.1 %copy-start.14 = (f32[1152]{0:T(1024)S(1)}, f32[1152]{0:T(1024)}, u32[]{:S(2)}) copy-start(f32[1152]{0:T(1024)} %bias_ref.2) | copy-start | bytes 13828
  0.0 14.1 %collective-permute-start = (bf16[128,1152]{1,0:T(8,128)(2,1)}, bf16[128,1152]{1,0:T(8,128)(2,1)S(1)}, u32[]{:S(2)}, u32[]{:S(2)}) collective-permute-start(bf16[128,1152]{1,0:T(8,128)(2,1)} %own_ref.6), channel_id=1, source_target_pairs={{0,4},{4,0},{1,5},{5,1},{2,6},{6,2},{3,7},{7,3},{8,12},{12,8},{9,1... | collective-permute-start | bytes 884744 | tf_op jit(solution)/shard_map/ppermute | solution.py:212
  3.0 11.1 %copy-start = (bf16[4608,2304]{1,0:T(8,128)(2,1)S(1)}, bf16[4608,2304]{1,0:T(8,128)(2,1)}, u32[]{:S(2)}) copy-start(bf16[4608,2304]{1,0:T(8,128)(2,1)} %fc1_ref.5) | copy-start | bytes 63700996
  4.4 15.2 %collective-permute-start.5 = (bf16[32,4096]{1,0:T(8,128)(2,1)S(1)}, bf16[32,4096]{1,0:T(8,128)(2,1)S(1)}, u32[]{:S(2)}, u32[]{:S(2)}) collective-permute-start(bf16[32,4096]{1,0:T(8,128)(2,1)S(1)} %get-tuple-element.51), channel_id=1, source_target_pairs={{0,24},{8,16},{16,8},{24,0},{1,25},{9,17},{17,9},{25,1},{2,26},{10... | collective-permute-start | bytes 786440 | tf_op jit(solution)/shard_map/ppermute | solution.py:212
  8.0 22.1 %collective-permute-start.4 = (bf16[32,4096]{1,0:T(8,128)(2,1)S(1)}, bf16[32,4096]{1,0:T(8,128)(2,1)S(1)}, u32[]{:S(2)}, u32[]{:S(2)}) collective-permute-start(bf16[32,4096]{1,0:T(8,128)(2,1)S(1)} %get-tuple-element.52), channel_id=1, source_target_pairs={{0,16},{8,24},{16,0},{24,8},{1,17},{9,25},{17,1},{25,9},{2,18},{10... | collective-permute-start | bytes 786440 | tf_op jit(solution)/shard_map/ppermute | solution.py:212
  8.0 22.1 %collective-permute-start.3 = (bf16[32,4096]{1,0:T(8,128)(2,1)S(1)}, bf16[32,4096]{1,0:T(8,128)(2,1)S(1)}, u32[]{:S(2)}, u32[]{:S(2)}) collective-permute-start(bf16[32,4096]{1,0:T(8,128)(2,1)S(1)} %get-tuple-element.53), channel_id=1, source_target_pairs={{0,8},{8,0},{16,24},{24,16},{1,9},{9,1},{17,25},{25,17},{2,10},{10... | collective-permute-start | bytes 786440 | tf_op jit(solution)/shard_map/ppermute | solution.py:212
  8.8 1.6 %copy-start.3 = (bf16[288,1152]{1,0:T(8,128)(2,1)S(1)}, bf16[288,1152]{1,0:T(8,128)(2,1)}, u32[]{:S(2)}) copy-start(bf16[288,1152]{1,0:T(8,128)(2,1)} %refs_4_.1) | copy-start | bytes 1990660
  10.4 1.6 %copy-start.12 = (bf16[288,3456]{1,0:T(8,128)(2,1)S(1)}, bf16[288,3456]{1,0:T(8,128)(2,1)}, u32[]{:S(2)}) copy-start(bf16[288,3456]{1,0:T(8,128)(2,1)} %qkv_ref.1) | copy-start | bytes 5971972
  12.0 2.1 %copy-start.5 = (bf16[128,1152]{1,0:T(8,128)(2,1)S(1)}, bf16[128,1152]{1,0:T(8,128)(2,1)}, u32[]{:S(2)}) copy-start(bf16[128,1152]{1,0:T(8,128)(2,1)} %own_ref.6) | copy-start | bytes 884740
  12.5 17.7 %copy-start.1 = (bf16[1,128,4096]{2,1,0:T(8,128)(2,1)S(1)}, bf16[1,128,4096]{2,1,0:T(8,128)(2,1)}, u32[]{:S(2)}) copy-start(bf16[1,128,4096]{2,1,0:T(8,128)(2,1)} %grad_ref.1) | copy-start | bytes 3145732
  12.5 17.7 %copy-start.11 = (s32[4]{0:T(128)S(1)}, s32[4]{0:T(128)}, u32[]{:S(2)}) copy-start(s32[4]{0:T(128)} %layer_ref.1) | copy-start | bytes 52
  12.5 27.5 %copy-start.9 = (s32[4,2]{0,1:T(2,128)S(1)}, s32[4,2]{0,1:T(2,128)}, u32[]{:S(2)}) copy-start(s32[4,2]{0,1:T(2,128)} %param.17) | copy-start | bytes 100
  12.5 27.4 %copy-start.10 = (s32[2,128]{1,0:T(2,128)S(1)}, s32[2,128]{1,0:T(2,128)}, u32[]{:S(2)}) copy-start(s32[2,128]{1,0:T(2,128)} %slot_ref.1) | copy-start | bytes 3076
  12.5 23.2 %collective-permute-start.2 = (bf16[288,720]{1,0:T(8,128)(2,1)S(1)}, bf16[288,720]{1,0:T(8,128)(2,1)S(1)}, u32[]{:S(2)}, u32[]{:S(2)}) collective-permute-start(bf16[288,720]{1,0:T(8,128)(2,1)S(1)} %get-tuple-element.28), channel_id=1, source_target_pairs={{0,8},{8,0},{16,24},{24,16},{1,9},{9,1},{17,25},{25,17},{2,10},{10... | collective-permute-start | bytes 1244168 | tf_op jit(solution)/shard_map/ppermute | solution.py:212
  31.0 7.4 %collective-permute-start.6 = (bf16[32,4096]{1,0:T(8,128)(2,1)S(1)}, bf16[32,4096]{1,0:T(8,128)(2,1)S(1)}, u32[]{:S(2)}, u32[]{:S(2)}) collective-permute-start(bf16[32,4096]{1,0:T(8,128)(2,1)S(1)} %shard_map.147.own_ref), channel_id=1, source_target_pairs={{0,4},{4,0},{1,5},{5,1},{2,6},{6,2},{3,7},{7,3},{8,12},{12,8},{9,1... | collective-permute-start | bytes 786440 | tf_op jit(solution)/shard_map/ppermute | solution.py:212
  31.6 21.1 %collective-permute-start.1 = (bf16[288,720]{1,0:T(8,128)(2,1)S(1)}, bf16[288,720]{1,0:T(8,128)(2,1)S(1)}, u32[]{:S(2)}, u32[]{:S(2)}) collective-permute-start(bf16[288,720]{1,0:T(8,128)(2,1)S(1)} %get-tuple-element.28), channel_id=1, source_target_pairs={{0,16},{8,24},{16,0},{24,8},{1,17},{9,25},{17,1},{25,9},{2,18},{10... | collective-permute-start | bytes 1244168 | tf_op jit(solution)/shard_map/ppermute | solution.py:212
  38.4 14.3 %collective-permute-start.7 = (bf16[288,720]{1,0:T(8,128)(2,1)S(1)}, bf16[288,720]{1,0:T(8,128)(2,1)S(1)}, u32[]{:S(2)}, u32[]{:S(2)}) collective-permute-start(bf16[288,720]{1,0:T(8,128)(2,1)S(1)} %collective-permute-done.2.refs_4_.refs_10_), channel_id=1, source_target_pairs={{0,2},{1,3},{2,0},{3,1},{4,6},{5,7},{6,4},{7,5},{8,10},{9,11},{10,... | collective-permute-start | bytes 1244168 | tf_op jit(solution)/shard_map/ppermute | solution.py:212
  40.0 25.4 %copy-start.2 = (bf16[128,1152]{1,0:T(8,128)(2,1)S(1)}, bf16[128,1152]{1,0:T(8,128)(2,1)}, u32[]{:S(2)}) copy-start(bf16[128,1152]{1,0:T(8,128)(2,1)} %own_ref.7) | copy-start | bytes 884740
  49.4 28.3 %copy-start.6 = (f32[1152]{0:T(1024)S(1)}, f32[1152]{0:T(1024)}, u32[]{:S(2)}) copy-start(f32[1152]{0:T(1024)} %gain_ref.7) | copy-start | bytes 13828
  49.4 28.3 %copy-start.8 = (f32[1152]{0:T(1024)S(1)}, f32[1152]{0:T(1024)}, u32[]{:S(2)}) copy-start(f32[1152]{0:T(1024)} %bias_ref.3) | copy-start | bytes 13828
  52.7 11.1 %collective-permute-start.9 = (bf16[288,720]{1,0:T(8,128)(2,1)S(1)}, bf16[288,720]{1,0:T(8,128)(2,1)S(1)}, u32[]{:S(2)}, u32[]{:S(2)}) collective-permute-start(bf16[288,720]{1,0:T(8,128)(2,1)S(1)} %collective-permute-done.1.refs_8_.refs_14_), channel_id=1, source_target_pairs={{0,8},{8,0},{16,24},{24,16},{1,9},{9,1},{17,25},{25,17},{2,10},{10... | collective-permute-start | bytes 1244168 | tf_op jit(solution)/shard_map/ppermute | solution.py:212
  52.7 11.1 %collective-permute-start.8 = (bf16[288,720]{1,0:T(8,128)(2,1)S(1)}, bf16[288,720]{1,0:T(8,128)(2,1)S(1)}, u32[]{:S(2)}, u32[]{:S(2)}) collective-permute-start(bf16[288,720]{1,0:T(8,128)(2,1)S(1)} %collective-permute-done.1.refs_8_.refs_14_), channel_id=1, source_target_pairs={{0,2},{1,3},{2,0},{3,1},{4,6},{5,7},{6,4},{7,5},{8,10},{9,11},{10,... | collective-permute-start | bytes 1244168 | tf_op jit(solution)/shard_map/ppermute | solution.py:212
  58.8 32.7 %copy-start.4 = (bf16[288,1152]{1,0:T(8,128)(2,1)S(1)}, bf16[288,1152]{1,0:T(8,128)(2,1)}, u32[]{:S(2)}) copy-start(bf16[288,1152]{1,0:T(8,128)(2,1)} %refs_4_.1) | copy-start | bytes 1990660
  63.8 10.3 %collective-permute-start.10 = (bf16[288,720]{1,0:T(8,128)(2,1)S(1)}, bf16[288,720]{1,0:T(8,128)(2,1)S(1)}, u32[]{:S(2)}, u32[]{:S(2)}) collective-permute-start(bf16[288,720]{1,0:T(8,128)(2,1)S(1)} %collective-permute-done.9.refs_12_.refs_18_), channel_id=1, source_target_pairs={{0,2},{1,3},{2,0},{3,1},{4,6},{5,7},{6,4},{7,5},{8,10},{9,11},{10,... | collective-permute-start | bytes 1244168 | tf_op jit(solution)/shard_map/ppermute | solution.py:212
  65.4 9.8 %collective-permute-start.14 = (bf16[288,720]{1,0:T(8,128)(2,1)S(1)}, bf16[288,720]{1,0:T(8,128)(2,1)S(1)}, u32[]{:S(2)}, u32[]{:S(2)}) collective-permute-start(bf16[288,720]{1,0:T(8,128)(2,1)S(1)} %collective-permute-done.2.refs_4_.refs_10_), channel_id=1, source_target_pairs={{0,1},{1,0},{2,3},{3,2},{4,5},{5,4},{6,7},{7,6},{8,9},{9,8},{10,11... | collective-permute-start | bytes 1244168 | tf_op jit(solution)/shard_map/ppermute | solution.py:212
  65.4 9.8 %collective-permute-start.13 = (bf16[128,1152]{1,0:T(8,128)(2,1)S(1)}, bf16[128,1152]{1,0:T(8,128)(2,1)S(1)}, u32[]{:S(2)}, u32[]{:S(2)}) collective-permute-start(bf16[128,1152]{1,0:T(8,128)(2,1)S(1)} %copy-done.2), channel_id=1, source_target_pairs={{0,4},{4,0},{1,5},{5,1},{2,6},{6,2},{3,7},{7,3},{8,12},{12,8},{9,1... | collective-permute-start | bytes 884744 | tf_op jit(solution)/shard_map/ppermute | solution.py:212
  67.5 8.2 %collective-permute-start.15 = (bf16[288,720]{1,0:T(8,128)(2,1)S(1)}, bf16[288,720]{1,0:T(8,128)(2,1)S(1)}, u32[]{:S(2)}, u32[]{:S(2)}) collective-permute-start(bf16[288,720]{1,0:T(8,128)(2,1)S(1)} %collective-permute-done.7.refs_6_.refs_12_), channel_id=1, source_target_pairs={{0,1},{1,0},{2,3},{3,2},{4,5},{5,4},{6,7},{7,6},{8,9},{9,8},{10,11... | collective-permute-start | bytes 1244168 | tf_op jit(solution)/shard_map/ppermute | solution.py:212
  67.7 9.8 %collective-permute-start.16 = (bf16[288,720]{1,0:T(8,128)(2,1)S(1)}, bf16[288,720]{1,0:T(8,128)(2,1)S(1)}, u32[]{:S(2)}, u32[]{:S(2)}) collective-permute-start(bf16[288,720]{1,0:T(8,128)(2,1)S(1)} %collective-permute-done.1.refs_8_.refs_14_), channel_id=1, source_target_pairs={{0,1},{1,0},{2,3},{3,2},{4,5},{5,4},{6,7},{7,6},{8,9},{9,8},{10,11... | collective-permute-start | bytes 1244168 | tf_op jit(solution)/shard_map/ppermute | solution.py:212
  74.1 3.6 %collective-permute-start.18 = (bf16[288,720]{1,0:T(8,128)(2,1)S(1)}, bf16[288,720]{1,0:T(8,128)(2,1)S(1)}, u32[]{:S(2)}, u32[]{:S(2)}) collective-permute-start(bf16[288,720]{1,0:T(8,128)(2,1)S(1)} %collective-permute-done.9.refs_12_.refs_18_), channel_id=1, source_target_pairs={{0,1},{1,0},{2,3},{3,2},{4,5},{5,4},{6,7},{7,6},{8,9},{9,8},{10,11... | collective-permute-start | bytes 1244168 | tf_op jit(solution)/shard_map/ppermute | solution.py:212
  75.1 2.6 %collective-permute-start.17 = (bf16[288,720]{1,0:T(8,128)(2,1)S(1)}, bf16[288,720]{1,0:T(8,128)(2,1)S(1)}, u32[]{:S(2)}, u32[]{:S(2)}) collective-permute-start(bf16[288,720]{1,0:T(8,128)(2,1)S(1)} %collective-permute-done.8.refs_10_.refs_16_), channel_id=1, source_target_pairs={{0,1},{1,0},{2,3},{3,2},{4,5},{5,4},{6,7},{7,6},{8,9},{9,8},{10,11... | collective-permute-start | bytes 1244168 | tf_op jit(solution)/shard_map/ppermute | solution.py:212
  75.2 2.6 %collective-permute-start.19 = (bf16[288,720]{1,0:T(8,128)(2,1)S(1)}, bf16[288,720]{1,0:T(8,128)(2,1)S(1)}, u32[]{:S(2)}, u32[]{:S(2)}) collective-permute-start(bf16[288,720]{1,0:T(8,128)(2,1)S(1)} %collective-permute-done.10.refs_14_.refs_20_), channel_id=1, source_target_pairs={{0,1},{1,0},{2,3},{3,2},{4,5},{5,4},{6,7},{7,6},{8,9},{9,8},{10,11... | collective-permute-start | bytes 1244168 | tf_op jit(solution)/shard_map/ppermute | solution.py:212
  75.7 9.9 %collective-permute-start.11 = (bf16[64,2304]{1,0:T(8,128)(2,1)S(1)}, bf16[64,2304]{1,0:T(8,128)(2,1)S(1)}, u32[]{:S(2)}, u32[]{:S(2)}) collective-permute-start(bf16[64,2304]{1,0:T(8,128)(2,1)S(1)} %shard_map.149.refs_0_), channel_id=1, source_target_pairs={{0,4},{4,0},{1,5},{5,1},{2,6},{6,2},{3,7},{7,3},{8,12},{12,8},{9,1... | collective-permute-start | bytes 884744 | tf_op jit(solution)/shard_map/ppermute | solution.py:212
  77.5 13.9 %collective-permute-start.12 = (bf16[64,2304]{1,0:T(8,128)(2,1)S(1)}, bf16[64,2304]{1,0:T(8,128)(2,1)S(1)}, u32[]{:S(2)}, u32[]{:S(2)}) collective-permute-start(bf16[64,2304]{1,0:T(8,128)(2,1)S(1)} %shard_map.150.refs_1_), channel_id=1, source_target_pairs={{0,4},{4,0},{1,5},{5,1},{2,6},{6,2},{3,7},{7,3},{8,12},{12,8},{9,1... | collective-permute-start | bytes 884744 | tf_op jit(solution)/shard_map/ppermute | solution.py:212
  99.4 8.7 %collective-permute-start.20 = (bf16[4,32,1152]{2,1,0:T(8,128)(2,1)S(1)}, bf16[4,32,1152]{2,1,0:T(8,128)(2,1)S(1)}, u32[]{:S(2)}, u32[]{:S(2)}) collective-permute-start(bf16[4,32,1152]{2,1,0:T(8,128)(2,1)S(1)} %get-tuple-element.49), channel_id=1, source_target_pairs={{0,4},{4,0},{1,5},{5,1},{2,6},{6,2},{3,7},{7,3},{8,12},{12,8},{9,1... | collective-permute-start | bytes 884744 | tf_op jit(solution)/shard_map/ppermute | solution.py:212

commit v2 on v1

--- a/solution.py
+++ b/solution.py
@@ -518,7 +518,7 @@
 
 
 def attention_back(
-    image_rows, own, other, gain, mine, theirs, proj_weight, projected, weights, head_dim
+    image_rows, own, other, gain, mine, theirs, proj_weight, proj_apart, projected, weights, head_dim
 ):
     patches, width = own.shape
     length = 2 * patches
@@ -531,6 +531,7 @@
     part_heads = part_rows // head_dim
     shard_sections = copies * group_heads // part_heads
     flat = [w for parts in weights for w in parts]
+    apart = list(proj_apart)
     chunks = len(mine)
     per_chunk = 4 // chunks
     score_scale = head_dim ** (-0.5)
@@ -541,6 +542,7 @@
         theirs_refs, refs = refs[:chunks], refs[chunks:]
         proj_ref, projected_ref, refs = refs[0], refs[1], refs[2:]
         w_refs, refs = refs[: len(flat)], refs[len(flat) :]
+        apart_refs, refs = dict(zip(apart, refs)), refs[len(apart) :]
         own_out, other_out, grad_out, x, og, og_parts, heads, acc = refs
         section, shard, copy = (lax.axis_index(name) for name in ("section", "vit", "dp"))
         ends = image_ends(image_ref, images)
@@ -574,7 +576,9 @@
                         put_heads(i, dot(proj_ref[...], og[...], 1, 1))
                     else:
                         fetched = [
-                            w_refs[k * copies + p][:, group_cols : group_cols + part_rows]
+                            apart_refs[k, p][...]
+                            if (k, p) in apart_refs
+                            else w_refs[k * copies + p][:, group_cols : group_cols + part_rows]
                             for p in range(copies)
                         ]
                         put_heads(
@@ -619,7 +623,7 @@
             other_out[j] = result[j * slots + half : (j + 1) * slots].astype(bf16)
 
     shape = (4, half, width)
-    operands = (own, other, gain, *mine, *theirs, proj_weight, projected, *flat)
+    operands = (own, other, gain, *mine, *theirs, proj_weight, projected, *flat, *proj_apart.values())
     return run_kernel(
         body,
         (1,),
@@ -721,20 +725,24 @@
     far_core = swap(far, "dp", 1)
     first = merge_part(pre_grad, fc1_weight, 0, 2)
     first_theirs = swap(first, "vit", 1)
-    far_chip, pre_grad, first, cross = lax.optimization_barrier((far_chip, pre_grad, first, cross))
-    cross_chip = swap(cross, "dp", 2)
+    second = merge_part(pre_grad, fc1_weight, 1, 2)
+    second, cross, far_chip = lax.optimization_barrier((second, cross, far_chip))
+    columns = own_parts[1].shape[1]
+    cross_chip = swap(cross[:, :columns], "dp", 2)
+    late_proj = swap(far_chip[:, columns:], "section", 1)
+    second_theirs = swap(second, "vit", 1)
+    cross_core = swap(cross, "dp", 1)
     far_diagonal = swap(far_chip, "dp", 1)
-    cross_core = swap(cross, "dp", 1)
-    second = merge_part(pre_grad, fc1_weight, 1, 2)
-    second_theirs = swap(second, "vit", 1)
-    second, cross_chip = lax.optimization_barrier((second, cross_chip))
+    cross_chip, late_proj = lax.optimization_barrier((cross_chip, late_proj))
     cross_diagonal = swap(cross_chip, "dp", 1)
+    late_proj_core = swap(late_proj, "dp", 1)
     weights = [
         own_parts,
         [near, near_core, near_chip, near_diagonal],
         [far, far_core, far_chip, far_diagonal],
         [cross, cross_core, cross_chip, cross_diagonal],
     ]
+    proj_apart = {(3, 2): late_proj, (3, 3): late_proj_core}
 
     projected = project(vit_in, vit_in_other, ln_gain, ln_bias, weights, head_dim)
     normed_mine, normed_sent, out_grad = attention_back(
@@ -745,6 +753,7 @@
         [first, second],
         [first_theirs, second_theirs],
         proj_weight,
+        proj_apart,
         projected,
         weights,
         head_dim,

time: 109 us -> 109 us (level)
    ppermute x21 -> x23, waiting for transfers between devices: 45.8 us -> 45.1 us  [swap(): return lax.ppermute(values, axis, [(i, i ^ bit) for i in range(count)])]
    ppermute x21 -> x23, starting transfers between devices: 21.3 us -> 21.3 us  [swap(): return lax.ppermute(values, axis, [(i, i ^ bit) for i in range(count)])]
  transfers between devices with their start and end apart: 21 -> 23, of which waited for: 10 -> 10; matrix products, arithmetic and copies ran while one was open for 1% -> 1% of each run, Pallas kernels for 26% -> 26%
where the time goes in v2:
time: 109 us
  waiting for transfers between devices  45.1 us (41%)
  Pallas kernels  37.5 us (34%)
  starting transfers between devices  21.3 us (20%)
  local copies, waits for them, and re-layouts  4.68 us (4%)
    ppermute x23, waiting for transfers between devices, swap(): return lax.ppermute(values, axis, [(i, i ^ bit) for i in range(count)])  45.1 us
    ppermute x23, starting transfers between devices, swap(): return lax.ppermute(values, axis, [(i, i ^ bit) for i in range(count)])  21.3 us
    pallas_call x1, Pallas kernels, pre_grad_of(): run_kernel(body, (1,), [whole(x) for x in (vis_slot, own, other, slope)]...  9.41 us
    pallas_call x2, Pallas kernels, merge_part(): run_kernel(body, (1,), [whole(pre_grad), RESIDENT], pl.BlockSpec((slots,...  9.06 us
    pallas_call x1, Pallas kernels, attention_back(): run_kernel(body, (1,), [whole(x) for x in operands], [pl.BlockSpec(shape,...  7.92 us
    pallas_call x1, Pallas kernels, slope_of(): run_kernel(body, (1,), [whole(x) for x in (own, other, gain, bias, fc1_bi...  5.47 us
    unnamed x30, local copies, waits for them, and re-layouts  3.22 us
    pallas_call x1, Pallas kernels, project(): run_kernel(body, (1,), [whole(x) for x in (own, other, gain, bias, *flat)...  3.03 us
  transfers between devices with their start and end apart: 23, of which 10 were waited for; matrix products, arithmetic and copies ran while one was open for 1% of the time, Pallas kernels for 26%

profile of v2, /device:TPU:0, one launch (start us, length us, event | category | flops | bytes accessed | tf_op | source)
XLA Modules:
  0.0 108.9 jit_solution(15322008639652631406)
XLA Ops:
  0.0 3.0 %collective-permute-start = (bf16[128,1152]{1,0:T(8,128)(2,1)}, bf16[128,1152]{1,0:T(8,128)(2,1)S(1)}, u32[]{:S(2)}, u32[]{:S(2)}) collective-permute-start(bf16[128,1152]{1,0:T(8,128)(2,1)} %own_ref.6), channel_id=1, source_target_pairs={{0,4},{4,0},{1,5},{5,1},{2,6},{6,2},{3,7},{7,3},{8,12},{12,8},{9,1... | collective-permute-start | bytes 884744 | tf_op jit(solution)/shard_map/ppermute | solution.py:212
  3.0 1.3 %dynamic-slice_bitcast_fusion = (bf16[32,4096]{1,0:T(8,128)(2,1)S(1)}, bf16[32,4096]{1,0:T(8,128)(2,1)S(1)}, bf16[32,4096]{1,0:T(8,128)(2,1)S(1)}) fusion(bf16[4,32,4096]{2,1,0:T(8,128)(2,1)} %bitcast.8, s32[]{:T(128)S(6)} %select_n.12, s32[]{:T(128)S(6)} %select_n.11, s32[]{:T(128)S(6)} %select_n.10), kind=kLoop, calls=%fused_computation | loop fusion | bytes 1572876 | tf_op jit(solution)/shard_map/jit(dynamic_index_in_dim)/squeeze | solution.py:702
  4.4 3.7 %collective-permute-start.5 = (bf16[32,4096]{1,0:T(8,128)(2,1)S(1)}, bf16[32,4096]{1,0:T(8,128)(2,1)S(1)}, u32[]{:S(2)}, u32[]{:S(2)}) collective-permute-start(bf16[32,4096]{1,0:T(8,128)(2,1)S(1)} %get-tuple-element.49), channel_id=1, source_target_pairs={{0,24},{8,16},{16,8},{24,0},{1,25},{9,17},{17,9},{25,1},{2,26},{10... | collective-permute-start | bytes 786440 | tf_op jit(solution)/shard_map/ppermute | solution.py:212
  8.0 0.8 collective-permute-start.3
  8.8 1.6 %copy-done.3 = bf16[288,1152]{1,0:T(8,128)(2,1)S(1)} copy-done((bf16[288,1152]{1,0:T(8,128)(2,1)S(1)}, bf16[288,1152]{1,0:T(8,128)(2,1)}, u32[]{:S(2)}) %copy-start.3) | copy-done | bytes 663576
  10.4 1.6 %copy-done.12 = bf16[288,3456]{1,0:T(8,128)(2,1)S(1)} copy-done((bf16[288,3456]{1,0:T(8,128)(2,1)S(1)}, bf16[288,3456]{1,0:T(8,128)(2,1)}, u32[]{:S(2)}) %copy-start.12) | copy-done | bytes 1990680
  12.0 0.5 shard_map.145
  12.5 0.0 copy-start.1
  12.5 0.0 copy-start.11
  12.5 0.0 copy-start.9
  12.5 0.0 copy-start.10
  12.5 0.0 copy-start.2
  12.5 1.6 %collective-permute-start.2 = (bf16[288,720]{1,0:T(8,128)(2,1)S(1)}, bf16[288,720]{1,0:T(8,128)(2,1)S(1)}, u32[]{:S(2)}, u32[]{:S(2)}) collective-permute-start(bf16[288,720]{1,0:T(8,128)(2,1)S(1)} %get-tuple-element.27), channel_id=1, source_target_pairs={{0,8},{8,0},{16,24},{24,16},{1,9},{9,1},{17,25},{25,17},{2,10},{10... | collective-permute-start | bytes 1244168 | tf_op jit(solution)/shard_map/ppermute | solution.py:212
  14.1 5.5 %shard_map.146.slope_ref = f32[64,2304]{1,0:T(8,128)S(1)} custom-call(bf16[128,1152]{1,0:T(8,128)(2,1)S(1)} %copy-done.5, bf16[128,1152]{1,0:T(8,128)(2,1)S(1)} %collective-permute-done.other_ref, f32[1152]{0:T(1024)S(1)} %copy-done.7, f32[1152]{0:T(1024)S(1)} %copy-done.14, f32[2304]{0:T(1024)S(1)} %copy-done.13, bf16[4608,2304]{1,0:T(8,128)(2,1)S(1)} %copy-done), custom_call_target="tpu_custom_call" | custom-call | flops 8000000000 | tf_op jit(solution)/shard_map/pallas_call | solution.py:369
  19.6 10.5 %collective-permute-done.4.refs_1_ = bf16[32,4096]{1,0:T(8,128)(2,1)S(1)} collective-permute-done((bf16[32,4096]{1,0:T(8,128)(2,1)S(1)}, bf16[32,4096]{1,0:T(8,128)(2,1)S(1)}, u32[]{:S(2)}, u32[]{:S(2)}) %collective-permute-start.4) | collective-permute-done | bytes 262176 | tf_op jit(solution)/shard_map/ppermute | solution.py:212
  30.2 0.9 shard_map.147.own_ref
  31.0 0.6 collective-permute-start.6
  31.6 4.1 %collective-permute-done.2.refs_4_.refs_10_ = bf16[288,720]{1,0:T(8,128)(2,1)S(1)} collective-permute-done((bf16[288,720]{1,0:T(8,128)(2,1)S(1)}, bf16[288,720]{1,0:T(8,128)(2,1)S(1)}, u32[]{:S(2)}, u32[]{:S(2)}) %collective-permute-start.2) | collective-permute-done | bytes 414752 | tf_op jit(solution)/shard_map/ppermute | solution.py:212
  35.8 2.7 %collective-permute-done.6.other_ref = bf16[32,4096]{1,0:T(8,128)(2,1)S(1)} collective-permute-done((bf16[32,4096]{1,0:T(8,128)(2,1)S(1)}, bf16[32,4096]{1,0:T(8,128)(2,1)S(1)}, u32[]{:S(2)}, u32[]{:S(2)}) %collective-permute-start.6) | collective-permute-done | bytes 262176 | tf_op jit(solution)/shard_map/ppermute | solution.py:212
  38.4 1.5 %collective-permute-start.7 = (bf16[288,720]{1,0:T(8,128)(2,1)S(1)}, bf16[288,720]{1,0:T(8,128)(2,1)S(1)}, u32[]{:S(2)}, u32[]{:S(2)}) collective-permute-start(bf16[288,720]{1,0:T(8,128)(2,1)S(1)} %collective-permute-done.2.refs_4_.refs_10_), channel_id=1, source_target_pairs={{0,2},{1,3},{2,0},{3,1},{4,6},{5,7},{6,4},{7,5},{8,10},{9,11},{10,... | collective-permute-start | bytes 1244168 | tf_op jit(solution)/shard_map/ppermute | solution.py:212
  40.0 9.4 %shard_map.148.pre_ref = bf16[64,2304]{1,0:T(8,128)(2,1)S(1)} custom-call(s32[2,4]{1,0:T(2,128)S(1)} %bitcast.9, s32[2,128]{1,0:T(2,128)S(1)} %copy-done.10, bf16[32,4096]{1,0:T(8,128)(2,1)S(1)} %shard_map.147.own_ref, bf16[32,4096]{1,0:T(8,128)(2,1)S(1)} %collective-permute-done.6.other_ref, f32[64,2304]{1,0:T(8,128)S(1)} %shard_map.146.slope_ref, ...), custom_call_target="tpu_custom_call" | custom-call | tf_op jit(solution)/shard_map/pallas_call | solution.py:429
  49.4 0.0 copy-start.6
  49.4 0.0 copy-start.8
  49.4 3.3 %collective-permute-done.1.refs_8_.refs_14_ = bf16[288,720]{1,0:T(8,128)(2,1)S(1)} collective-permute-done((bf16[288,720]{1,0:T(8,128)(2,1)S(1)}, bf16[288,720]{1,0:T(8,128)(2,1)S(1)}, u32[]{:S(2)}, u32[]{:S(2)}) %collective-permute-start.1) | collective-permute-done | bytes 414752 | tf_op jit(solution)/shard_map/ppermute | solution.py:212
  52.7 1.5 %collective-permute-start.9 = (bf16[288,720]{1,0:T(8,128)(2,1)S(1)}, bf16[288,720]{1,0:T(8,128)(2,1)S(1)}, u32[]{:S(2)}, u32[]{:S(2)}) collective-permute-start(bf16[288,720]{1,0:T(8,128)(2,1)S(1)} %collective-permute-done.1.refs_8_.refs_14_), channel_id=1, source_target_pairs={{0,2},{1,3},{2,0},{3,1},{4,6},{5,7},{6,4},{7,5},{8,10},{9,11},{10,... | collective-permute-start | bytes 1244168 | tf_op jit(solution)/shard_map/ppermute | solution.py:212
  54.2 1.4 %collective-permute-start.12 = (bf16[128,1152]{1,0:T(8,128)(2,1)S(1)}, bf16[128,1152]{1,0:T(8,128)(2,1)S(1)}, u32[]{:S(2)}, u32[]{:S(2)}) collective-permute-start(bf16[128,1152]{1,0:T(8,128)(2,1)S(1)} %copy-done.2), channel_id=1, source_target_pairs={{0,4},{4,0},{1,5},{5,1},{2,6},{6,2},{3,7},{7,3},{8,12},{12,8},{9,1... | collective-permute-start | bytes 884744 | tf_op jit(solution)/shard_map/ppermute | solution.py:212
  55.7 0.2 collective-permute-start.14
  55.9 8.0 %collective-permute-done.9.refs_10_.refs_16_ = bf16[288,720]{1,0:T(8,128)(2,1)S(1)} collective-permute-done((bf16[288,720]{1,0:T(8,128)(2,1)S(1)}, bf16[288,720]{1,0:T(8,128)(2,1)S(1)}, u32[]{:S(2)}, u32[]{:S(2)}) %collective-permute-start.9) | collective-permute-done | bytes 414752 | tf_op jit(solution)/shard_map/ppermute | solution.py:212
  63.8 4.5 %shard_map.150.refs_1_ = bf16[64,2304]{1,0:T(8,128)(2,1)S(1)} custom-call(bf16[64,2304]{1,0:T(8,128)(2,1)S(1)} %shard_map.148.pre_ref, bf16[4608,2304]{1,0:T(8,128)(2,1)S(1)} %copy-done), custom_call_target="tpu_custom_call" | custom-call | tf_op jit(solution)/shard_map/pallas_call | solution.py:467
  68.4 0.0 copy-start.4
  68.4 0.6 collective-permute-start.16
  69.0 1.6 %collective-permute-start.18 = (bf16[288,432]{1,0:T(8,128)(2,1)S(1)}, bf16[288,432]{1,0:T(8,128)(2,1)S(1)}, u32[]{:S(2)}, u32[]{:S(2)}) collective-permute-start(bf16[288,432]{1,0:T(8,128)(2,1)S(1)} %slice.6), channel_id=1, source_target_pairs={{0,2},{1,3},{2,0},{3,1},{4,6},{5,7},{6,4},{7,5},{8,10},{9,11},{10,... | collective-permute-start | bytes 746504 | tf_op jit(solution)/shard_map/ppermute | solution.py:212
  70.6 0.1 slice.7
  70.7 0.1 collective-permute-start.19
  70.8 0.1 collective-permute-start.17
  70.9 4.5 %shard_map.149.refs_0_ = bf16[64,2304]{1,0:T(8,128)(2,1)S(1)} custom-call(bf16[64,2304]{1,0:T(8,128)(2,1)S(1)} %shard_map.148.pre_ref, bf16[4608,2304]{1,0:T(8,128)(2,1)S(1)} %copy-done), custom_call_target="tpu_custom_call" | custom-call | tf_op jit(solution)/shard_map/pallas_call | solution.py:467
  75.5 2.4 %collective-permute-done.19.refs_22_ = bf16[288,288]{1,0:T(8,128)(2,1)S(1)} collective-permute-done((bf16[288,288]{1,0:T(8,128)(2,1)S(1)}, bf16[288,288]{1,0:T(8,128)(2,1)S(1)}, u32[]{:S(2)}, u32[]{:S(2)}) %collective-permute-start.19) | collective-permute-done | bytes 165920 | tf_op jit(solution)/shard_map/ppermute | solution.py:212
  77.9 2.1 %collective-permute-start.10 = (bf16[64,2304]{1,0:T(8,128)(2,1)S(1)}, bf16[64,2304]{1,0:T(8,128)(2,1)S(1)}, u32[]{:S(2)}, u32[]{:S(2)}) collective-permute-start(bf16[64,2304]{1,0:T(8,128)(2,1)S(1)} %shard_map.149.refs_0_), channel_id=1, source_target_pairs={{0,4},{4,0},{1,5},{5,1},{2,6},{6,2},{3,7},{7,3},{8,12},{12,8},{9,1... | collective-permute-start | bytes 884744 | tf_op jit(solution)/shard_map/ppermute | solution.py:212
  80.0 0.1 collective-permute-start.11
  80.1 0.5 collective-permute-start.21
  80.6 1.1 collective-permute-done.20.refs_15_.refs_21_
  81.7 3.0 %shard_map.151.refs_5_ = bf16[4,6,72,256]{3,2,1,0:T(8,128)(2,1)S(1)} custom-call(bf16[128,1152]{1,0:T(8,128)(2,1)S(1)} %copy-done.2, bf16[128,1152]{1,0:T(8,128)(2,1)S(1)} %collective-permute-done.12.other_ref, f32[1152]{0:T(1024)S(1)} %copy-done.6, f32[1152]{0:T(1024)S(1)} %copy-done.8, bf16[288,432]{1,0:T(8,128)(2,1)S(1)} %get-tuple-element.37.refs_0_.refs_6_, ...), custom_call_target="tpu_custom_call" | custom-call | tf_op jit(solution)/shard_map/pallas_call | solution.py:506
  84.7 3.1 %collective-permute-done.10.refs_2_ = bf16[64,2304]{1,0:T(8,128)(2,1)S(1)} collective-permute-done((bf16[64,2304]{1,0:T(8,128)(2,1)S(1)}, bf16[64,2304]{1,0:T(8,128)(2,1)S(1)}, u32[]{:S(2)}, u32[]{:S(2)}) %collective-permute-start.10) | collective-permute-done | bytes 294944 | tf_op jit(solution)/shard_map/ppermute | solution.py:212
  87.8 4.5 %collective-permute-done.11.refs_3_ = bf16[64,2304]{1,0:T(8,128)(2,1)S(1)} collective-permute-done((bf16[64,2304]{1,0:T(8,128)(2,1)S(1)}, bf16[64,2304]{1,0:T(8,128)(2,1)S(1)}, u32[]{:S(2)}, u32[]{:S(2)}) %collective-permute-start.11) | collective-permute-done | bytes 294944 | tf_op jit(solution)/shard_map/ppermute | solution.py:212
  92.4 7.9 %shard_map.152 = (f32[4,32,1152]{2,1,0:T(8,128)S(1)}, bf16[4,32,1152]{2,1,0:T(8,128)(2,1)S(1)}, bf16[4,32,1152]{2,1,0:T(8,128)(2,1)S(1)}) custom-call(s32[2,4]{1,0:T(2,128)S(1)} %bitcast.10, bf16[128,1152]{1,0:T(8,128)(2,1)S(1)} %copy-done.5, bf16[128,1152]{1,0:T(8,128)(2,1)S(1)} %collective-permute-done.other_ref, f32[1152]{0:T(1024)S(1)} %copy-done.7, ...), custom_call_target="tpu_custom_call" | custom-call | tf_op jit(solution)/shard_map/pallas_call | solution.py:627
  100.3 1.9 %collective-permute-start.22 = (bf16[4,32,1152]{2,1,0:T(8,128)(2,1)S(1)}, bf16[4,32,1152]{2,1,0:T(8,128)(2,1)S(1)}, u32[]{:S(2)}, u32[]{:S(2)}) collective-permute-start(bf16[4,32,1152]{2,1,0:T(8,128)(2,1)S(1)} %get-tuple-element.47), channel_id=1, source_target_pairs={{0,4},{4,0},{1,5},{5,1},{2,6},{6,2},{3,7},{7,3},{8,12},{12,8},{9,1... | collective-permute-start | bytes 884744 | tf_op jit(solution)/shard_map/ppermute | solution.py:212
  102.2 5.3 %collective-permute-done.22.theirs_ref = bf16[4,32,1152]{2,1,0:T(8,128)(2,1)S(1)} collective-permute-done((bf16[4,32,1152]{2,1,0:T(8,128)(2,1)S(1)}, bf16[4,32,1152]{2,1,0:T(8,128)(2,1)S(1)}, u32[]{:S(2)}, u32[]{:S(2)}) %collective-permute-start.22) | collective-permute-done | bytes 294944 | tf_op jit(solution)/shard_map/ppermute | solution.py:212
  107.6 1.3 %shard_map.153 = bf16[128,1152]{1,0:T(8,128)(2,1)} custom-call(bf16[128,1152]{1,0:T(8,128)(2,1)S(1)} %copy-done.2, f32[1152]{0:T(1024)S(1)} %copy-done.6, f32[4,32,1152]{2,1,0:T(8,128)S(1)} %get-tuple-element.46.mine_ref, bf16[4,32,1152]{2,1,0:T(8,128)(2,1)S(1)} %collective-permute-done.22.theirs_ref, bf16[4,32,1152]{2,1,0:T(8,128)(2,1)S(1)} %get-tuple-element.48.grad_ref), custom_call_target="tpu_custom_call" | custom-call | tf_op jit(solution)/shard_map/pallas_call | solution.py:662
  (40 shorter events, 0.1 us)
Async XLA Ops:
  0.0 14.1 %copy-start.7 = (f32[1152]{0:T(1024)S(1)}, f32[1152]{0:T(1024)}, u32[]{:S(2)}) copy-start(f32[1152]{0:T(1024)} %gain_ref.6) | copy-start | bytes 13828
  0.0 14.1 %copy-start.13 = (f32[2304]{0:T(1024)S(1)}, f32[2304]{0:T(1024)}, u32[]{:S(2)}) copy-start(f32[2304]{0:T(1024)} %fc1b_ref.1) | copy-start | bytes 27652
  0.0 14.1 %copy-start.14 = (f32[1152]{0:T(1024)S(1)}, f32[1152]{0:T(1024)}, u32[]{:S(2)}) copy-start(f32[1152]{0:T(1024)} %bias_ref.2) | copy-start | bytes 13828
  0.0 14.1 %collective-permute-start = (bf16[128,1152]{1,0:T(8,128)(2,1)}, bf16[128,1152]{1,0:T(8,128)(2,1)S(1)}, u32[]{:S(2)}, u32[]{:S(2)}) collective-permute-start(bf16[128,1152]{1,0:T(8,128)(2,1)} %own_ref.6), channel_id=1, source_target_pairs={{0,4},{4,0},{1,5},{5,1},{2,6},{6,2},{3,7},{7,3},{8,12},{12,8},{9,1... | collective-permute-start | bytes 884744 | tf_op jit(solution)/shard_map/ppermute | solution.py:212
  3.0 11.1 %copy-start = (bf16[4608,2304]{1,0:T(8,128)(2,1)S(1)}, bf16[4608,2304]{1,0:T(8,128)(2,1)}, u32[]{:S(2)}) copy-start(bf16[4608,2304]{1,0:T(8,128)(2,1)} %fc1_ref.5) | copy-start | bytes 63700996
  4.4 15.3 %collective-permute-start.5 = (bf16[32,4096]{1,0:T(8,128)(2,1)S(1)}, bf16[32,4096]{1,0:T(8,128)(2,1)S(1)}, u32[]{:S(2)}, u32[]{:S(2)}) collective-permute-start(bf16[32,4096]{1,0:T(8,128)(2,1)S(1)} %get-tuple-element.49), channel_id=1, source_target_pairs={{0,24},{8,16},{16,8},{24,0},{1,25},{9,17},{17,9},{25,1},{2,26},{10... | collective-permute-start | bytes 786440 | tf_op jit(solution)/shard_map/ppermute | solution.py:212
  8.0 22.1 %collective-permute-start.4 = (bf16[32,4096]{1,0:T(8,128)(2,1)S(1)}, bf16[32,4096]{1,0:T(8,128)(2,1)S(1)}, u32[]{:S(2)}, u32[]{:S(2)}) collective-permute-start(bf16[32,4096]{1,0:T(8,128)(2,1)S(1)} %get-tuple-element.50), channel_id=1, source_target_pairs={{0,16},{8,24},{16,0},{24,8},{1,17},{9,25},{17,1},{25,9},{2,18},{10... | collective-permute-start | bytes 786440 | tf_op jit(solution)/shard_map/ppermute | solution.py:212
  8.0 22.1 %collective-permute-start.3 = (bf16[32,4096]{1,0:T(8,128)(2,1)S(1)}, bf16[32,4096]{1,0:T(8,128)(2,1)S(1)}, u32[]{:S(2)}, u32[]{:S(2)}) collective-permute-start(bf16[32,4096]{1,0:T(8,128)(2,1)S(1)} %get-tuple-element.51), channel_id=1, source_target_pairs={{0,8},{8,0},{16,24},{24,16},{1,9},{9,1},{17,25},{25,17},{2,10},{10... | collective-permute-start | bytes 786440 | tf_op jit(solution)/shard_map/ppermute | solution.py:212
  8.8 1.6 %copy-start.3 = (bf16[288,1152]{1,0:T(8,128)(2,1)S(1)}, bf16[288,1152]{1,0:T(8,128)(2,1)}, u32[]{:S(2)}) copy-start(bf16[288,1152]{1,0:T(8,128)(2,1)} %refs_4_.1) | copy-start | bytes 1990660
  10.4 1.6 %copy-start.12 = (bf16[288,3456]{1,0:T(8,128)(2,1)S(1)}, bf16[288,3456]{1,0:T(8,128)(2,1)}, u32[]{:S(2)}) copy-start(bf16[288,3456]{1,0:T(8,128)(2,1)} %qkv_ref.1) | copy-start | bytes 5971972
  12.0 2.2 %copy-start.5 = (bf16[128,1152]{1,0:T(8,128)(2,1)S(1)}, bf16[128,1152]{1,0:T(8,128)(2,1)}, u32[]{:S(2)}) copy-start(bf16[128,1152]{1,0:T(8,128)(2,1)} %own_ref.6) | copy-start | bytes 884740
  12.5 17.7 %copy-start.1 = (bf16[1,128,4096]{2,1,0:T(8,128)(2,1)S(1)}, bf16[1,128,4096]{2,1,0:T(8,128)(2,1)}, u32[]{:S(2)}) copy-start(bf16[1,128,4096]{2,1,0:T(8,128)(2,1)} %grad_ref.1) | copy-start | bytes 3145732
  12.5 17.7 %copy-start.11 = (s32[4]{0:T(128)S(1)}, s32[4]{0:T(128)}, u32[]{:S(2)}) copy-start(s32[4]{0:T(128)} %layer_ref.1) | copy-start | bytes 52
  12.5 27.5 %copy-start.9 = (s32[4,2]{0,1:T(2,128)S(1)}, s32[4,2]{0,1:T(2,128)}, u32[]{:S(2)}) copy-start(s32[4,2]{0,1:T(2,128)} %param.17) | copy-start | bytes 100
  12.5 27.4 %copy-start.10 = (s32[2,128]{1,0:T(2,128)S(1)}, s32[2,128]{1,0:T(2,128)}, u32[]{:S(2)}) copy-start(s32[2,128]{1,0:T(2,128)} %slot_ref.1) | copy-start | bytes 3076
  12.5 41.7 %copy-start.2 = (bf16[128,1152]{1,0:T(8,128)(2,1)S(1)}, bf16[128,1152]{1,0:T(8,128)(2,1)}, u32[]{:S(2)}) copy-start(bf16[128,1152]{1,0:T(8,128)(2,1)} %own_ref.7) | copy-start | bytes 884740
  12.5 23.2 %collective-permute-start.2 = (bf16[288,720]{1,0:T(8,128)(2,1)S(1)}, bf16[288,720]{1,0:T(8,128)(2,1)S(1)}, u32[]{:S(2)}, u32[]{:S(2)}) collective-permute-start(bf16[288,720]{1,0:T(8,128)(2,1)S(1)} %get-tuple-element.27), channel_id=1, source_target_pairs={{0,8},{8,0},{16,24},{24,16},{1,9},{9,1},{17,25},{25,17},{2,10},{10... | collective-permute-start | bytes 1244168 | tf_op jit(solution)/shard_map/ppermute | solution.py:212
  31.0 7.4 %collective-permute-start.6 = (bf16[32,4096]{1,0:T(8,128)(2,1)S(1)}, bf16[32,4096]{1,0:T(8,128)(2,1)S(1)}, u32[]{:S(2)}, u32[]{:S(2)}) collective-permute-start(bf16[32,4096]{1,0:T(8,128)(2,1)S(1)} %shard_map.147.own_ref), channel_id=1, source_target_pairs={{0,4},{4,0},{1,5},{5,1},{2,6},{6,2},{3,7},{7,3},{8,12},{12,8},{9,1... | collective-permute-start | bytes 786440 | tf_op jit(solution)/shard_map/ppermute | solution.py:212
  31.6 21.1 %collective-permute-start.1 = (bf16[288,720]{1,0:T(8,128)(2,1)S(1)}, bf16[288,720]{1,0:T(8,128)(2,1)S(1)}, u32[]{:S(2)}, u32[]{:S(2)}) collective-permute-start(bf16[288,720]{1,0:T(8,128)(2,1)S(1)} %get-tuple-element.27), channel_id=1, source_target_pairs={{0,16},{8,24},{16,0},{24,8},{1,17},{9,25},{17,1},{25,9},{2,18},{10... | collective-permute-start | bytes 1244168 | tf_op jit(solution)/shard_map/ppermute | solution.py:212
  38.4 14.3 %collective-permute-start.7 = (bf16[288,720]{1,0:T(8,128)(2,1)S(1)}, bf16[288,720]{1,0:T(8,128)(2,1)S(1)}, u32[]{:S(2)}, u32[]{:S(2)}) collective-permute-start(bf16[288,720]{1,0:T(8,128)(2,1)S(1)} %collective-permute-done.2.refs_4_.refs_10_), channel_id=1, source_target_pairs={{0,2},{1,3},{2,0},{3,1},{4,6},{5,7},{6,4},{7,5},{8,10},{9,11},{10,... | collective-permute-start | bytes 1244168 | tf_op jit(solution)/shard_map/ppermute | solution.py:212
  49.4 32.3 %copy-start.6 = (f32[1152]{0:T(1024)S(1)}, f32[1152]{0:T(1024)}, u32[]{:S(2)}) copy-start(f32[1152]{0:T(1024)} %gain_ref.7) | copy-start | bytes 13828
  49.4 32.3 %copy-start.8 = (f32[1152]{0:T(1024)S(1)}, f32[1152]{0:T(1024)}, u32[]{:S(2)}) copy-start(f32[1152]{0:T(1024)} %bias_ref.3) | copy-start | bytes 13828
  52.7 11.1 %collective-permute-start.9 = (bf16[288,720]{1,0:T(8,128)(2,1)S(1)}, bf16[288,720]{1,0:T(8,128)(2,1)S(1)}, u32[]{:S(2)}, u32[]{:S(2)}) collective-permute-start(bf16[288,720]{1,0:T(8,128)(2,1)S(1)} %collective-permute-done.1.refs_8_.refs_14_), channel_id=1, source_target_pairs={{0,2},{1,3},{2,0},{3,1},{4,6},{5,7},{6,4},{7,5},{8,10},{9,11},{10,... | collective-permute-start | bytes 1244168 | tf_op jit(solution)/shard_map/ppermute | solution.py:212
  54.2 14.2 %collective-permute-start.8 = (bf16[288,720]{1,0:T(8,128)(2,1)S(1)}, bf16[288,720]{1,0:T(8,128)(2,1)S(1)}, u32[]{:S(2)}, u32[]{:S(2)}) collective-permute-start(bf16[288,720]{1,0:T(8,128)(2,1)S(1)} %collective-permute-done.1.refs_8_.refs_14_), channel_id=1, source_target_pairs={{0,8},{8,0},{16,24},{24,16},{1,9},{9,1},{17,25},{25,17},{2,10},{10... | collective-permute-start | bytes 1244168 | tf_op jit(solution)/shard_map/ppermute | solution.py:212
  54.2 16.5 %collective-permute-start.13 = (bf16[288,720]{1,0:T(8,128)(2,1)S(1)}, bf16[288,720]{1,0:T(8,128)(2,1)S(1)}, u32[]{:S(2)}, u32[]{:S(2)}) collective-permute-start(bf16[288,720]{1,0:T(8,128)(2,1)S(1)} %collective-permute-done.2.refs_4_.refs_10_), channel_id=1, source_target_pairs={{0,1},{1,0},{2,3},{3,2},{4,5},{5,4},{6,7},{7,6},{8,9},{9,8},{10,11... | collective-permute-start | bytes 1244168 | tf_op jit(solution)/shard_map/ppermute | solution.py:212
  54.2 14.8 %collective-permute-start.12 = (bf16[128,1152]{1,0:T(8,128)(2,1)S(1)}, bf16[128,1152]{1,0:T(8,128)(2,1)S(1)}, u32[]{:S(2)}, u32[]{:S(2)}) collective-permute-start(bf16[128,1152]{1,0:T(8,128)(2,1)S(1)} %copy-done.2), channel_id=1, source_target_pairs={{0,4},{4,0},{1,5},{5,1},{2,6},{6,2},{3,7},{7,3},{8,12},{12,8},{9,1... | collective-permute-start | bytes 884744 | tf_op jit(solution)/shard_map/ppermute | solution.py:212
  55.7 15.1 %collective-permute-start.14 = (bf16[288,720]{1,0:T(8,128)(2,1)S(1)}, bf16[288,720]{1,0:T(8,128)(2,1)S(1)}, u32[]{:S(2)}, u32[]{:S(2)}) collective-permute-start(bf16[288,720]{1,0:T(8,128)(2,1)S(1)} %collective-permute-done.7.refs_6_.refs_12_), channel_id=1, source_target_pairs={{0,1},{1,0},{2,3},{3,2},{4,5},{5,4},{6,7},{7,6},{8,9},{9,8},{10,11... | collective-permute-start | bytes 1244168 | tf_op jit(solution)/shard_map/ppermute | solution.py:212
  63.8 16.3 %collective-permute-start.15 = (bf16[288,720]{1,0:T(8,128)(2,1)S(1)}, bf16[288,720]{1,0:T(8,128)(2,1)S(1)}, u32[]{:S(2)}, u32[]{:S(2)}) collective-permute-start(bf16[288,720]{1,0:T(8,128)(2,1)S(1)} %collective-permute-done.1.refs_8_.refs_14_), channel_id=1, source_target_pairs={{0,1},{1,0},{2,3},{3,2},{4,5},{5,4},{6,7},{7,6},{8,9},{9,8},{10,11... | collective-permute-start | bytes 1244168 | tf_op jit(solution)/shard_map/ppermute | solution.py:212
  68.4 24.0 %copy-start.4 = (bf16[288,1152]{1,0:T(8,128)(2,1)S(1)}, bf16[288,1152]{1,0:T(8,128)(2,1)}, u32[]{:S(2)}) copy-start(bf16[288,1152]{1,0:T(8,128)(2,1)} %refs_4_.1) | copy-start | bytes 1990660
  68.4 11.7 %collective-permute-start.16 = (bf16[288,720]{1,0:T(8,128)(2,1)S(1)}, bf16[288,720]{1,0:T(8,128)(2,1)S(1)}, u32[]{:S(2)}, u32[]{:S(2)}) collective-permute-start(bf16[288,720]{1,0:T(8,128)(2,1)S(1)} %collective-permute-done.9.refs_10_.refs_16_), channel_id=1, source_target_pairs={{0,1},{1,0},{2,3},{3,2},{4,5},{5,4},{6,7},{7,6},{8,9},{9,8},{10,11... | collective-permute-start | bytes 1244168 | tf_op jit(solution)/shard_map/ppermute | solution.py:212
  69.0 11.0 %collective-permute-start.18 = (bf16[288,432]{1,0:T(8,128)(2,1)S(1)}, bf16[288,432]{1,0:T(8,128)(2,1)S(1)}, u32[]{:S(2)}, u32[]{:S(2)}) collective-permute-start(bf16[288,432]{1,0:T(8,128)(2,1)S(1)} %slice.6), channel_id=1, source_target_pairs={{0,2},{1,3},{2,0},{3,1},{4,6},{5,7},{6,4},{7,5},{8,10},{9,11},{10,... | collective-permute-start | bytes 746504 | tf_op jit(solution)/shard_map/ppermute | solution.py:212
  70.7 7.1 %collective-permute-start.19 = (bf16[288,288]{1,0:T(8,128)(2,1)S(1)}, bf16[288,288]{1,0:T(8,128)(2,1)S(1)}, u32[]{:S(2)}, u32[]{:S(2)}) collective-permute-start(bf16[288,288]{1,0:T(8,128)(2,1)S(1)} %slice.7), channel_id=1, source_target_pairs={{0,8},{8,0},{16,24},{24,16},{1,9},{9,1},{17,25},{25,17},{2,10},{10... | collective-permute-start | bytes 497672 | tf_op jit(solution)/shard_map/ppermute | solution.py:212
  70.8 9.8 %collective-permute-start.17 = (bf16[288,720]{1,0:T(8,128)(2,1)S(1)}, bf16[288,720]{1,0:T(8,128)(2,1)S(1)}, u32[]{:S(2)}, u32[]{:S(2)}) collective-permute-start(bf16[288,720]{1,0:T(8,128)(2,1)S(1)} %collective-permute-done.8.refs_12_.refs_18_), channel_id=1, source_target_pairs={{0,1},{1,0},{2,3},{3,2},{4,5},{5,4},{6,7},{7,6},{8,9},{9,8},{10,11... | collective-permute-start | bytes 1244168 | tf_op jit(solution)/shard_map/ppermute | solution.py:212
  77.9 10.0 %collective-permute-start.10 = (bf16[64,2304]{1,0:T(8,128)(2,1)S(1)}, bf16[64,2304]{1,0:T(8,128)(2,1)S(1)}, u32[]{:S(2)}, u32[]{:S(2)}) collective-permute-start(bf16[64,2304]{1,0:T(8,128)(2,1)S(1)} %shard_map.149.refs_0_), channel_id=1, source_target_pairs={{0,4},{4,0},{1,5},{5,1},{2,6},{6,2},{3,7},{7,3},{8,12},{12,8},{9,1... | collective-permute-start | bytes 884744 | tf_op jit(solution)/shard_map/ppermute | solution.py:212
  80.0 12.4 %collective-permute-start.11 = (bf16[64,2304]{1,0:T(8,128)(2,1)S(1)}, bf16[64,2304]{1,0:T(8,128)(2,1)S(1)}, u32[]{:S(2)}, u32[]{:S(2)}) collective-permute-start(bf16[64,2304]{1,0:T(8,128)(2,1)S(1)} %shard_map.150.refs_1_), channel_id=1, source_target_pairs={{0,4},{4,0},{1,5},{5,1},{2,6},{6,2},{3,7},{7,3},{8,12},{12,8},{9,1... | collective-permute-start | bytes 884744 | tf_op jit(solution)/shard_map/ppermute | solution.py:212
  80.1 1.6 %collective-permute-start.20 = (bf16[288,432]{1,0:T(8,128)(2,1)S(1)}, bf16[288,432]{1,0:T(8,128)(2,1)S(1)}, u32[]{:S(2)}, u32[]{:S(2)}) collective-permute-start(bf16[288,432]{1,0:T(8,128)(2,1)S(1)} %collective-permute-done.18.refs_14_.refs_20_), channel_id=1, source_target_pairs={{0,1},{1,0},{2,3},{3,2},{4,5},{5,4},{6,7},{7,6},{8,9},{9,8},{10,11... | collective-permute-start | bytes 746504 | tf_op jit(solution)/shard_map/ppermute | solution.py:212
  80.1 12.2 %collective-permute-start.21 = (bf16[288,288]{1,0:T(8,128)(2,1)S(1)}, bf16[288,288]{1,0:T(8,128)(2,1)S(1)}, u32[]{:S(2)}, u32[]{:S(2)}) collective-permute-start(bf16[288,288]{1,0:T(8,128)(2,1)S(1)} %collective-permute-done.19.refs_22_), channel_id=1, source_target_pairs={{0,1},{1,0},{2,3},{3,2},{4,5},{5,4},{6,7},{7,6},{8,9},{9,8},{10,11... | collective-permute-start | bytes 497672 | tf_op jit(solution)/shard_map/ppermute | solution.py:212
  100.3 7.3 %collective-permute-start.22 = (bf16[4,32,1152]{2,1,0:T(8,128)(2,1)S(1)}, bf16[4,32,1152]{2,1,0:T(8,128)(2,1)S(1)}, u32[]{:S(2)}, u32[]{:S(2)}) collective-permute-start(bf16[4,32,1152]{2,1,0:T(8,128)(2,1)S(1)} %get-tuple-element.47), channel_id=1, source_target_pairs={{0,4},{4,0},{1,5},{5,1},{2,6},{6,2},{3,7},{7,3},{8,12},{12,8},{9,1... | collective-permute-start | bytes 884744 | tf_op jit(solution)/shard_map/ppermute | solution.py:212

commit v3 on v2

--- a/solution.py
+++ b/solution.py
@@ -474,17 +474,15 @@
     )(pre_grad, fc1_weight)
 
 
-def project(own, other, gain, bias, weights, head_dim):
+def project_early(own, other, gain, bias, weights, sections):
     patches, width = own.shape
-    length = 2 * patches
-    slots = length // 4
-    sections, copies = len(weights), len(weights[0])
+    slots = 2 * patches // 4
+    copies = len(weights[0])
     part_rows, group_cols = weights[0][0].shape
-    pieces = group_cols // head_dim
     flat = [w for parts in weights for w in parts]
 
     def body(own_ref, other_ref, gain_ref, bias_ref, *refs):
-        w_refs, (out_ref, x, n) = refs[: len(flat)], refs[len(flat) :]
+        w_refs, (sum_ref, last_ref, x, n) = refs[: len(flat)], refs[len(flat) :]
         section = lax.axis_index("section")
         put_rows(x, 0, own_ref[...].astype(f32))
         put_rows(x, patches, other_ref[...].astype(f32))
@@ -494,27 +492,51 @@
             rows = (rows * gain + bias).astype(bf16)
             for t in range(sections):
                 n[t, j * slots : (j + 1) * slots, :] = rows[:, t * part_rows : (t + 1) * part_rows]
+        last_ref[...] = n[section ^ (sections - 1)]
         for p in range(copies):
-            total = sum(
+            sum_ref[p] = sum(
                 dot(n[section ^ k], w_refs[k * copies + p][:, :group_cols])
-                for k in range(sections)
-            ).T
-            for c in range(pieces):
-                out_ref[p, c] = total[c * head_dim : (c + 1) * head_dim].astype(bf16)
-
-    shape = (copies, pieces, head_dim, length)
+                for k in range(len(weights))
+            )
+
+    shapes = [(copies, 2 * patches, group_cols), (2 * patches, part_rows)]
     return run_kernel(
         body,
         (1,),
         [whole(x) for x in (own, other, gain, bias, *flat)],
-        pl.BlockSpec(shape, lambda i, *_: (0, 0, 0, 0)),
-        struct(shape, bf16),
         [
-            pltpu.VMEM((width // LANES, length, LANES), f32),
-            pltpu.VMEM((sections, length, part_rows), bf16),
+            pl.BlockSpec(shapes[0], lambda i, *_: (0, 0, 0)),
+            pl.BlockSpec(shapes[1], lambda i, *_: (0, 0)),
+        ],
+        [struct(shapes[0], f32), struct(shapes[1], bf16)],
+        [
+            pltpu.VMEM((width // LANES, 2 * patches, LANES), f32),
+            pltpu.VMEM((sections, 2 * patches, part_rows), bf16),
         ],
         limit=30,
     )(own, other, gain, bias, *flat)
+
+
+def project_late(sums, rows, weights, head_dim):
+    copies, length, group_cols = sums.shape
+    pieces = group_cols // head_dim
+
+    def body(sum_ref, rows_ref, *refs):
+        w_refs, out_ref = refs[:-1], refs[-1]
+        for p in range(copies):
+            total = (sum_ref[p] + dot(rows_ref[...], w_refs[p][:, :group_cols])).T
+            for c in range(pieces):
+                out_ref[p, c] = total[c * head_dim : (c + 1) * head_dim].astype(bf16)
+
+    shape = (copies, pieces, head_dim, length)
+    return run_kernel(
+        body,
+        (1,),
+        [whole(x) for x in (sums, rows, *weights)],
+        pl.BlockSpec(shape, lambda i, *_: (0, 0, 0, 0)),
+        struct(shape, bf16),
+        limit=20,
+    )(sums, rows, *weights)
 
 
 def attention_back(
@@ -733,7 +755,19 @@
     second_theirs = swap(second, "vit", 1)
     cross_core = swap(cross, "dp", 1)
     far_diagonal = swap(far_chip, "dp", 1)
-    cross_chip, late_proj = lax.optimization_barrier((cross_chip, late_proj))
+    sums, last_rows = project_early(
+        vit_in,
+        vit_in_other,
+        ln_gain,
+        ln_bias,
+        [
+            own_parts,
+            [near, near_core, near_chip, near_diagonal],
+            [far, far_core, far_chip, far_diagonal],
+        ],
+        sections,
+    )
+    cross_chip, late_proj, sums = lax.optimization_barrier((cross_chip, late_proj, sums))
     cross_diagonal = swap(cross_chip, "dp", 1)
     late_proj_core = swap(late_proj, "dp", 1)
     weights = [
@@ -744,7 +778,7 @@
     ]
     proj_apart = {(3, 2): late_proj, (3, 3): late_proj_core}
 
-    projected = project(vit_in, vit_in_other, ln_gain, ln_bias, weights, head_dim)
+    projected = project_late(sums, last_rows, weights[-1], head_dim)
     normed_mine, normed_sent, out_grad = attention_back(
         image_rows,
         vit_out,

time: 109 us -> 105 us (0.963)
  waiting for transfers between devices: 45.1 us -> 36.8 us
  starting transfers between devices: 21.3 us -> 26.2 us
    ppermute x23, waiting for transfers between devices: 45.1 us -> 36.8 us  [swap(): return lax.ppermute(values, axis, [(i, i ^ bit) for i in range(count)])]
    ppermute x23, starting transfers between devices: 21.3 us -> 26.2 us  [swap(): return lax.ppermute(values, axis, [(i, i ^ bit) for i in range(count)])]
    pallas_call x1 -> x2, Pallas kernels: 3.03 us -> 3.23 us  [the longest x1 2.39 us: project_early(): run_kernel(body, (1,), [whole(x) for x in (own, other, gain, bias, *flat)...]
  transfers between devices with their start and end apart: 23 -> 23, of which waited for: 10 -> 8; matrix products, arithmetic and copies ran while one was open for 1% -> 0% of each run, Pallas kernels for 26% -> 27%
where the time goes in v3:
time: 105 us
  Pallas kernels  37.7 us (36%)
  waiting for transfers between devices  36.8 us (35%)
  starting transfers between devices  26.2 us (25%)
  local copies, waits for them, and re-layouts  4.18 us (4%)
    ppermute x23, waiting for transfers between devices, swap(): return lax.ppermute(values, axis, [(i, i ^ bit) for i in range(count)])  36.8 us
    ppermute x23, starting transfers between devices, swap(): return lax.ppermute(values, axis, [(i, i ^ bit) for i in range(count)])  26.2 us
    pallas_call x1, Pallas kernels, pre_grad_of(): run_kernel(body, (1,), [whole(x) for x in (vis_slot, own, other, slope)]...  9.4 us
    pallas_call x2, Pallas kernels, merge_part(): run_kernel(body, (1,), [whole(pre_grad), RESIDENT], pl.BlockSpec((slots,...  9.06 us
    pallas_call x1, Pallas kernels, attention_back(): run_kernel(body, (1,), [whole(x) for x in operands], [pl.BlockSpec(shape,...  7.94 us
    pallas_call x1, Pallas kernels, slope_of(): run_kernel(body, (1,), [whole(x) for x in (own, other, gain, bias, fc1_bi...  5.47 us
    unnamed x30, local copies, waits for them, and re-layouts  2.71 us
    pallas_call x1, Pallas kernels, project_early(): run_kernel(body, (1,), [whole(x) for x in (own, other, gain, bias, *flat)...  2.39 us
  transfers between devices with their start and end apart: 23, of which 8 were waited for; matrix products, arithmetic and copies ran while one was open for 0% of the time, Pallas kernels for 27%

profile of v3, /device:TPU:0, one launch (start us, length us, event | category | flops | bytes accessed | tf_op | source)
XLA Modules:
  0.0 105.2 jit_solution(15964289815644140068)
XLA Ops:
  0.0 1.3 %dynamic-slice_bitcast_fusion = (bf16[32,4096]{1,0:T(8,128)(2,1)S(1)}, bf16[32,4096]{1,0:T(8,128)(2,1)S(1)}, bf16[32,4096]{1,0:T(8,128)(2,1)S(1)}) fusion(bf16[4,32,4096]{2,1,0:T(8,128)(2,1)} %bitcast.8, s32[]{:T(128)S(6)} %select_n.12, s32[]{:T(128)S(6)} %select_n.11, s32[]{:T(128)S(6)} %select_n.10), kind=kLoop, calls=%fused_computation | loop fusion | bytes 1572876 | tf_op jit(solution)/shard_map/jit(dynamic_index_in_dim)/squeeze | solution.py:724
  1.3 3.2 %collective-permute-start.3 = (bf16[32,4096]{1,0:T(8,128)(2,1)S(1)}, bf16[32,4096]{1,0:T(8,128)(2,1)S(1)}, u32[]{:S(2)}, u32[]{:S(2)}) collective-permute-start(bf16[32,4096]{1,0:T(8,128)(2,1)S(1)} %get-tuple-element.57), channel_id=1, source_target_pairs={{0,8},{8,0},{16,24},{24,16},{1,9},{9,1},{17,25},{25,17},{2,10},{10... | collective-permute-start | bytes 786440 | tf_op jit(solution)/shard_map/ppermute | solution.py:212
  4.5 2.6 %collective-permute-start.4 = (bf16[32,4096]{1,0:T(8,128)(2,1)S(1)}, bf16[32,4096]{1,0:T(8,128)(2,1)S(1)}, u32[]{:S(2)}, u32[]{:S(2)}) collective-permute-start(bf16[32,4096]{1,0:T(8,128)(2,1)S(1)} %get-tuple-element.56), channel_id=1, source_target_pairs={{0,16},{8,24},{16,0},{24,8},{1,17},{9,25},{17,1},{25,9},{2,18},{10... | collective-permute-start | bytes 786440 | tf_op jit(solution)/shard_map/ppermute | solution.py:212
  7.1 1.7 %collective-permute-start = (bf16[128,1152]{1,0:T(8,128)(2,1)}, bf16[128,1152]{1,0:T(8,128)(2,1)S(1)}, u32[]{:S(2)}, u32[]{:S(2)}) collective-permute-start(bf16[128,1152]{1,0:T(8,128)(2,1)} %own_ref.6), channel_id=1, source_target_pairs={{0,4},{4,0},{1,5},{5,1},{2,6},{6,2},{3,7},{7,3},{8,12},{12,8},{9,1... | collective-permute-start | bytes 884744 | tf_op jit(solution)/shard_map/ppermute | solution.py:212
  8.8 1.1 %copy-done.3 = bf16[288,1152]{1,0:T(8,128)(2,1)S(1)} copy-done((bf16[288,1152]{1,0:T(8,128)(2,1)S(1)}, bf16[288,1152]{1,0:T(8,128)(2,1)}, u32[]{:S(2)}) %copy-start.3) | copy-done | bytes 663576
  9.9 1.6 %copy-done.12 = bf16[288,3456]{1,0:T(8,128)(2,1)S(1)} copy-done((bf16[288,3456]{1,0:T(8,128)(2,1)S(1)}, bf16[288,3456]{1,0:T(8,128)(2,1)}, u32[]{:S(2)}) %copy-start.12) | copy-done | bytes 1990680
  11.4 0.5 shard_map.145
  11.9 0.0 copy-start.1
  11.9 0.0 copy-start.11
  12.0 0.0 copy-start.9
  12.0 0.0 copy-start.10
  12.0 0.0 copy-start.2
  12.0 0.7 collective-permute-start.2
  12.7 2.7 %collective-permute-done.other_ref = bf16[128,1152]{1,0:T(8,128)(2,1)S(1)} collective-permute-done((bf16[128,1152]{1,0:T(8,128)(2,1)}, bf16[128,1152]{1,0:T(8,128)(2,1)S(1)}, u32[]{:S(2)}, u32[]{:S(2)}) %collective-permute-start) | collective-permute-done | bytes 294944 | tf_op jit(solution)/shard_map/ppermute | solution.py:212
  15.5 5.5 %shard_map.146.slope_ref = f32[64,2304]{1,0:T(8,128)S(1)} custom-call(bf16[128,1152]{1,0:T(8,128)(2,1)S(1)} %copy-done.5, bf16[128,1152]{1,0:T(8,128)(2,1)S(1)} %collective-permute-done.other_ref, f32[1152]{0:T(1024)S(1)} %copy-done.8, f32[1152]{0:T(1024)S(1)} %copy-done.14, f32[2304]{0:T(1024)S(1)} %copy-done.13, bf16[4608,2304]{1,0:T(8,128)(2,1)S(1)} %copy-done), custom_call_target="tpu_custom_call" | custom-call | flops 8000000000 | tf_op jit(solution)/shard_map/pallas_call | solution.py:369
  21.0 4.8 %collective-permute-done.4.refs_1_ = bf16[32,4096]{1,0:T(8,128)(2,1)S(1)} collective-permute-done((bf16[32,4096]{1,0:T(8,128)(2,1)S(1)}, bf16[32,4096]{1,0:T(8,128)(2,1)S(1)}, u32[]{:S(2)}, u32[]{:S(2)}) %collective-permute-start.4) | collective-permute-done | bytes 262176 | tf_op jit(solution)/shard_map/ppermute | solution.py:212
  25.8 0.9 shard_map.147.own_ref
  26.7 1.6 %collective-permute-start.6 = (bf16[32,4096]{1,0:T(8,128)(2,1)S(1)}, bf16[32,4096]{1,0:T(8,128)(2,1)S(1)}, u32[]{:S(2)}, u32[]{:S(2)}) collective-permute-start(bf16[32,4096]{1,0:T(8,128)(2,1)S(1)} %shard_map.147.own_ref), channel_id=1, source_target_pairs={{0,4},{4,0},{1,5},{5,1},{2,6},{6,2},{3,7},{7,3},{8,12},{12,8},{9,1... | collective-permute-start | bytes 786440 | tf_op jit(solution)/shard_map/ppermute | solution.py:212
  28.3 5.8 %collective-permute-start.1 = (bf16[288,720]{1,0:T(8,128)(2,1)S(1)}, bf16[288,720]{1,0:T(8,128)(2,1)S(1)}, u32[]{:S(2)}, u32[]{:S(2)}) collective-permute-start(bf16[288,720]{1,0:T(8,128)(2,1)S(1)} %get-tuple-element.30), channel_id=1, source_target_pairs={{0,16},{8,24},{16,0},{24,8},{1,17},{9,25},{17,1},{25,9},{2,18},{10... | collective-permute-start | bytes 1244168 | tf_op jit(solution)/shard_map/ppermute | solution.py:212
  34.1 1.5 %collective-permute-start.7 = (bf16[288,720]{1,0:T(8,128)(2,1)S(1)}, bf16[288,720]{1,0:T(8,128)(2,1)S(1)}, u32[]{:S(2)}, u32[]{:S(2)}) collective-permute-start(bf16[288,720]{1,0:T(8,128)(2,1)S(1)} %collective-permute-done.2.refs_4_.refs_10_), channel_id=1, source_target_pairs={{0,2},{1,3},{2,0},{3,1},{4,6},{5,7},{6,4},{7,5},{8,10},{9,11},{10,... | collective-permute-start | bytes 1244168 | tf_op jit(solution)/shard_map/ppermute | solution.py:212
  35.6 9.4 %shard_map.148.pre_ref = bf16[64,2304]{1,0:T(8,128)(2,1)S(1)} custom-call(s32[2,4]{1,0:T(2,128)S(1)} %bitcast.9, s32[2,128]{1,0:T(2,128)S(1)} %copy-done.10, bf16[32,4096]{1,0:T(8,128)(2,1)S(1)} %shard_map.147.own_ref, bf16[32,4096]{1,0:T(8,128)(2,1)S(1)} %collective-permute-done.6.other_ref, f32[64,2304]{1,0:T(8,128)S(1)} %shard_map.146.slope_ref, ...), custom_call_target="tpu_custom_call" | custom-call | tf_op jit(solution)/shard_map/pallas_call | solution.py:429
  45.0 0.0 copy-start.6
  45.1 7.3 %collective-permute-done.1.refs_8_.refs_14_ = bf16[288,720]{1,0:T(8,128)(2,1)S(1)} collective-permute-done((bf16[288,720]{1,0:T(8,128)(2,1)S(1)}, bf16[288,720]{1,0:T(8,128)(2,1)S(1)}, u32[]{:S(2)}, u32[]{:S(2)}) %collective-permute-start.1) | collective-permute-done | bytes 414752 | tf_op jit(solution)/shard_map/ppermute | solution.py:212
  52.4 1.5 %collective-permute-start.9 = (bf16[288,720]{1,0:T(8,128)(2,1)S(1)}, bf16[288,720]{1,0:T(8,128)(2,1)S(1)}, u32[]{:S(2)}, u32[]{:S(2)}) collective-permute-start(bf16[288,720]{1,0:T(8,128)(2,1)S(1)} %collective-permute-done.1.refs_8_.refs_14_), channel_id=1, source_target_pairs={{0,2},{1,3},{2,0},{3,1},{4,6},{5,7},{6,4},{7,5},{8,10},{9,11},{10,... | collective-permute-start | bytes 1244168 | tf_op jit(solution)/shard_map/ppermute | solution.py:212
  53.9 0.5 collective-permute-start.16
  54.4 0.5 collective-permute-start.14
  54.9 4.5 %shard_map.150.refs_1_ = bf16[64,2304]{1,0:T(8,128)(2,1)S(1)} custom-call(bf16[64,2304]{1,0:T(8,128)(2,1)S(1)} %shard_map.148.pre_ref, bf16[4608,2304]{1,0:T(8,128)(2,1)S(1)} %copy-done), custom_call_target="tpu_custom_call" | custom-call | tf_op jit(solution)/shard_map/pallas_call | solution.py:467
  59.5 0.0 copy-start.4
  59.5 3.9 %collective-permute-done.8.refs_0_.refs_18_ = bf16[288,720]{1,0:T(8,128)(2,1)S(1)} collective-permute-done((bf16[288,720]{1,0:T(8,128)(2,1)S(1)}, bf16[288,720]{1,0:T(8,128)(2,1)S(1)}, u32[]{:S(2)}, u32[]{:S(2)}) %collective-permute-start.8) | collective-permute-done | bytes 414752 | tf_op jit(solution)/shard_map/ppermute | solution.py:212
  63.4 0.5 collective-permute-start.18
  63.9 1.6 %collective-permute-start.12 = (bf16[288,432]{1,0:T(8,128)(2,1)S(1)}, bf16[288,432]{1,0:T(8,128)(2,1)S(1)}, u32[]{:S(2)}, u32[]{:S(2)}) collective-permute-start(bf16[288,432]{1,0:T(8,128)(2,1)S(1)} %slice.6), channel_id=1, source_target_pairs={{0,2},{1,3},{2,0},{3,1},{4,6},{5,7},{6,4},{7,5},{8,10},{9,11},{10,... | collective-permute-start | bytes 746504 | tf_op jit(solution)/shard_map/ppermute | solution.py:212
  65.5 0.1 slice.7
  65.7 1.3 %collective-permute-start.13 = (bf16[288,288]{1,0:T(8,128)(2,1)S(1)}, bf16[288,288]{1,0:T(8,128)(2,1)S(1)}, u32[]{:S(2)}, u32[]{:S(2)}) collective-permute-start(bf16[288,288]{1,0:T(8,128)(2,1)S(1)} %slice.7), channel_id=1, source_target_pairs={{0,8},{8,0},{16,24},{24,16},{1,9},{9,1},{17,25},{25,17},{2,10},{10... | collective-permute-start | bytes 497672 | tf_op jit(solution)/shard_map/ppermute | solution.py:212
  67.0 4.5 %shard_map.149.refs_0_ = bf16[64,2304]{1,0:T(8,128)(2,1)S(1)} custom-call(bf16[64,2304]{1,0:T(8,128)(2,1)S(1)} %shard_map.148.pre_ref, bf16[4608,2304]{1,0:T(8,128)(2,1)S(1)} %copy-done), custom_call_target="tpu_custom_call" | custom-call | tf_op jit(solution)/shard_map/pallas_call | solution.py:467
  71.5 0.0 collective-permute-done.17.refs_9_.refs_15_
  71.5 0.3 collective-permute-start.10
  71.9 1.8 %collective-permute-start.11 = (bf16[64,2304]{1,0:T(8,128)(2,1)S(1)}, bf16[64,2304]{1,0:T(8,128)(2,1)S(1)}, u32[]{:S(2)}, u32[]{:S(2)}) collective-permute-start(bf16[64,2304]{1,0:T(8,128)(2,1)S(1)} %shard_map.150.refs_1_), channel_id=1, source_target_pairs={{0,4},{4,0},{1,5},{5,1},{2,6},{6,2},{3,7},{7,3},{8,12},{12,8},{9,1... | collective-permute-start | bytes 884744 | tf_op jit(solution)/shard_map/ppermute | solution.py:212
  73.6 2.4 %shard_map.151 = (f32[4,256,432]{2,1,0:T(8,128)S(1)}, bf16[256,288]{1,0:T(8,128)(2,1)S(1)}) custom-call(bf16[128,1152]{1,0:T(8,128)(2,1)S(1)} %copy-done.2, bf16[128,1152]{1,0:T(8,128)(2,1)S(1)} %collective-permute-done.14.other_ref, f32[1152]{0:T(1024)S(1)} %copy-done.6, f32[1152]{0:T(1024)S(1)} %copy-done.7, ...), custom_call_target="tpu_custom_call" | custom-call | tf_op jit(solution)/shard_map/pallas_call | solution.py:503
  76.1 0.1 collective-permute-start.20
  76.1 0.5 collective-permute-start.21
  76.6 1.1 %collective-permute-done.20.refs_3_.refs_21_ = bf16[288,432]{1,0:T(8,128)(2,1)S(1)} collective-permute-done((bf16[288,432]{1,0:T(8,128)(2,1)S(1)}, bf16[288,432]{1,0:T(8,128)(2,1)S(1)}, u32[]{:S(2)}, u32[]{:S(2)}) %collective-permute-start.20) | collective-permute-done | bytes 248864 | tf_op jit(solution)/shard_map/ppermute | solution.py:212
  77.7 0.8 shard_map.152.refs_5_
  78.6 2.9 %collective-permute-done.10.refs_2_ = bf16[64,2304]{1,0:T(8,128)(2,1)S(1)} collective-permute-done((bf16[64,2304]{1,0:T(8,128)(2,1)S(1)}, bf16[64,2304]{1,0:T(8,128)(2,1)S(1)}, u32[]{:S(2)}, u32[]{:S(2)}) %collective-permute-start.10) | collective-permute-done | bytes 294944 | tf_op jit(solution)/shard_map/ppermute | solution.py:212
  81.5 5.9 %collective-permute-done.11.refs_3_ = bf16[64,2304]{1,0:T(8,128)(2,1)S(1)} collective-permute-done((bf16[64,2304]{1,0:T(8,128)(2,1)S(1)}, bf16[64,2304]{1,0:T(8,128)(2,1)S(1)}, u32[]{:S(2)}, u32[]{:S(2)}) %collective-permute-start.11) | collective-permute-done | bytes 294944 | tf_op jit(solution)/shard_map/ppermute | solution.py:212
  87.4 7.9 %shard_map.153 = (f32[4,32,1152]{2,1,0:T(8,128)S(1)}, bf16[4,32,1152]{2,1,0:T(8,128)(2,1)S(1)}, bf16[4,32,1152]{2,1,0:T(8,128)(2,1)S(1)}) custom-call(s32[2,4]{1,0:T(2,128)S(1)} %bitcast.10, bf16[128,1152]{1,0:T(8,128)(2,1)S(1)} %copy-done.5, bf16[128,1152]{1,0:T(8,128)(2,1)S(1)} %collective-permute-done.other_ref, f32[1152]{0:T(1024)S(1)} %copy-done.8, ...), custom_call_target="tpu_custom_call" | custom-call | tf_op jit(solution)/shard_map/pallas_call | solution.py:649
  95.3 0.5 collective-permute-start.22
  95.8 8.1 %collective-permute-done.22.theirs_ref = bf16[4,32,1152]{2,1,0:T(8,128)(2,1)S(1)} collective-permute-done((bf16[4,32,1152]{2,1,0:T(8,128)(2,1)S(1)}, bf16[4,32,1152]{2,1,0:T(8,128)(2,1)S(1)}, u32[]{:S(2)}, u32[]{:S(2)}) %collective-permute-start.22) | collective-permute-done | bytes 294944 | tf_op jit(solution)/shard_map/ppermute | solution.py:212
  103.9 1.3 %shard_map.154 = bf16[128,1152]{1,0:T(8,128)(2,1)} custom-call(bf16[128,1152]{1,0:T(8,128)(2,1)S(1)} %copy-done.2, f32[1152]{0:T(1024)S(1)} %copy-done.6, f32[4,32,1152]{2,1,0:T(8,128)S(1)} %get-tuple-element.52.mine_ref, bf16[4,32,1152]{2,1,0:T(8,128)(2,1)S(1)} %collective-permute-done.22.theirs_ref, bf16[4,32,1152]{2,1,0:T(8,128)(2,1)S(1)} %get-tuple-element.54.grad_ref), custom_call_target="tpu_custom_call" | custom-call | tf_op jit(solution)/shard_map/pallas_call | solution.py:684
  (41 shorter events, 0.1 us)
Async XLA Ops:
  0.0 15.5 %copy-start.8 = (f32[1152]{0:T(1024)S(1)}, f32[1152]{0:T(1024)}, u32[]{:S(2)}) copy-start(f32[1152]{0:T(1024)} %gain_ref.6) | copy-start | bytes 13828
  0.0 15.5 %copy-start.14 = (f32[1152]{0:T(1024)S(1)}, f32[1152]{0:T(1024)}, u32[]{:S(2)}) copy-start(f32[1152]{0:T(1024)} %bias_ref.2) | copy-start | bytes 13828
  0.0 15.5 %copy-start.13 = (f32[2304]{0:T(1024)S(1)}, f32[2304]{0:T(1024)}, u32[]{:S(2)}) copy-start(f32[2304]{0:T(1024)} %fc1b_ref.1) | copy-start | bytes 27652
  0.0 15.5 %copy-start = (bf16[4608,2304]{1,0:T(8,128)(2,1)S(1)}, bf16[4608,2304]{1,0:T(8,128)(2,1)}, u32[]{:S(2)}) copy-start(bf16[4608,2304]{1,0:T(8,128)(2,1)} %fc1_ref.5) | copy-start | bytes 63700996
  1.3 19.7 %collective-permute-start.3 = (bf16[32,4096]{1,0:T(8,128)(2,1)S(1)}, bf16[32,4096]{1,0:T(8,128)(2,1)S(1)}, u32[]{:S(2)}, u32[]{:S(2)}) collective-permute-start(bf16[32,4096]{1,0:T(8,128)(2,1)S(1)} %get-tuple-element.57), channel_id=1, source_target_pairs={{0,8},{8,0},{16,24},{24,16},{1,9},{9,1},{17,25},{25,17},{2,10},{10... | collective-permute-start | bytes 786440 | tf_op jit(solution)/shard_map/ppermute | solution.py:212
  4.5 21.4 %collective-permute-start.4 = (bf16[32,4096]{1,0:T(8,128)(2,1)S(1)}, bf16[32,4096]{1,0:T(8,128)(2,1)S(1)}, u32[]{:S(2)}, u32[]{:S(2)}) collective-permute-start(bf16[32,4096]{1,0:T(8,128)(2,1)S(1)} %get-tuple-element.56), channel_id=1, source_target_pairs={{0,16},{8,24},{16,0},{24,8},{1,17},{9,25},{17,1},{25,9},{2,18},{10... | collective-permute-start | bytes 786440 | tf_op jit(solution)/shard_map/ppermute | solution.py:212
  7.1 18.8 %collective-permute-start.5 = (bf16[32,4096]{1,0:T(8,128)(2,1)S(1)}, bf16[32,4096]{1,0:T(8,128)(2,1)S(1)}, u32[]{:S(2)}, u32[]{:S(2)}) collective-permute-start(bf16[32,4096]{1,0:T(8,128)(2,1)S(1)} %get-tuple-element.55), channel_id=1, source_target_pairs={{0,24},{8,16},{16,8},{24,0},{1,25},{9,17},{17,9},{25,1},{2,26},{10... | collective-permute-start | bytes 786440 | tf_op jit(solution)/shard_map/ppermute | solution.py:212
  7.1 8.4 %collective-permute-start = (bf16[128,1152]{1,0:T(8,128)(2,1)}, bf16[128,1152]{1,0:T(8,128)(2,1)S(1)}, u32[]{:S(2)}, u32[]{:S(2)}) collective-permute-start(bf16[128,1152]{1,0:T(8,128)(2,1)} %own_ref.6), channel_id=1, source_target_pairs={{0,4},{4,0},{1,5},{5,1},{2,6},{6,2},{3,7},{7,3},{8,12},{12,8},{9,1... | collective-permute-start | bytes 884744 | tf_op jit(solution)/shard_map/ppermute | solution.py:212
  8.8 1.1 %copy-start.3 = (bf16[288,1152]{1,0:T(8,128)(2,1)S(1)}, bf16[288,1152]{1,0:T(8,128)(2,1)}, u32[]{:S(2)}) copy-start(bf16[288,1152]{1,0:T(8,128)(2,1)} %refs_4_.1) | copy-start | bytes 1990660
  9.9 1.6 %copy-start.12 = (bf16[288,3456]{1,0:T(8,128)(2,1)S(1)}, bf16[288,3456]{1,0:T(8,128)(2,1)}, u32[]{:S(2)}) copy-start(bf16[288,3456]{1,0:T(8,128)(2,1)} %qkv_ref.1) | copy-start | bytes 5971972
  11.4 4.1 %copy-start.5 = (bf16[128,1152]{1,0:T(8,128)(2,1)S(1)}, bf16[128,1152]{1,0:T(8,128)(2,1)}, u32[]{:S(2)}) copy-start(bf16[128,1152]{1,0:T(8,128)(2,1)} %own_ref.6) | copy-start | bytes 884740
  11.9 13.9 %copy-start.1 = (bf16[1,128,4096]{2,1,0:T(8,128)(2,1)S(1)}, bf16[1,128,4096]{2,1,0:T(8,128)(2,1)}, u32[]{:S(2)}) copy-start(bf16[1,128,4096]{2,1,0:T(8,128)(2,1)} %grad_ref.1) | copy-start | bytes 3145732
  11.9 13.9 %copy-start.11 = (s32[4]{0:T(128)S(1)}, s32[4]{0:T(128)}, u32[]{:S(2)}) copy-start(s32[4]{0:T(128)} %layer_ref.1) | copy-start | bytes 52
  12.0 23.7 %copy-start.9 = (s32[4,2]{0,1:T(2,128)S(1)}, s32[4,2]{0,1:T(2,128)}, u32[]{:S(2)}) copy-start(s32[4,2]{0,1:T(2,128)} %param.17) | copy-start | bytes 100
  12.0 23.7 %copy-start.10 = (s32[2,128]{1,0:T(2,128)S(1)}, s32[2,128]{1,0:T(2,128)}, u32[]{:S(2)}) copy-start(s32[2,128]{1,0:T(2,128)} %slot_ref.1) | copy-start | bytes 3076
  12.0 42.4 %copy-start.2 = (bf16[128,1152]{1,0:T(8,128)(2,1)S(1)}, bf16[128,1152]{1,0:T(8,128)(2,1)}, u32[]{:S(2)}) copy-start(bf16[128,1152]{1,0:T(8,128)(2,1)} %own_ref.7) | copy-start | bytes 884740
  12.0 22.1 %collective-permute-start.2 = (bf16[288,720]{1,0:T(8,128)(2,1)S(1)}, bf16[288,720]{1,0:T(8,128)(2,1)S(1)}, u32[]{:S(2)}, u32[]{:S(2)}) collective-permute-start(bf16[288,720]{1,0:T(8,128)(2,1)S(1)} %get-tuple-element.30), channel_id=1, source_target_pairs={{0,8},{8,0},{16,24},{24,16},{1,9},{9,1},{17,25},{25,17},{2,10},{10... | collective-permute-start | bytes 1244168 | tf_op jit(solution)/shard_map/ppermute | solution.py:212
  26.7 7.4 %collective-permute-start.6 = (bf16[32,4096]{1,0:T(8,128)(2,1)S(1)}, bf16[32,4096]{1,0:T(8,128)(2,1)S(1)}, u32[]{:S(2)}, u32[]{:S(2)}) collective-permute-start(bf16[32,4096]{1,0:T(8,128)(2,1)S(1)} %shard_map.147.own_ref), channel_id=1, source_target_pairs={{0,4},{4,0},{1,5},{5,1},{2,6},{6,2},{3,7},{7,3},{8,12},{12,8},{9,1... | collective-permute-start | bytes 786440 | tf_op jit(solution)/shard_map/ppermute | solution.py:212
  28.3 24.1 %collective-permute-start.1 = (bf16[288,720]{1,0:T(8,128)(2,1)S(1)}, bf16[288,720]{1,0:T(8,128)(2,1)S(1)}, u32[]{:S(2)}, u32[]{:S(2)}) collective-permute-start(bf16[288,720]{1,0:T(8,128)(2,1)S(1)} %get-tuple-element.30), channel_id=1, source_target_pairs={{0,16},{8,24},{16,0},{24,8},{1,17},{9,25},{17,1},{25,9},{2,18},{10... | collective-permute-start | bytes 1244168 | tf_op jit(solution)/shard_map/ppermute | solution.py:212
  34.1 18.3 %collective-permute-start.7 = (bf16[288,720]{1,0:T(8,128)(2,1)S(1)}, bf16[288,720]{1,0:T(8,128)(2,1)S(1)}, u32[]{:S(2)}, u32[]{:S(2)}) collective-permute-start(bf16[288,720]{1,0:T(8,128)(2,1)S(1)} %collective-permute-done.2.refs_4_.refs_10_), channel_id=1, source_target_pairs={{0,2},{1,3},{2,0},{3,1},{4,6},{5,7},{6,4},{7,5},{8,10},{9,11},{10,... | collective-permute-start | bytes 1244168 | tf_op jit(solution)/shard_map/ppermute | solution.py:212
  45.0 28.6 %copy-start.6 = (f32[1152]{0:T(1024)S(1)}, f32[1152]{0:T(1024)}, u32[]{:S(2)}) copy-start(f32[1152]{0:T(1024)} %gain_ref.7) | copy-start | bytes 13828
  45.0 28.6 %copy-start.7 = (f32[1152]{0:T(1024)S(1)}, f32[1152]{0:T(1024)}, u32[]{:S(2)}) copy-start(f32[1152]{0:T(1024)} %bias_ref.3) | copy-start | bytes 13828
  52.4 11.0 %collective-permute-start.8 = (bf16[288,720]{1,0:T(8,128)(2,1)S(1)}, bf16[288,720]{1,0:T(8,128)(2,1)S(1)}, u32[]{:S(2)}, u32[]{:S(2)}) collective-permute-start(bf16[288,720]{1,0:T(8,128)(2,1)S(1)} %collective-permute-done.1.refs_8_.refs_14_), channel_id=1, source_target_pairs={{0,8},{8,0},{16,24},{24,16},{1,9},{9,1},{17,25},{25,17},{2,10},{10... | collective-permute-start | bytes 1244168 | tf_op jit(solution)/shard_map/ppermute | solution.py:212
  52.4 11.0 %collective-permute-start.9 = (bf16[288,720]{1,0:T(8,128)(2,1)S(1)}, bf16[288,720]{1,0:T(8,128)(2,1)S(1)}, u32[]{:S(2)}, u32[]{:S(2)}) collective-permute-start(bf16[288,720]{1,0:T(8,128)(2,1)S(1)} %collective-permute-done.1.refs_8_.refs_14_), channel_id=1, source_target_pairs={{0,2},{1,3},{2,0},{3,1},{4,6},{5,7},{6,4},{7,5},{8,10},{9,11},{10,... | collective-permute-start | bytes 1244168 | tf_op jit(solution)/shard_map/ppermute | solution.py:212
  53.9 11.8 %collective-permute-start.15 = (bf16[288,720]{1,0:T(8,128)(2,1)S(1)}, bf16[288,720]{1,0:T(8,128)(2,1)S(1)}, u32[]{:S(2)}, u32[]{:S(2)}) collective-permute-start(bf16[288,720]{1,0:T(8,128)(2,1)S(1)} %collective-permute-done.2.refs_4_.refs_10_), channel_id=1, source_target_pairs={{0,1},{1,0},{2,3},{3,2},{4,5},{5,4},{6,7},{7,6},{8,9},{9,8},{10,11... | collective-permute-start | bytes 1244168 | tf_op jit(solution)/shard_map/ppermute | solution.py:212
  53.9 13.1 %collective-permute-start.16 = (bf16[288,720]{1,0:T(8,128)(2,1)S(1)}, bf16[288,720]{1,0:T(8,128)(2,1)S(1)}, u32[]{:S(2)}, u32[]{:S(2)}) collective-permute-start(bf16[288,720]{1,0:T(8,128)(2,1)S(1)} %collective-permute-done.7.refs_6_.refs_12_), channel_id=1, source_target_pairs={{0,1},{1,0},{2,3},{3,2},{4,5},{5,4},{6,7},{7,6},{8,9},{9,8},{10,11... | collective-permute-start | bytes 1244168 | tf_op jit(solution)/shard_map/ppermute | solution.py:212
  54.4 9.5 %collective-permute-start.14 = (bf16[128,1152]{1,0:T(8,128)(2,1)S(1)}, bf16[128,1152]{1,0:T(8,128)(2,1)S(1)}, u32[]{:S(2)}, u32[]{:S(2)}) collective-permute-start(bf16[128,1152]{1,0:T(8,128)(2,1)S(1)} %copy-done.2), channel_id=1, source_target_pairs={{0,4},{4,0},{1,5},{5,1},{2,6},{6,2},{3,7},{7,3},{8,12},{12,8},{9,1... | collective-permute-start | bytes 884744 | tf_op jit(solution)/shard_map/ppermute | solution.py:212
  59.5 27.9 %copy-start.4 = (bf16[288,1152]{1,0:T(8,128)(2,1)S(1)}, bf16[288,1152]{1,0:T(8,128)(2,1)}, u32[]{:S(2)}) copy-start(bf16[288,1152]{1,0:T(8,128)(2,1)} %refs_4_.1) | copy-start | bytes 1990660
  63.4 8.1 %collective-permute-start.17 = (bf16[288,720]{1,0:T(8,128)(2,1)S(1)}, bf16[288,720]{1,0:T(8,128)(2,1)S(1)}, u32[]{:S(2)}, u32[]{:S(2)}) collective-permute-start(bf16[288,720]{1,0:T(8,128)(2,1)S(1)} %collective-permute-done.1.refs_8_.refs_14_), channel_id=1, source_target_pairs={{0,1},{1,0},{2,3},{3,2},{4,5},{5,4},{6,7},{7,6},{8,9},{9,8},{10,11... | collective-permute-start | bytes 1244168 | tf_op jit(solution)/shard_map/ppermute | solution.py:212
  63.4 8.5 %collective-permute-start.18 = (bf16[288,720]{1,0:T(8,128)(2,1)S(1)}, bf16[288,720]{1,0:T(8,128)(2,1)S(1)}, u32[]{:S(2)}, u32[]{:S(2)}) collective-permute-start(bf16[288,720]{1,0:T(8,128)(2,1)S(1)} %collective-permute-done.9.refs_10_.refs_16_), channel_id=1, source_target_pairs={{0,1},{1,0},{2,3},{3,2},{4,5},{5,4},{6,7},{7,6},{8,9},{9,8},{10,11... | collective-permute-start | bytes 1244168 | tf_op jit(solution)/shard_map/ppermute | solution.py:212
  63.9 12.1 %collective-permute-start.12 = (bf16[288,432]{1,0:T(8,128)(2,1)S(1)}, bf16[288,432]{1,0:T(8,128)(2,1)S(1)}, u32[]{:S(2)}, u32[]{:S(2)}) collective-permute-start(bf16[288,432]{1,0:T(8,128)(2,1)S(1)} %slice.6), channel_id=1, source_target_pairs={{0,2},{1,3},{2,0},{3,1},{4,6},{5,7},{6,4},{7,5},{8,10},{9,11},{10,... | collective-permute-start | bytes 746504 | tf_op jit(solution)/shard_map/ppermute | solution.py:212
  65.7 10.4 %collective-permute-start.13 = (bf16[288,288]{1,0:T(8,128)(2,1)S(1)}, bf16[288,288]{1,0:T(8,128)(2,1)S(1)}, u32[]{:S(2)}, u32[]{:S(2)}) collective-permute-start(bf16[288,288]{1,0:T(8,128)(2,1)S(1)} %slice.7), channel_id=1, source_target_pairs={{0,8},{8,0},{16,24},{24,16},{1,9},{9,1},{17,25},{25,17},{2,10},{10... | collective-permute-start | bytes 497672 | tf_op jit(solution)/shard_map/ppermute | solution.py:212
  67.0 9.7 %collective-permute-start.19 = (bf16[288,720]{1,0:T(8,128)(2,1)S(1)}, bf16[288,720]{1,0:T(8,128)(2,1)S(1)}, u32[]{:S(2)}, u32[]{:S(2)}) collective-permute-start(bf16[288,720]{1,0:T(8,128)(2,1)S(1)} %collective-permute-done.8.refs_0_.refs_18_), channel_id=1, source_target_pairs={{0,1},{1,0},{2,3},{3,2},{4,5},{5,4},{6,7},{7,6},{8,9},{9,8},{10,11... | collective-permute-start | bytes 1244168 | tf_op jit(solution)/shard_map/ppermute | solution.py:212
  71.5 9.9 %collective-permute-start.10 = (bf16[64,2304]{1,0:T(8,128)(2,1)S(1)}, bf16[64,2304]{1,0:T(8,128)(2,1)S(1)}, u32[]{:S(2)}, u32[]{:S(2)}) collective-permute-start(bf16[64,2304]{1,0:T(8,128)(2,1)S(1)} %shard_map.149.refs_0_), channel_id=1, source_target_pairs={{0,4},{4,0},{1,5},{5,1},{2,6},{6,2},{3,7},{7,3},{8,12},{12,8},{9,1... | collective-permute-start | bytes 884744 | tf_op jit(solution)/shard_map/ppermute | solution.py:212
  71.9 15.5 %collective-permute-start.11 = (bf16[64,2304]{1,0:T(8,128)(2,1)S(1)}, bf16[64,2304]{1,0:T(8,128)(2,1)S(1)}, u32[]{:S(2)}, u32[]{:S(2)}) collective-permute-start(bf16[64,2304]{1,0:T(8,128)(2,1)S(1)} %shard_map.150.refs_1_), channel_id=1, source_target_pairs={{0,4},{4,0},{1,5},{5,1},{2,6},{6,2},{3,7},{7,3},{8,12},{12,8},{9,1... | collective-permute-start | bytes 884744 | tf_op jit(solution)/shard_map/ppermute | solution.py:212
  76.1 1.6 %collective-permute-start.20 = (bf16[288,432]{1,0:T(8,128)(2,1)S(1)}, bf16[288,432]{1,0:T(8,128)(2,1)S(1)}, u32[]{:S(2)}, u32[]{:S(2)}) collective-permute-start(bf16[288,432]{1,0:T(8,128)(2,1)S(1)} %collective-permute-done.12.refs_2_.refs_20_), channel_id=1, source_target_pairs={{0,1},{1,0},{2,3},{3,2},{4,5},{5,4},{6,7},{7,6},{8,9},{9,8},{10,11... | collective-permute-start | bytes 746504 | tf_op jit(solution)/shard_map/ppermute | solution.py:212
  76.1 11.2 %collective-permute-start.21 = (bf16[288,288]{1,0:T(8,128)(2,1)S(1)}, bf16[288,288]{1,0:T(8,128)(2,1)S(1)}, u32[]{:S(2)}, u32[]{:S(2)}) collective-permute-start(bf16[288,288]{1,0:T(8,128)(2,1)S(1)} %collective-permute-done.13.refs_22_), channel_id=1, source_target_pairs={{0,1},{1,0},{2,3},{3,2},{4,5},{5,4},{6,7},{7,6},{8,9},{9,8},{10,11... | collective-permute-start | bytes 497672 | tf_op jit(solution)/shard_map/ppermute | solution.py:212
  95.3 8.6 %collective-permute-start.22 = (bf16[4,32,1152]{2,1,0:T(8,128)(2,1)S(1)}, bf16[4,32,1152]{2,1,0:T(8,128)(2,1)S(1)}, u32[]{:S(2)}, u32[]{:S(2)}) collective-permute-start(bf16[4,32,1152]{2,1,0:T(8,128)(2,1)S(1)} %get-tuple-element.53), channel_id=1, source_target_pairs={{0,4},{4,0},{1,5},{5,1},{2,6},{6,2},{3,7},{7,3},{8,12},{12,8},{9,1... | collective-permute-start | bytes 884744 | tf_op jit(solution)/shard_map/ppermute | solution.py:212
